TPU v7x, 32 devices: a whole 2x2x4 slice. The times are simulated.
32 devices in a mesh: fsdp: 4 (over z), ctx: 2 (over x), tp: 4 (over y, core).
Axes of the slice: x: 2, y: 2, z: 4, core: 2. Of those that a mesh axis runs over, the one named last changes fastest.
Arguments:
- resid_in: float32 [4, 2048, 1024], P('fsdp', 'ctx'), may hold values from -6 to 6
- segment_ids: int32 [4, 2048], P('fsdp'), may hold values from 0 to 5, never falling along the last dimension, each value on 1 to 768 neighbouring positions
- cotangent: float32 [4, 2048, 1024], P('fsdp', 'ctx'), may hold values from -6 to 6
- w_factor_a: float32 [1, 1024, 160], P(None, ('fsdp', 'ctx'), 'tp'), may hold values from -0.5 to 0.5
- w_factor_b: float32 [1, 1024, 640], P(None, ('fsdp', 'ctx', 'tp')), may hold values from -0.1875 to 0.1875
- w_out: float32 [1, 1024, 1024], P(None, 'tp', ('fsdp', 'ctx')), may hold values from -0.375 to 0.375
- w_gate_up: float32 [1, 2, 1024, 2816], P(None, None, ('fsdp', 'ctx'), 'tp'), may hold values from -0.1875 to 0.1875
- w_down: float32 [1, 2816, 1024], P(None, 'tp', ('fsdp', 'ctx')), may hold values from -0.109375 to 0.109375
- attn_gains: float32 [1, 1024], P(None, ('fsdp', 'ctx', 'tp')), may hold values from 0.25 to 1.75
- ffn_gains: float32 [1, 1024], P(None, ('fsdp', 'ctx', 'tp')), may hold values from 0.25 to 1.75
Outputs:
- block_out: float32 [4, 2048, 1024], P('fsdp', 'ctx')
- resid_grad: float32 [4, 2048, 1024], P('fsdp', 'ctx')
- grad_factor_a: float32 [1, 1024, 160], P(None, ('fsdp', 'ctx'), 'tp')
- grad_factor_b: float32 [1, 1024, 640], P(None, ('fsdp', 'ctx', 'tp'))
- grad_out: float32 [1, 1024, 1024], P(None, 'tp', ('fsdp', 'ctx'))
- grad_gate_up: float32 [1, 2, 1024, 2816], P(None, None, ('fsdp', 'ctx'), 'tp')
- grad_down: float32 [1, 2816, 1024], P(None, 'tp', ('fsdp', 'ctx'))
- grad_attn_gains: float32 [1, 1024], P(None, ('fsdp', 'ctx', 'tp'))
- grad_ffn_gains: float32 [1, 1024], P(None, ('fsdp', 'ctx', 'tp'))
Inputs may be any that keep to these rules, and one draw needn't show every extreme that they name: `segment_ids`: along each row the ids never fall and run through all 6 documents; each document holds 1 to 768 tokens.
All inputs are finite; a program needn't handle non-finite values.
Results may differ from a plain program's by a relative error of at most 0.024.
The roundings to bfloat16 on the way count: a program that leaves them out, or rounds other values in their place, can miss the bound.
Values may be sent and summed in bfloat16 or wider, within the bound.
No kernel may reach another device: no remote copies, remote signals or barrier semaphores. Data moves between devices by JAX's collectives and lax.ppermute only.
A program may use at most 192 MiB of HBM per device.

v0:
```python
import math

import jax
import jax.numpy as jnp
from jax import lax
from jax.experimental import pallas as pl
from jax.experimental.pallas import tpu as pltpu
from jax.sharding import PartitionSpec as P

HEAD_DIM = 64
RANK_Q = 6
RANK_KV = 2
RANKS = 10
KV = 2 * RANK_KV
MOST_DOC = 768
EPSILON = 1e-05
LANES = 128
BF16 = jnp.bfloat16
F32 = jnp.float32
MASKED = -1e30


def inverse_rms(values):
    return lax.rsqrt(jnp.mean(values * values, axis=-1, keepdims=True) + EPSILON)


def norm_back(grad_value, values, inverse, gain):
    scaled = grad_value * gain
    normal = values * inverse
    return inverse * (scaled - normal * jnp.mean(scaled * normal, axis=-1, keepdims=True))


def dot(left, right, dims):
    return lax.dot_general(left, right, (dims, ((), ())), preferred_element_type=F32)


def shift(value, axes, size, step, label="shift"):
    with jax.named_scope(label):
        return lax.ppermute(value, axes, [(i, (i + step) % size) for i in range(size)])


def swap(value, axis, size, bit, label="swap"):
    with jax.named_scope(label):
        return lax.ppermute(value, axis, [(i, i ^ bit) for i in range(size)])


def gather_direct(value, axis, size):
    me = lax.axis_index(axis)
    parts = [(me, value)]
    for step in range(1, size):
        parts.append(((me - step) % size, shift(value, axis, size, step)))
    out = jnp.zeros((size,) + value.shape, value.dtype)
    for place, part in parts:
        out = lax.dynamic_update_slice(out, part[None], (place,) + (0,) * value.ndim)
    return out


def gather_pair(value, axis, size, bit):
    mine = (lax.axis_index(axis) // bit) % 2 == 0
    other = swap(value, axis, size, bit)
    return jnp.stack([jnp.where(mine, value, other), jnp.where(mine, other, value)])


def after(value, *others):
    return lax.optimization_barrier((value,) + others)[0]


def take(value, index):
    return lax.dynamic_index_in_dim(value, index, 0, keepdims=False)


def scatter_direct(value, axis, size):
    me = lax.axis_index(axis)
    got = [
        shift(take(value, (me + step) % size), axis, size, step) for step in range(1, size)
    ]
    total = take(value, me).astype(F32)
    for part in got:
        total = total + part.astype(F32)
    return total


def scatter_pair(value, axis, size, bit):
    mine = (lax.axis_index(axis) // bit) % 2
    got = swap(take(value, 1 - mine).astype(BF16), axis, size, bit)
    return take(value, mine).astype(F32) + got.astype(F32)


def attention_mask(first_ref, window, block):
    start = first_ref[...]
    place = lax.broadcasted_iota(jnp.int32, (window, block), 0)
    query_place = lax.broadcasted_iota(jnp.int32, (window, block), 1) + (window - block)
    return jnp.where((place >= start) & (place <= query_place), 0.0, MASKED)


def head_rows(wa_ref, wide_ref, head):
    factors = wa_ref[head].astype(F32)
    key_rows = (factors[0:1] * wide_ref[0] + factors[1:2] * wide_ref[1]) * (1.0 / RANK_KV)
    value_rows = (factors[2:3] * wide_ref[2] + factors[3:4] * wide_ref[3]) * (1.0 / RANK_KV)
    return factors, key_rows.astype(BF16), value_rows.astype(BF16)


def forward_kernel(
    first_ref, a_ref, bq_ref, wa_ref, wb_ref, mixed_ref, lse_ref, q_ref, bias_ref, wide_ref, s_ref
):
    heads = a_ref.shape[0]
    window, block = bias_ref.shape
    bias_ref[...] = attention_mask(first_ref, window, block)
    wide_ref[...] = wb_ref[...].astype(F32)
    spans = [pl.ds(j * block, block) for j in range(window // block)]

    def one_head(head, carry):
        factors = a_ref[head]
        query = factors[0:1] * bq_ref[0]
        for r in range(1, RANK_Q):
            query = query + factors[r : r + 1] * bq_ref[r]
        query = (query * (1.0 / RANK_Q)).astype(BF16) * jnp.asarray(HEAD_DIM**-0.5, BF16)
        q_ref[head] = query
        _, key_rows, value_rows = head_rows(wa_ref, wide_ref, head)
        top = jnp.full((1, block), MASKED, F32)
        for j, span in enumerate(spans):
            keys = key_rows[:, j * block : (j + 1) * block]
            scores = dot(keys, query, ((0,), (0,))) + bias_ref[span, :]
            s_ref[span, :] = scores
            top = jnp.maximum(top, jnp.max(scores, axis=0, keepdims=True))
        total = jnp.zeros((1, block), F32)
        for span in spans:
            weight = jnp.exp(s_ref[span, :] - top)
            s_ref[span, :] = weight
            total = total + jnp.sum(weight, axis=0, keepdims=True)
        lse_ref[head] = top + jnp.log(total)
        scale = 1.0 / total
        mixed = jnp.zeros((HEAD_DIM, block), F32)
        for j, span in enumerate(spans):
            probs = (s_ref[span, :] * scale).astype(BF16)
            mixed = mixed + dot(
                value_rows[:, j * block : (j + 1) * block], probs, ((1,), (0,))
            )
        mixed_ref[head] = mixed.astype(BF16)
        return carry

    lax.fori_loop(0, heads, one_head, 0)


def backward_kernel(
    first_ref,
    a_ref,
    bq_ref,
    wa_ref,
    wb_ref,
    lse_ref,
    q_ref,
    go_ref,
    ga_ref,
    gbq_ref,
    gwa_ref,
    gwb_ref,
    bias_ref,
    wide_ref,
    p_ref,
    dp_ref,
):
    heads = a_ref.shape[0]
    window, block = bias_ref.shape
    bias_ref[...] = attention_mask(first_ref, window, block)
    wide_ref[...] = wb_ref[...].astype(F32)
    gbq_ref[...] = jnp.zeros_like(gbq_ref)
    gwb_ref[...] = jnp.zeros_like(gwb_ref)
    count = window // block
    spans = [pl.ds(j * block, block) for j in range(count)]

    def one_head(head, carry):
        factors, key_rows, value_rows = head_rows(wa_ref, wide_ref, head)
        query = q_ref[head]
        grad_out = go_ref[head]
        lse = lse_ref[head]
        inner = jnp.zeros((1, block), F32)
        for j, span in enumerate(spans):
            cut = slice(j * block, (j + 1) * block)
            scores = dot(key_rows[:, cut], query, ((0,), (0,))) + bias_ref[span, :]
            probs = jnp.exp(scores - lse)
            grad_probs = dot(value_rows[:, cut], grad_out, ((0,), (0,)))
            p_ref[span, :] = probs
            dp_ref[span, :] = grad_probs
            inner = inner + jnp.sum(probs * grad_probs, axis=0, keepdims=True)
        grad_query = jnp.zeros((HEAD_DIM, block), F32)
        for j, span in enumerate(spans):
            cut = slice(j * block, (j + 1) * block)
            probs = p_ref[span, :]
            grad_scores = (probs * (dp_ref[span, :] - inner)).astype(BF16)
            grad_query = grad_query + dot(key_rows[:, cut], grad_scores, ((1,), (0,)))
            grad_keys = dot(query, grad_scores, ((1,), (1,))) * (1.0 / RANK_KV)
            grad_values = dot(grad_out, probs.astype(BF16), ((1,), (1,))) * (1.0 / RANK_KV)
            rows = []
            for r in range(KV):
                grad = grad_keys if r < RANK_KV else grad_values
                rows.append(jnp.sum(grad * wide_ref[r, :, span], axis=0, keepdims=True))
                gwb_ref[r, :, span] += factors[r : r + 1, cut] * grad
            gwa_ref[head, :, span] = jnp.concatenate(rows, axis=0)
        grad_query = grad_query * (HEAD_DIM**-0.5 / RANK_Q)
        own = a_ref[head]
        rows = []
        for r in range(RANK_Q):
            rows.append(jnp.sum(grad_query * bq_ref[r], axis=0, keepdims=True))
            gbq_ref[r] += own[r : r + 1] * grad_query
        ga_ref[head] = jnp.concatenate(rows, axis=0)
        return carry

    lax.fori_loop(0, heads, one_head, 0)


VMEM_LIMIT = 56 * 1024 * 1024


def whole_specs(count):
    return [pl.BlockSpec(memory_space=pltpu.VMEM)] * count


def attend_forward(first, a_rows, b_query, win_a, win_b):
    heads, _, block = a_rows.shape
    window = win_a.shape[-1]
    return pl.pallas_call(
        forward_kernel,
        out_shape=(
            jax.ShapeDtypeStruct((heads, HEAD_DIM, block), BF16),
            jax.ShapeDtypeStruct((heads, 1, block), F32),
            jax.ShapeDtypeStruct((heads, HEAD_DIM, block), BF16),
        ),
        in_specs=whole_specs(5),
        out_specs=tuple(whole_specs(3)),
        scratch_shapes=[
            pltpu.VMEM((window, block), F32),
            pltpu.VMEM((KV, HEAD_DIM, window), F32),
            pltpu.VMEM((window, block), F32),
        ],
        compiler_params=pltpu.CompilerParams(vmem_limit_bytes=VMEM_LIMIT),
        name="attend_forward",
    )(first, a_rows, b_query, win_a, win_b)


def attend_backward(first, a_rows, b_query, win_a, win_b, lse, query, grad_mixed):
    heads, _, block = a_rows.shape
    window = win_a.shape[-1]
    return pl.pallas_call(
        backward_kernel,
        out_shape=(
            jax.ShapeDtypeStruct((heads, RANK_Q, block), F32),
            jax.ShapeDtypeStruct((RANK_Q, HEAD_DIM, block), F32),
            jax.ShapeDtypeStruct((heads, KV, window), F32),
            jax.ShapeDtypeStruct((KV, HEAD_DIM, window), F32),
        ),
        in_specs=whole_specs(8),
        out_specs=tuple(whole_specs(4)),
        scratch_shapes=[
            pltpu.VMEM((window, block), F32),
            pltpu.VMEM((KV, HEAD_DIM, window), F32),
            pltpu.VMEM((window, block), F32),
            pltpu.VMEM((window, block), F32),
        ],
        compiler_params=pltpu.CompilerParams(vmem_limit_bytes=VMEM_LIMIT),
        name="attend_backward",
    )(first, a_rows, b_query, win_a, win_b, lse, query, grad_mixed)


def rotate(rows, cosine, sine):
    half = HEAD_DIM // 2
    lower, upper = rows[:, :half], rows[:, half:]
    return jnp.concatenate(
        [lower * cosine - upper * sine, lower * sine + upper * cosine], axis=1
    )


def make_general(mesh):
    n_f, n_c, n_tp = mesh.shape["fsdp"], mesh.shape["ctx"], mesh.shape["tp"]
    n_hi, n_lo = 2, n_tp // 2

    def shards(
        resid_in,
        segment_ids,
        cotangent,
        w_factor_a,
        w_factor_b,
        w_out,
        w_gate_up,
        w_down,
        attn_gains,
        ffn_gains,
    ):
        seq_count, local_len, width = resid_in.shape
        assert seq_count == 1 and w_factor_a.shape[0] == 1 and n_lo == 2
        full_len = segment_ids.shape[1]
        block = local_len // n_tp
        extra = -(-(MOST_DOC - 1) // block)
        window = (extra + 1) * block
        a_cols = w_factor_a.shape[2]
        heads = n_tp * a_cols // RANKS
        b_cols = w_factor_b.shape[2]
        b_rows = w_factor_b.shape[1]
        b_parts = b_cols // LANES
        fc_cols = w_down.shape[2]
        hidden = w_down.shape[1]
        o_rows = w_out.shape[1]

        f_index, c_index, t_index = (
            lax.axis_index("fsdp"),
            lax.axis_index("ctx"),
            lax.axis_index("tp"),
        )
        hi, lo = t_index // 2, t_index % 2
        place = c_index * n_tp + t_index
        n_place = n_c * n_tp

        gains = jnp.concatenate([attn_gains, ffn_gains], axis=1).astype(BF16)
        gain_count = gains.shape[1]
        gain_rows = 16 * (-(-gain_count // (16 * LANES)))
        gains = jnp.pad(gains.reshape(-1), (0, gain_rows * LANES - gain_count))
        b_shard = w_factor_b[0].astype(BF16).reshape(b_rows, b_parts, LANES)
        a_shard = w_factor_a[0].astype(BF16).T
        pack = jnp.concatenate(
            [
                b_shard.transpose(1, 0, 2).reshape(-1, LANES),
                a_shard.reshape(-1, LANES),
                gains.reshape(-1, LANES),
            ],
            axis=0,
        )
        n_b = b_parts * b_rows
        n_a = a_cols * fc_cols // LANES
        pack = gather_direct(pack, "fsdp", n_f)
        after_pack = pack
        pack = gather_pair(pack, "ctx", n_c, 1)
        pack = gather_pair(pack, "tp", n_tp, 2)
        pack = gather_pair(pack, "tp", n_tp, 1)
        pack = pack.transpose(3, 2, 1, 0, 4, 5)
        weight_b = pack[:, :, :, :, :n_b].reshape(-1, b_parts, b_rows, LANES)
        weight_b = weight_b.transpose(0, 2, 1, 3).reshape(width, b_cols)
        weight_a = pack[:, :, :, :, n_b : n_b + n_a].reshape(n_f, n_c, n_tp, a_cols, fc_cols)
        weight_a = weight_a.transpose(2, 3, 0, 1, 4).reshape(n_tp * a_cols, width)
        gains_all = pack[:, :, :, :, n_b + n_a :].reshape(-1, gain_rows * LANES)[:, :gain_count]
        gains_all = gains_all.reshape(-1, 2, gain_count // 2).transpose(1, 0, 2)
        gains_all = gains_all.reshape(2, width).astype(F32)
        gain_attn, gain_ffn = gains_all[0:1], gains_all[1:2]

        big = jnp.concatenate(
            [
                w_gate_up[0, 0].astype(BF16).T,
                w_gate_up[0, 1].astype(BF16).T,
                w_down[0].astype(BF16),
                w_out[0].astype(BF16),
            ],
            axis=0,
        )
        big, _ = lax.optimization_barrier((big, after_pack))
        big = gather_direct(big, "fsdp", n_f)
        big = gather_pair(big, "ctx", n_c, 1)
        big = big.transpose(2, 1, 0, 3).reshape(-1, width)
        weight_g = big[:hidden]
        weight_u = big[hidden : 2 * hidden]
        weight_d = big[2 * hidden : 3 * hidden]
        weight_o = gather_pair(big[3 * hidden :], "tp", n_tp, 2)
        weight_o = gather_pair(weight_o, "tp", n_tp, 1)
        weight_o = weight_o.transpose(1, 0, 2, 3).reshape(n_tp * o_rows, width)

        seg_here = lax.dynamic_slice_in_dim(segment_ids[0], place * block, block, 0)
        first = jnp.sum((segment_ids[0][:, None] < seg_here[None, :]).astype(jnp.int32), axis=0)
        token = place * block + jnp.arange(block, dtype=jnp.int32)
        position = (token - first).astype(F32)
        first = (first - place * block + extra * block).reshape(1, block)
        frequency = 10000.0 ** (
            -2.0 * jnp.arange(HEAD_DIM // 2, dtype=F32) / HEAD_DIM
        )
        angles = frequency[:, None] * position[None, :]
        cosine, sine = jnp.cos(angles)[None], jnp.sin(angles)[None]

        stream = resid_in[0].reshape(n_tp, block, width)
        own = take(stream, t_index)
        inverse_attn = inverse_rms(own)
        normed = (own * inverse_attn * gain_attn).astype(BF16)
        a_rows = dot(weight_a, normed, ((1,), (1,))).reshape(heads, RANKS, block)
        b_raw = dot(weight_b, normed, ((0,), (1,))).reshape(RANKS, HEAD_DIM, block)
        b_rot = rotate(b_raw[: RANK_Q + RANK_KV], cosine, sine)
        b_query = b_rot[:RANK_Q]
        b_kv = jnp.concatenate([b_rot[RANK_Q:], b_raw[RANK_Q + RANK_KV :]], axis=0)
        payload = jnp.concatenate(
            [
                b_kv.reshape(KV * HEAD_DIM, block),
                a_rows[:, RANK_Q:].reshape(heads * KV, block),
            ],
            axis=0,
        ).astype(BF16)
        around = [
            lax.ppermute(
                payload, ("ctx", "tp"), [(i, i + step) for i in range(n_place - step)]
            )
            for step in range(extra, 0, -1)
        ]
        win = jnp.concatenate(around + [payload], axis=1)
        win_b = win[: KV * HEAD_DIM].reshape(KV, HEAD_DIM, window)
        win_a = win[KV * HEAD_DIM :].reshape(heads, KV, window)

        mixed, lse, query = attend_forward(first, a_rows, b_query, win_a, win_b)
        mixed = mixed.reshape(heads * HEAD_DIM, block)
        attn_out = dot(mixed, weight_o, ((0,), (0,)))
        mid = own + attn_out
        inverse_ffn = inverse_rms(mid)
        normed_ffn = (mid * inverse_ffn * gain_ffn).astype(BF16)

        near_rows = gather_pair(normed_ffn, "tp", n_tp, 1)
        far_rows = gather_pair(swap(normed_ffn, "tp", n_tp, 2), "tp", n_tp, 1)
        grad_all = cotangent[0].reshape(n_hi, n_lo * block, width)

        def half(rows, grad_rows):
            rows = rows.reshape(n_lo * block, width)
            gate = dot(rows, weight_g, ((1,), (1,)))
            up = dot(rows, weight_u, ((1,), (1,)))
            grad_act = dot(grad_rows, weight_d, ((1,), (1,)))
            squash = jax.nn.sigmoid(gate)
            act = (gate * squash * up).astype(BF16)
            grad_gate = (grad_act * up * squash * (1.0 + gate * (1.0 - squash))).astype(BF16)
            grad_up = (grad_act * gate * squash).astype(BF16)
            back = dot(grad_gate, weight_g, ((1,), (0,))) + dot(grad_up, weight_u, ((1,), (0,)))
            ahead = dot(act, weight_d, ((1,), (0,)))
            both = lambda v: v.reshape(n_lo, block, width)
            return rows, act, grad_gate, grad_up, both(back), both(ahead)

        grad_near = take(grad_all, hi).astype(BF16)
        grad_far = take(grad_all, 1 - hi).astype(BF16)
        near = half(near_rows, grad_near)
        far = half(far_rows, grad_far)
        back_far = scatter_pair(far[4], "tp", n_tp, 1).astype(BF16)
        back_far = swap(back_far, "tp", n_tp, 2)
        grad_normed_ffn = scatter_pair(near[4], "tp", n_tp, 1) + back_far.astype(F32)
        ahead_far = scatter_pair(far[5], "tp", n_tp, 1).astype(BF16)
        ahead_far = swap(ahead_far, "tp", n_tp, 2)
        ffn_out = scatter_pair(near[5], "tp", n_tp, 1) + ahead_far.astype(F32)

        def spread(value):
            beside = swap(value, "tp", n_tp, 1)
            across = swap(value, "tp", n_tp, 2)
            diagonal = swap(across, "tp", n_tp, 1)
            out = jnp.zeros((n_tp,) + value.shape, value.dtype)
            for bit, part in enumerate((value, beside, across, diagonal)):
                out = lax.dynamic_update_slice(out, part[None], (t_index ^ bit, 0, 0))
            return out.reshape(local_len, width).astype(F32)

        block_out = resid_in + spread((attn_out + ffn_out).astype(BF16))[None]

        def columns(value, which):
            value = value.reshape(value.shape[0], n_f, n_c, fc_cols)
            value = lax.dynamic_index_in_dim(value, which, 2, keepdims=False)
            return value.reshape(value.shape[0], n_f * fc_cols)

        rows_all = jnp.concatenate([near[0], far[0]], axis=0)
        act_all = jnp.concatenate([near[1], far[1]], axis=0)
        gate_all = jnp.concatenate([near[2], far[2]], axis=0)
        up_all = jnp.concatenate([near[3], far[3]], axis=0)
        cot_all = jnp.concatenate([grad_near, grad_far], axis=0)

        def big_grads(which):
            rows_cut = columns(rows_all, which)
            cot_cut = columns(cot_all, which)
            return jnp.concatenate(
                [
                    dot(gate_all, rows_cut, ((0,), (0,))),
                    dot(up_all, rows_cut, ((0,), (0,))),
                    dot(act_all, cot_cut, ((0,), (0,))),
                ],
                axis=0,
            )

        def over_fc(send, keep):
            total = keep + swap(send.astype(BF16), "ctx", n_c, 1).astype(F32)
            total = total.astype(BF16).reshape(-1, n_f, fc_cols).transpose(1, 0, 2)
            return scatter_direct(total, "fsdp", n_f)

        grad_big = over_fc(big_grads(1 - c_index), big_grads(c_index))
        grad_gate_w = grad_big[:hidden].T
        grad_up_w = grad_big[hidden : 2 * hidden].T
        grad_down_w = grad_big[2 * hidden :]

        own_cot = take(cotangent[0].reshape(n_tp, block, width), t_index)
        gain_grad_ffn = jnp.sum(grad_normed_ffn * mid * inverse_ffn, axis=0)
        delta_mid = norm_back(grad_normed_ffn, mid, inverse_ffn, gain_ffn)
        grad_attn = (own_cot + delta_mid).astype(BF16)
        grad_out = dot(mixed, grad_attn, ((1,), (0,))).reshape(n_hi, n_lo, o_rows, width)
        grad_out = scatter_pair(grad_out.transpose(1, 0, 2, 3), "tp", n_tp, 1)
        grad_out = scatter_pair(grad_out, "tp", n_tp, 2)
        grad_out = over_fc(columns(grad_out, 1 - c_index), columns(grad_out, c_index))

        grad_mixed = dot(weight_o, grad_attn, ((1,), (1,))).astype(BF16)
        ga_q, gb_q, gw_a, gw_b = attend_backward(
            first,
            a_rows,
            b_query,
            win_a,
            win_b,
            lse,
            query,
            grad_mixed.reshape(heads, HEAD_DIM, block),
        )
        gw = jnp.concatenate(
            [gw_b.reshape(KV * HEAD_DIM, window), gw_a.reshape(heads * KV, window)], axis=0
        )
        total = gw[:, extra * block :]
        for step in range(1, extra + 1):
            part = gw[:, (extra - step) * block : (extra - step + 1) * block].astype(BF16)
            part = lax.ppermute(
                part, ("ctx", "tp"), [(i + step, i) for i in range(n_place - step)]
            )
            total = total + part.astype(F32)
        gb_kv = total[: KV * HEAD_DIM].reshape(KV, HEAD_DIM, block)
        ga_kv = total[KV * HEAD_DIM :].reshape(heads, KV, block)
        grad_b = jnp.concatenate(
            [
                rotate(jnp.concatenate([gb_q, gb_kv[:RANK_KV]], axis=0), cosine, -sine),
                gb_kv[RANK_KV:],
            ],
            axis=0,
        )
        grad_b = grad_b.reshape(b_cols, block).astype(BF16)
        grad_a = jnp.concatenate([ga_q, ga_kv], axis=1).reshape(heads * RANKS, block).astype(BF16)
        grad_normed = dot(grad_a, weight_a, ((0,), (0,))) + dot(grad_b, weight_b, ((0,), (1,)))
        gain_grad_attn = jnp.sum(grad_normed * own * inverse_attn, axis=0)
        delta = delta_mid + norm_back(grad_normed, own, inverse_attn, gain_attn)
        resid_grad = cotangent + spread(delta.astype(BF16))[None]

        grad_wa = dot(grad_a, normed, ((1,), (0,))).astype(BF16)
        grad_wa = grad_wa.reshape(n_hi, n_lo, a_cols, n_f, n_c, fc_cols)
        grad_wa = grad_wa.transpose(1, 0, 4, 3, 2, 5).reshape(n_lo, n_hi, n_c, n_f, n_a, LANES)
        grad_wb = jnp.einsum(
            "pkt,td->pdk",
            grad_b.reshape(b_parts, LANES, block),
            normed,
            preferred_element_type=F32,
        ).astype(BF16)
        grad_wb = grad_wb.reshape(b_parts, n_f, n_c, n_hi, n_lo, b_rows, LANES)
        grad_wb = grad_wb.transpose(4, 3, 2, 1, 0, 5, 6)
        grad_wb = grad_wb.reshape(n_lo, n_hi, n_c, n_f, n_b, LANES)
        gain_grads = jnp.stack([gain_grad_attn, gain_grad_ffn]).astype(BF16)
        gain_grads = gain_grads.reshape(2, n_f, n_c, n_hi, n_lo, gain_count // 2)
        gain_grads = gain_grads.transpose(4, 3, 2, 1, 0, 5).reshape(
            n_lo, n_hi, n_c, n_f, gain_count
        )
        gain_grads = jnp.pad(
            gain_grads, [(0, 0)] * 4 + [(0, gain_rows * LANES - gain_count)]
        ).reshape(n_lo, n_hi, n_c, n_f, gain_rows, LANES)
        pack = jnp.concatenate([grad_wb, grad_wa, gain_grads], axis=4)
        pack = scatter_pair(pack, "tp", n_tp, 1)
        pack = scatter_pair(pack, "tp", n_tp, 2)
        pack = scatter_pair(pack, "ctx", n_c, 1).astype(BF16)
        pack = scatter_direct(pack, "fsdp", n_f)
        part_b = pack[:n_b].reshape(b_parts, b_rows, LANES).transpose(1, 0, 2)
        part_b = part_b.reshape(1, b_rows, b_cols)
        part_a = pack[n_b : n_b + n_a].reshape(a_cols, fc_cols).T[None]
        part_gain = pack[n_b + n_a :].reshape(-1)[:gain_count].reshape(2, 1, gain_count // 2)
        return (
            block_out,
            resid_grad,
            part_a,
            part_b,
            grad_out[None],
            jnp.stack([grad_gate_w, grad_up_w])[None],
            grad_down_w[None],
            part_gain[0],
            part_gain[1],
        )

    return shards


def rotated(rows, cosine, sine):
    half = HEAD_DIM // 2
    lower, upper = rows[:half], rows[half:]
    return jnp.concatenate([lower * cosine - upper * sine, lower * sine + upper * cosine], axis=0)


def make_fused(mesh):
    n_f, n_c, n_tp = mesh.shape["fsdp"], mesh.shape["ctx"], mesh.shape["tp"]
    n_piece = n_f * n_c
    AT_TP = n_piece
    AT_ME = n_piece + n_tp

    def shards(
        resid_in,
        segment_ids,
        cotangent,
        w_factor_a,
        w_factor_b,
        w_out,
        w_gate_up,
        w_down,
        attn_gains,
        ffn_gains,
    ):
        _, local_len, width = resid_in.shape
        block = local_len // n_tp
        extra = -(-(MOST_DOC - 1) // block)
        windows = extra + 1
        a_cols = w_factor_a.shape[2]
        group = a_cols // RANKS
        heads = n_tp * group
        feats = group * HEAD_DIM
        a_pad = 16 * (-(-a_cols // 16))
        b_rows, b_cols = w_factor_b.shape[1:]
        b_parts = b_cols // LANES
        n_b = b_parts * b_rows
        pack_rows = n_b + a_pad + 16
        fc_cols = w_down.shape[2]
        hidden = w_down.shape[1]
        o_rows = w_out.shape[1]
        gain_part = attn_gains.shape[1]
        kv_b = KV * HEAD_DIM
        kv_rows = kv_b + heads * KV
        half_width = width // n_c
        pairs = heads // 2
        pair_rows = 8 * (-(-2 * RANKS // 8))
        early = 2 * hidden + 16 * (hidden // 64)
        assert n_f == 4 and fc_cols == LANES and o_rows == feats and n_tp == 4 and n_c == 2

        f_index, c_index, t_index = (
            lax.axis_index("fsdp"),
            lax.axis_index("ctx"),
            lax.axis_index("tp"),
        )
        place = c_index * n_tp + t_index
        n_place = n_c * n_tp
        columns = [
            ((f_index - s) % n_f) * n_c + (c_index if near == 0 else 1 - c_index)
            for near in range(n_c)
            for s in range(n_f)
        ]
        members = [t_index ^ (lo + 2 * hi) for lo in range(2) for hi in range(2)]
        beside_shift = jnp.where(f_index % 2 == 0, n_f - 1, 1)
        meta = jnp.stack(columns + members + [t_index, f_index, beside_shift]).astype(jnp.int32)

        resid_in = pltpu.with_memory_space_constraint(resid_in, pltpu.HBM)
        cotangent = pltpu.with_memory_space_constraint(cotangent, pltpu.HBM)

        def column(meta_ref, j):
            return pl.ds(pl.multiple_of(meta_ref[j] * LANES, LANES), LANES)

        def member(meta_ref, lo, hi):
            return meta_ref[AT_TP + 2 * lo + hi]

        def to_arrival(meta_ref, load):
            return jnp.concatenate([load(column(meta_ref, j)) for j in range(n_piece)], axis=1)

        WHOLE = pl.BlockSpec(memory_space=pltpu.VMEM)
        REMOTE = pl.BlockSpec(memory_space=pl.ANY)

        def call(
            kernel, name, outs, args, specs=None, scratch=(), grid=(1,), out_specs=None, room=4,
            scalars=meta,
        ):
            held = 0
            for arg, spec in zip((*args, *args[:1]), (specs or []) + (out_specs or [])):
                if spec.block_shape:
                    held += 2 * math.prod(spec.block_shape) * arg.dtype.itemsize
            for item in scratch:
                if hasattr(item, "shape") and item.memory_space == pltpu.VMEM:
                    held += math.prod(item.shape) * jnp.dtype(item.dtype).itemsize
            limit = min(held + room * 2**20, VMEM_LIMIT)
            return pl.pallas_call(
                kernel,
                out_shape=[jax.ShapeDtypeStruct(s, d) for s, d in outs],
                grid_spec=pltpu.PrefetchScalarGridSpec(
                    num_scalar_prefetch=1,
                    grid=grid,
                    in_specs=specs or [WHOLE] * len(args),
                    out_specs=out_specs or [WHOLE] * len(outs),
                    scratch_shapes=list(scratch),
                ),
                compiler_params=pltpu.CompilerParams(vmem_limit_bytes=limit),
                name=name,
            )(scalars, *args)


        def pack_kernel(meta_ref, b_ref, a_ref, g0_ref, g1_ref, out_ref):
            for k in range(b_parts):
                out_ref[k * b_rows : (k + 1) * b_rows, :] = b_ref[
                    0, :, k * LANES : (k + 1) * LANES
                ].astype(BF16)
            a_shard = jnp.concatenate([a_ref[0], jnp.zeros((a_pad - a_cols, LANES), F32)], axis=0)
            out_ref[n_b : n_b + a_pad, :] = a_shard.astype(BF16)
            both = jnp.concatenate([g0_ref[...], g1_ref[...]], axis=0)
            both = jnp.concatenate([both, jnp.zeros((6, gain_part), F32)], axis=0)
            both = jnp.concatenate([both, jnp.zeros((8, LANES - gain_part), F32)], axis=1)
            both = pltpu.roll(both, meta_ref[AT_ME] * gain_part, 1)
            both = jnp.concatenate([both, jnp.zeros((8, LANES), F32)], axis=0)
            out_ref[n_b + a_pad :, :] = both.astype(BF16)

        def big_kernel(meta_ref, gu_ref, d_ref, gu_out_ref, d_out_ref):
            for k in range(2):
                gu_out_ref[k * hidden : (k + 1) * hidden, :] = gu_ref[0, k].astype(BF16)
            gu_out_ref[2 * hidden :, :] = d_ref[0, : early - 2 * hidden, :].astype(BF16)
            d_out_ref[...] = d_ref[0, early - 2 * hidden :, :].astype(BF16)

        def factor_kernel(
            meta_ref,
            x_ref,
            p0_ref,
            p1_ref,
            cos_ref,
            sin_ref,
            wb_ref,
            wa_ref,
            gain_ref,
            normed_ref,
            a_ref,
            bq_ref,
            pay_ref,
        ):
            gain_ref[...] = jnp.zeros_like(gain_ref)
            for lo, hi in ((0, 0), (0, 1), (1, 0), (1, 1)):
                part = (p0_ref, p1_ref)[lo]
                tp = member(meta_ref, lo, hi)
                for near in range(n_c):
                    for s in range(n_f):
                        j = near * n_f + s
                        lanes = column(meta_ref, j)
                        row = pl.multiple_of((meta_ref[j] * n_tp + tp) * b_rows, b_rows)
                        for k in range(b_parts):
                            wb_ref[pl.ds(row, b_rows), k * LANES : (k + 1) * LANES] = part[
                                near, hi, s, k * b_rows : (k + 1) * b_rows, :
                            ]
                        wa_ref[tp, :, lanes] = part[near, hi, s, n_b : n_b + a_pad, :]
                        gain_ref[:, lanes] += part[near, hi, s, n_b + a_pad :, :].astype(F32)
            x = x_ref[...]
            normed = (x * inverse_rms(x) * gain_ref[0:1]).astype(BF16)
            normed_ref[...] = normed
            cosine, sine = cos_ref[...], sin_ref[...]
            b_raw = jnp.transpose(dot(normed, wb_ref[...], ((1,), (0,))))
            for r in range(RANK_Q):
                bq_ref[r] = rotated(b_raw[r * HEAD_DIM : (r + 1) * HEAD_DIM], cosine, sine)
            for r in range(KV):
                rows = b_raw[(RANK_Q + r) * HEAD_DIM : (RANK_Q + r + 1) * HEAD_DIM]
                if r < RANK_KV:
                    rows = rotated(rows, cosine, sine)
                pay_ref[r * HEAD_DIM : (r + 1) * HEAD_DIM, :] = rows.astype(BF16)
            for tp in range(n_tp):
                a_raw = dot(wa_ref[tp], normed, ((1,), (1,)))
                a_ref[tp] = a_raw
                kv = [a_raw[g * RANKS + RANK_Q : (g + 1) * RANKS] for g in range(group)]
                start = kv_b + tp * group * KV
                pay_ref[start : start + group * KV, :] = jnp.concatenate(kv, axis=0).astype(BF16)

        def set_mask(first_ref, bias_ref):
            bias_ref[...] = attention_mask(first_ref, windows * block, block)

        def is_even(meta_ref):
            return lax.rem(meta_ref[AT_ME], 2) == 0

        def widen(meta_ref, arrived, win_ref, wide_ref):
            third, second, beside_second, beside, own = arrived
            win_ref[1] = second[...]
            win_ref[3] = own[...]

            @pl.when(is_even(meta_ref))
            def _():
                win_ref[0] = third[...]
                win_ref[2] = beside_second[...]

            @pl.when(jnp.logical_not(is_even(meta_ref)))
            def _():
                win_ref[0] = beside_second[...]
                win_ref[2] = beside[...]

            for j in range(windows):
                for r in range(KV):
                    wide_ref[j, r] = win_ref[j, r * HEAD_DIM : (r + 1) * HEAD_DIM, :].astype(F32)

        def spread_factors(a_ref, win_ref, own_ref, kv_ref):
            for pair in range(pairs):
                start = pair % (group // 2) * 2 * RANKS
                own_ref[pair, : 2 * RANKS, :] = a_ref[pair * 2 // group, start : start + 2 * RANKS, :]
            for j in range(windows):
                kv_ref[j] = win_ref[j, kv_b:, :].astype(F32)

        def kv_factors(kv_ref, pair):
            start = pl.multiple_of(pair * (2 * KV), 2 * KV)
            return [kv_ref[j, pl.ds(start, 2 * KV), :] for j in range(windows)]

        def head_place(pair, g):
            tp, half = pair // (group // 2), lax.rem(pair, group // 2)
            return tp, 2 * half + g, pl.ds(pl.multiple_of((2 * half + g) * HEAD_DIM, HEAD_DIM), HEAD_DIM)

        def kv_rows_of(factors, wide_ref, g, j):
            def mix(r):
                a0 = factors[j][g * KV + r : g * KV + r + 1]
                a1 = factors[j][g * KV + r + 1 : g * KV + r + 2]
                rows = a0 * wide_ref[j, r] + a1 * wide_ref[j, r + 1]
                return (rows * (1.0 / RANK_KV)).astype(BF16)

            return mix(0), mix(RANK_KV)

        def attention_kernel(
            meta_ref,
            first_ref,
            a_ref,
            bq_ref,
            w0_ref,
            w1_ref,
            w2_ref,
            w3_ref,
            w4_ref,
            lse_ref,
            q_ref,
            mixed_ref,
            win_ref,
            bias_ref,
            wide_ref,
            s_ref,
            own_ref,
            kv_ref,
        ):
            set_mask(first_ref, bias_ref)
            widen(meta_ref, (w0_ref, w1_ref, w2_ref, w3_ref, w4_ref), win_ref, wide_ref)
            spread_factors(a_ref, win_ref, own_ref, kv_ref)
            spans = [pl.ds(j * block, block) for j in range(windows)]

            def one_pair(pair, carry):
                own = own_ref[pair]
                factors = kv_factors(kv_ref, pair)
                for g in range(2):
                    tp, head, rows = head_place(pair, g)
                    query = own[g * RANKS : g * RANKS + 1] * bq_ref[0]
                    for r in range(1, RANK_Q):
                        query = query + own[g * RANKS + r : g * RANKS + r + 1] * bq_ref[r]
                    query = (query * (1.0 / RANK_Q)).astype(BF16)
                    query = query * jnp.asarray(HEAD_DIM**-0.5, BF16)
                    q_ref[tp, head] = query
                    top = jnp.full((1, block), MASKED, F32)
                    values = []
                    for j, span in enumerate(spans):
                        keys, value_rows = kv_rows_of(factors, wide_ref, g, j)
                        values.append(value_rows)
                        scores = dot(keys, query, ((0,), (0,))) + bias_ref[span, :]
                        s_ref[g, span, :] = scores
                        top = jnp.maximum(top, jnp.max(scores, axis=0, keepdims=True))
                    total = jnp.zeros((1, block), F32)
                    for span in spans:
                        weight = jnp.exp(s_ref[g, span, :] - top)
                        s_ref[g, span, :] = weight
                        total = total + jnp.sum(weight, axis=0, keepdims=True)
                    lse_ref[pair, g : g + 1, :] = top + jnp.log(total)
                    scale = 1.0 / total
                    mixed = jnp.zeros((HEAD_DIM, block), F32)
                    for j, span in enumerate(spans):
                        probs = (s_ref[g, span, :] * scale).astype(BF16)
                        mixed = mixed + dot(values[j], probs, ((1,), (0,)))
                    mixed_ref[tp, rows, :] = mixed.astype(BF16)
                return carry

            lax.fori_loop(0, pairs, one_pair, 0)

        def project_kernel(
            meta_ref, x_ref, mixed_ref, o0_ref, o1_ref, gain_ref, mid_ref, attn_ref, nf_ref
        ):
            attn = jnp.zeros((block, width), F32)
            for lo, ref in enumerate((o0_ref, o1_ref)):
                for hi in range(2):
                    rows = mixed_ref[member(meta_ref, lo, hi)]
                    attn = attn + dot(rows, ref[hi * o_rows : (hi + 1) * o_rows, :], ((0,), (0,)))
            attn_ref[...] = attn
            mid = to_arrival(meta_ref, lambda lanes: x_ref[:, lanes]) + attn
            mid_ref[...] = mid
            gain = to_arrival(meta_ref, lambda lanes: gain_ref[1:2, lanes])
            nf_ref[...] = (mid * inverse_rms(mid) * gain).astype(BF16)

        def rows_kernel(
            meta_ref, x_hbm, cot_ref, x_ref, own_ref, near_ref, far_ref, cot_buf, sems
        ):
            row = pl.multiple_of(meta_ref[AT_ME] * block, block)
            own_load = pltpu.make_async_copy(x_hbm.at[0, pl.ds(row, block), :], x_ref, sems.at[4])
            own_load.start()
            loads = []
            for side in range(2):
                for i in range(2):
                    row = pl.multiple_of(member(meta_ref, i, side) * block, block)
                    k = 2 * side + i
                    loads.append(
                        pltpu.make_async_copy(
                            cot_ref.at[0, pl.ds(row, block), :], cot_buf.at[k], sems.at[k]
                        )
                    )
                    loads[-1].start()
            for k, load in enumerate(loads):
                load.wait()
                out_ref = (near_ref, far_ref)[k // 2]
                rows = slice(k % 2 * block, (k % 2 + 1) * block)
                for j in range(n_piece):
                    lanes = slice(j * LANES, (j + 1) * LANES)
                    part = cot_buf[k, :, column(meta_ref, j)]
                    out_ref[rows, lanes] = part.astype(BF16)
                    if k == 0:
                        own_ref[:, lanes] = part
            own_load.wait()

        def feed_rows(n_refs, gb_ref, w_ref, ht_ref, back0_ref, back1_ref):
            for i in range(2):
                cut = slice(i * block, (i + 1) * block)
                rows = n_refs[i][...]
                gate = dot(w_ref[0:hidden, :], rows, ((1,), (1,)))
                up = dot(w_ref[hidden : 2 * hidden, :], rows, ((1,), (1,)))
                grad_act = dot(w_ref[2 * hidden :, :], gb_ref[cut, :], ((1,), (1,)))
                squash = jax.nn.sigmoid(gate)
                soft = gate * squash
                ht_ref[2 * hidden :, cut] = (soft * up).astype(BF16)
                ht_ref[0:hidden, cut] = (
                    grad_act * up * squash * (1.0 + gate * (1.0 - squash))
                ).astype(BF16)
                ht_ref[hidden : 2 * hidden, cut] = (grad_act * soft).astype(BF16)
            back = dot(ht_ref[: 2 * hidden, :], w_ref[: 2 * hidden, :], ((0,), (0,)))
            back0_ref[...] = back[:block]
            back1_ref[...] = back[block:].astype(BF16)

        def far_kernel(meta_ref, n0_ref, n1_ref, gb_ref, *refs):
            own_gu_ref, far_gu_ref, pair_gu_ref, gu_across_ref, gu_rest_ref = refs[:5]
            dn_refs = refs[5 : 5 + n_f]
            ht_ref, back0_ref, back1_ref, w_ref, sems = refs[5 + n_f :]
            gate_up = [own_gu_ref, far_gu_ref, pair_gu_ref.at[0], pair_gu_ref.at[1], gu_across_ref]
            gate_up += [gu_rest_ref.at[s] for s in range(n_f - 1)]
            beside_shift = meta_ref[AT_ME + 2]
            arrivals = [0, 2, beside_shift, n_f - beside_shift]
            down = [ref.at[near] for near in range(n_c) for ref in dn_refs]
            loads = []
            for j in range(n_piece):
                lanes = pl.ds(j * LANES, LANES)
                at = pl.multiple_of((arrivals[j % n_f] + j // n_f * n_f) * LANES, LANES)
                loads.append(
                    pltpu.make_async_copy(
                        gate_up[j],
                        w_ref.at[pl.ds(0, early), pl.ds(at, LANES)],
                        sems.at[j],
                    )
                )
                loads.append(
                    pltpu.make_async_copy(
                        down[j], w_ref.at[pl.ds(early, 3 * hidden - early), lanes], sems.at[n_piece + j]
                    )
                )
            for load in loads:
                load.start()
            for load in loads:
                load.wait()
            feed_rows((n0_ref, n1_ref), gb_ref, w_ref, ht_ref, back0_ref, back1_ref)

        def near_kernel(meta_ref, n0_ref, n1_ref, gb_ref, w_ref, far_ht_ref, ht_ref, *refs):
            back0_ref, back1_ref, *ahead_refs = refs
            feed_rows((n0_ref, n1_ref), gb_ref, w_ref, ht_ref, back0_ref, back1_ref)
            for k, ref in enumerate((ht_ref, far_ht_ref)):
                ahead = dot(ref[2 * hidden :, :], w_ref[2 * hidden :, :], ((0,), (0,)))
                ahead_refs[2 * k][...] = ahead[:block]
                ahead_refs[2 * k + 1][...] = ahead[block:].astype(BF16)

        def weight_grad(refs, start, stop, right):
            hts, n_near, n_far, gbs = refs[0:2], refs[2:4], refs[4:6], refs[6:8]
            total = jnp.zeros((stop - start, width), F32)
            for side in range(2):
                left = hts[side]
                if right == 1:
                    total = total + dot(left[start:stop, :], gbs[side][...], ((1,), (0,)))
                    continue
                for i in range(2):
                    rows = (n_near, n_far)[side][i][...]
                    cut = slice(i * block, (i + 1) * block)
                    total = total + dot(left[start:stop, cut], rows, ((1,), (0,)))
            return total

        def gate_up_grad_kernel(meta_ref, *refs):
            keep_ref, send_ref = refs[8:]
            for k in range(2):
                cut = slice(k * hidden, (k + 1) * hidden)
                total = weight_grad(refs, k * hidden, (k + 1) * hidden, 0)
                keep_ref[cut, :] = total[:, :half_width].astype(BF16)
                send_ref[cut, :] = total[:, half_width:].astype(BF16)

        def down_grad_kernel(meta_ref, *refs):
            keep_ref, send_ref = refs[8:]
            total = weight_grad(refs, 2 * hidden, 3 * hidden, 1)

            def chunk(s, near):
                start = near * half_width + s * LANES
                return total[:, start : start + LANES]

            for near in range(n_c):
                keep_ref[0, near] = chunk(0, near)
                keep_ref[1, near] = chunk(2, near)

            @pl.when(lax.rem(meta_ref[AT_ME + 1], 2) == 0)
            def _():
                for near in range(n_c):
                    send_ref[0, near] = chunk(3, near).astype(BF16)
                    send_ref[1, near] = chunk(1, near).astype(BF16)

            @pl.when(lax.rem(meta_ref[AT_ME + 1], 2) == 1)
            def _():
                for near in range(n_c):
                    send_ref[0, near] = chunk(1, near).astype(BF16)
                    send_ref[1, near] = chunk(3, near).astype(BF16)

        def middle_kernel(
            meta_ref,
            cot_ref,
            back_ref,
            beside_ref,
            across_ref,
            mid_ref,
            gain_ref,
            o0_ref,
            o1_ref,
            mixed_ref,
            dmid_ref,
            gg_ref,
            go_ref,
            keep_ref,
            send_ref,
        ):
            back = back_ref[...] + beside_ref[...].astype(F32) + across_ref[...].astype(F32)
            mid = mid_ref[...]
            inverse = inverse_rms(mid)
            gain = to_arrival(meta_ref, lambda lanes: gain_ref[1:2, lanes])
            normal = mid * inverse
            gains = jnp.sum(back * normal, axis=0, keepdims=True)
            for j in range(n_piece):
                gg_ref[:, column(meta_ref, j)] = jnp.broadcast_to(
                    gains[:, j * LANES : (j + 1) * LANES], (8, LANES)
                )
            scaled = back * gain
            delta = inverse * (
                scaled - normal * jnp.mean(scaled * normal, axis=-1, keepdims=True)
            )
            dmid_ref[...] = delta
            grad = (cot_ref[...] + delta).astype(BF16)
            for lo, ref in enumerate((o0_ref, o1_ref)):
                for hi in range(2):
                    tp = member(meta_ref, lo, hi)
                    cut = slice(hi * o_rows, (hi + 1) * o_rows)
                    go_ref[tp] = dot(ref[cut, :], grad, ((1,), (1,))).astype(BF16)
                    weight = dot(mixed_ref[tp], grad, ((1,), (0,))).astype(BF16)
                    (keep_ref, send_ref)[lo][cut, :] = weight

        def attention_back_kernel(
            part,
            meta_ref,
            first_ref,
            a_ref,
            bq_ref,
            w0_ref,
            w1_ref,
            w2_ref,
            w3_ref,
            w4_ref,
            lse_ref,
            q_ref,
            go_ref,
            *refs,
        ):
            win_ref, bias_ref, wide_ref, p_ref, dp_ref, own_ref, kv_ref = refs[-7:]
            if part == 0:
                ga_ref, gbq_ref, gwb_ref, gwa_ref = refs[:4]
            else:
                ga_ref, gbq_ref, second_ref, beside_ref, third_ref, own_out_ref = refs[3:9]
                gwb_ref, gwa_ref = refs[-9:-7]
            set_mask(first_ref, bias_ref)
            widen(meta_ref, (w0_ref, w1_ref, w2_ref, w3_ref, w4_ref), win_ref, wide_ref)
            spread_factors(a_ref, win_ref, own_ref, kv_ref)
            if part == 0:
                gbq_ref[...] = jnp.zeros_like(gbq_ref)
                gwb_ref[...] = jnp.zeros_like(gwb_ref)
            else:
                gbq_ref[...] = refs[0][...]
                gwb_ref[...] = refs[1][...]
                gwa_ref[...] = refs[2][...]
            spans = [pl.ds(j * block, block) for j in range(windows)]
            first_pair = part * (pairs // 2)

            def one_pair(pair, carry):
                own = own_ref[pair]
                factors = kv_factors(kv_ref, pair)
                grad_a = []
                grad_kv = [[] for _ in spans]
                for g in range(2):
                    tp, head, rows = head_place(pair, g)
                    query = q_ref[tp, head]
                    grad_out = go_ref[tp, rows, :]
                    lse = lse_ref[pair, g : g + 1, :]
                    inner = jnp.zeros((1, block), F32)
                    keys = []
                    for j, span in enumerate(spans):
                        key_rows, value_rows = kv_rows_of(factors, wide_ref, g, j)
                        keys.append(key_rows)
                        scores = dot(key_rows, query, ((0,), (0,))) + bias_ref[span, :]
                        probs = jnp.exp(scores - lse)
                        grad_probs = dot(value_rows, grad_out, ((0,), (0,)))
                        p_ref[g % 2, span, :] = probs
                        dp_ref[g % 2, span, :] = grad_probs
                        inner = inner + jnp.sum(probs * grad_probs, axis=0, keepdims=True)
                    grad_query = jnp.zeros((HEAD_DIM, block), F32)
                    for j, span in enumerate(spans):
                        probs = p_ref[g % 2, span, :]
                        grad_scores = (probs * (dp_ref[g % 2, span, :] - inner)).astype(BF16)
                        grad_query = grad_query + dot(keys[j], grad_scores, ((1,), (0,)))
                        grad_keys = dot(query, grad_scores, ((1,), (1,))) * (1.0 / RANK_KV)
                        grad_values = dot(grad_out, probs.astype(BF16), ((1,), (1,)))
                        grad_values = grad_values * (1.0 / RANK_KV)
                        for r in range(KV):
                            grad = grad_keys if r < RANK_KV else grad_values
                            grad_kv[j].append(
                                jnp.sum(grad * wide_ref[j, r], axis=0, keepdims=True)
                            )
                            gwb_ref[j, r] += factors[j][g * KV + r : g * KV + r + 1] * grad
                    grad_query = grad_query * (HEAD_DIM**-0.5 / RANK_Q)
                    for r in range(RANK_Q):
                        grad_a.append(jnp.sum(grad_query * bq_ref[r], axis=0, keepdims=True))
                        gbq_ref[r] += own[g * RANKS + r : g * RANKS + r + 1] * grad_query
                    grad_a.append(jnp.zeros((KV, block), F32))
                grad_a.append(jnp.zeros((pair_rows - 2 * RANKS, block), F32))
                ga_ref[pair - first_pair] = jnp.concatenate(grad_a, axis=0)
                start = pl.multiple_of(pair * (2 * KV), 2 * KV)
                for j in range(windows):
                    gwa_ref[j, pl.ds(start, 2 * KV), :] = jnp.concatenate(grad_kv[j], axis=0)
                return carry

            lax.fori_loop(first_pair, first_pair + pairs // 2, one_pair, 0)
            if part == 0:
                return

            def put(ref, start, j):
                for r in range(KV):
                    row = start + r * HEAD_DIM
                    ref[row : row + HEAD_DIM, :] = gwb_ref[j, r].astype(ref.dtype)
                ref[start + kv_b : start + kv_rows, :] = gwa_ref[j].astype(ref.dtype)

            put(own_out_ref, 0, 3)
            put(beside_ref, 0, 2)
            put(third_ref, 0, 0)
            put(second_ref, 0, 1)

        def last_kernel(
            meta_ref,
            x_ref,
            own_ref,
            second_ref,
            beside_ref,
            third_ref,
            gbq_ref,
            ga0_ref,
            ga1_ref,
            cos_ref,
            sin_ref,
            wb_ref,
            wa_ref,
            normed_ref,
            gain_ref,
            dmid_ref,
            gg_ref,
            delta_ref,
            keep0_ref,
            keep1_ref,
            send0_ref,
            send1_ref,
            b_buf,
            a_buf,
            d_buf,
            g_buf,
        ):
            total = own_ref[...]
            for ref in (second_ref, beside_ref, third_ref):
                total = total + ref[...].astype(F32)
            cosine, sine = cos_ref[...], -sin_ref[...]
            rows = [rotated(gbq_ref[r], cosine, sine) for r in range(RANK_Q)]
            for r in range(KV):
                part = total[r * HEAD_DIM : (r + 1) * HEAD_DIM]
                rows.append(rotated(part, cosine, sine) if r < RANK_KV else part)
            grad_b = jnp.transpose(jnp.concatenate(rows, axis=0)).astype(BF16)
            normed = normed_ref[...]
            back = dot(grad_b, wb_ref[...], ((1,), (1,)))
            for tp in range(n_tp):
                parts = []
                for g in range(group):
                    start = kv_b + (tp * group + g) * KV
                    parts.append(jnp.zeros((RANK_Q, block), F32))
                    parts.append(total[start : start + KV])
                parts.append(jnp.zeros((a_pad - a_cols, block), F32))
                half = group // 2
                at = [tp * half + k for k in range(half)]
                own_a = [
                    (ga0_ref, ga1_ref)[k * 2 // pairs][k % (pairs // 2), : 2 * RANKS, :] for k in at
                ]
                own_a.append(jnp.zeros((a_pad - a_cols, block), F32))
                own_a = jnp.concatenate(own_a, axis=0)
                grad_a = (own_a + jnp.concatenate(parts, axis=0)).astype(BF16)
                back = back + dot(grad_a, wa_ref[tp], ((0,), (0,)))
                a_buf[tp] = dot(grad_a, normed, ((1,), (0,)))
            b_buf[...] = dot(normed, grad_b, ((0,), (0,)))
            x = x_ref[...]
            inverse = inverse_rms(x)
            normal = x * inverse
            gains = jnp.sum(back * normal, axis=0, keepdims=True)
            g_buf[...] = jnp.broadcast_to(gains, (8, width))
            scaled = back * gain_ref[0:1]
            delta = inverse * (
                scaled - normal * jnp.mean(scaled * normal, axis=-1, keepdims=True)
            )
            d_buf[...] = delta
            for j in range(n_piece):
                lanes = column(meta_ref, j)
                cut = slice(j * LANES, (j + 1) * LANES)
                delta_ref[:, lanes] = (d_buf[:, lanes] + dmid_ref[:, cut]).astype(BF16)
            row_index = lax.broadcasted_iota(jnp.int32, (16, LANES), 0)
            for lo, hi in ((0, 0), (0, 1), (1, 0), (1, 1)):
                outs = ((keep0_ref, keep1_ref), (send0_ref, send1_ref))[lo]
                tp = member(meta_ref, lo, hi)
                for near in range(n_c):
                    out = outs[near]
                    for s in range(n_f):
                        j = near * n_f + s
                        lanes = column(meta_ref, j)
                        row = pl.multiple_of((meta_ref[j] * n_tp + tp) * b_rows, b_rows)
                        for k in range(b_parts):
                            out[hi, s, k * b_rows : (k + 1) * b_rows, :] = b_buf[
                                pl.ds(row, b_rows), k * LANES : (k + 1) * LANES
                            ].astype(BF16)
                        out[hi, s, n_b : n_b + a_pad, :] = a_buf[tp, :, lanes].astype(BF16)
                        pair = jnp.where(
                            row_index == 0, g_buf[0:1, lanes], gg_ref[0:1, lanes]
                        )
                        out[hi, s, n_b + a_pad :, :] = pair.astype(BF16)

        def add_kernel(arrival, meta_ref, x_ref, d0_ref, d1_ref, d2_ref, d3_ref, out_ref):
            step = pl.program_id(0) // 2
            rows = pl.ds(pl.multiple_of((pl.program_id(0) % 2) * (block // 2), 8), block // 2)
            for i, ref in enumerate((d0_ref, d1_ref, d2_ref, d3_ref)):

                @pl.when(step == i)
                def _(ref=ref):
                    if not arrival:
                        out_ref[0] = x_ref[0] + ref[rows, :].astype(F32)
                        return
                    for j in range(n_piece):
                        lanes = column(meta_ref, j)
                        out_ref[0, :, lanes] = x_ref[0, :, lanes] + ref[
                            rows, j * LANES : (j + 1) * LANES
                        ].astype(F32)

        def split_kernel(meta_ref, keep_ref, got_ref, own_ref, send_ref):
            def total(s):
                lanes = slice(s * LANES, (s + 1) * LANES)
                return keep_ref[:, lanes].astype(F32) + got_ref[: keep_ref.shape[0], lanes].astype(
                    F32
                )

            own_ref[0] = total(0)
            own_ref[1] = total(2)

            @pl.when(lax.rem(meta_ref[AT_ME + 1], 2) == 0)
            def _():
                send_ref[0] = total(3).astype(BF16)
                send_ref[1] = total(1).astype(BF16)

            @pl.when(lax.rem(meta_ref[AT_ME + 1], 2) == 1)
            def _():
                send_ref[0] = total(1).astype(BF16)
                send_ref[1] = total(3).astype(BF16)

        def unpack_kernel(
            meta_ref, p_ref, got_ref, b_ref, a_ref, g0_ref, g1_ref, o_ref
        ):
            total = p_ref[...].astype(F32) + got_ref[...].astype(F32)
            for k in range(b_parts):
                b_ref[0, :, k * LANES : (k + 1) * LANES] = total[k * b_rows : (k + 1) * b_rows]
            a_ref[0] = total[n_b : n_b + a_cols]
            rows = total[n_b + a_pad : n_b + a_pad + 8]
            rows = pltpu.roll(rows, (n_tp - meta_ref[AT_ME]) * gain_part, 1)
            g0_ref[...] = rows[0:1, :gain_part]
            g1_ref[...] = rows[1:2, :gain_part]
            o_ref[0] = total[pack_rows:]

        core = lambda v, label="row": swap(v, "tp", n_tp, 1, "core_" + label)
        chip = lambda v, label="row": swap(v, "tp", n_tp, 2, "y_" + label)
        ctx = lambda v, label="row": swap(v, "ctx", n_c, 1, "x_" + label)
        ahead = lambda v, s, label="row": shift(v, "fsdp", n_f, s, "z_" + label)

        (pack,) = call(
            pack_kernel,
            "pack",
            [((pack_rows, LANES), BF16)],
            (w_factor_b, w_factor_a.transpose(0, 2, 1), attn_gains, ffn_gains),
        )
        o_rows_all = w_out[0].astype(BF16)
        pack = jnp.stack([pack] + [ahead(pack, s, "pack") for s in range(1, n_f)])
        o_parts = [o_rows_all] + [ahead(o_rows_all, s, "wo") for s in range(1, n_f)]
        o_parts = jnp.concatenate(o_parts, axis=0)
        gu_in = after(w_gate_up.transpose(0, 1, 3, 2), pack)
        own_gu, own_dn = call(
            big_kernel,
            "big_pack",
            [((early, LANES), BF16), ((3 * hidden - early, LANES), BF16)],
            (gu_in, w_down),
        )
        pack = jnp.stack([pack, ctx(pack, "pack")])
        far_gu = swap(own_gu, "fsdp", n_f, 2, "z_gate_up")
        dn_pair = jnp.stack([own_dn, ctx(own_dn, "down")])
        gu_across = ctx(own_gu, "gate_up")
        o_across = ctx(o_parts, "wo")
        o_parts = jnp.concatenate(
            [
                half[s * o_rows : (s + 1) * o_rows]
                for half in (o_parts, o_across)
                for s in range(n_f)
            ],
            axis=1,
        )
        own_x, own_cot, near_cot, far_cot = call(
            rows_kernel,
            "rows",
            [((block, width), F32)] * 2 + [((2 * block, width), BF16)] * 2,
            (resid_in, cotangent),
            [REMOTE] * 2,
            [pltpu.VMEM((4, block, width), F32), pltpu.SemaphoreType.DMA((5,))],
            scalars=after(meta, o_across),
        )
        pack_across, far_gu, dn_pair, o_parts, near_cot, far_cot = lax.optimization_barrier(
            (chip(pack, "pack"), far_gu, dn_pair, o_parts, near_cot, far_cot)
        )
        pair_gu = swap(jnp.stack([own_gu, far_gu]), "fsdp", n_f, 1, "z_gate_up_pair")
        pack = jnp.stack([pack, pack_across], axis=1)
        other_pack = core(pack, "pack")

        def add_rows(whole, parts, arrival):
            rows = pl.BlockSpec(
                (1, block // 2, width), lambda i, m: (0, 2 * m[AT_TP + i // 2] + i % 2, 0)
            )
            (out,) = call(
                lambda *refs: add_kernel(arrival, *refs),
                "add_rows",
                [(whole.shape, F32)],
                (whole, *parts),
                [rows] + [WHOLE] * 4,
                (),
                (2 * n_tp,),
                [rows],
            )
            return out

        def split(keep, got):
            size = keep.shape[0]
            return call(
                split_kernel,
                "split",
                [((2, size, LANES), F32), ((2, size, LANES), BF16)],
                (keep, got),
            )

        def first_step(send, label):
            return swap(send, "fsdp", n_f, 1, "z1_" + label)

        def second_step(own, got, label):
            total = own + got.astype(F32)
            return total[0], swap(total[1].astype(BF16), "fsdp", n_f, 2, "z2_" + label)

        seg_here = lax.dynamic_slice_in_dim(segment_ids[0], place * block, block, 0)
        first = jnp.sum((segment_ids[0][:, None] < seg_here[None, :]).astype(jnp.int32), axis=0)
        token = place * block + jnp.arange(block, dtype=jnp.int32)
        position = (token - first).astype(F32)
        first = (first - place * block + extra * block).reshape(1, block)
        frequency = 10000.0 ** (-2.0 * jnp.arange(HEAD_DIM // 2, dtype=F32) / HEAD_DIM)
        angles = frequency[:, None] * position[None, :]
        cosine, sine = jnp.cos(angles), jnp.sin(angles)

        weight_b, weight_a, gains, normed, a_rows, b_query, payload = call(
            factor_kernel,
            "factors",
            [
                ((width, b_cols), BF16),
                ((n_tp, a_pad, width), BF16),
                ((16, width), F32),
                ((block, width), BF16),
                ((n_tp, a_pad, block), F32),
                ((RANK_Q, HEAD_DIM, block), F32),
                ((kv_rows, block), BF16),
            ],
            (own_x, pack, other_pack, cosine, sine),
        )
        def places(value, step, chosen, label):
            pairs = [(i, i + step) for i in chosen if 0 <= i + step < n_place]
            with jax.named_scope(label):
                return lax.ppermute(value, ("ctx", "tp"), pairs)

        every, odd, even = range(n_place), range(1, n_place, 2), range(0, n_place, 2)
        second = places(payload, 2, every, "x_kv_second")
        third = places(payload, 3, odd, "x_kv_third")
        beside_kv = core(payload, "kv")
        o_own = jnp.concatenate([o_parts, chip(o_parts, "wo")], axis=0)
        second, pair_gu, gu_across = lax.optimization_barrier((second, pair_gu, gu_across))
        gu_rest = ctx(jnp.concatenate([far_gu[None], pair_gu], axis=0), "gate_up_rest")
        dn_parts = [dn_pair, ahead(dn_pair, 1, "down1")]
        beside_second = core(second, "kv_second")
        tied = lax.optimization_barrier((third, second, beside_second, beside_kv, o_own))
        wins = (*tied[:4], payload)
        o_own = tied[4]
        o_other = core(o_own, "wo")
        window = windows * block
        factor_scratch = [
            pltpu.VMEM((pairs, pair_rows, block), F32),
            pltpu.VMEM((windows, heads * KV, block), F32),
        ]
        lse, query, mixed = call(
            attention_kernel,
            "attention",
            [
                ((pairs, 2, block), F32),
                ((n_tp, group, HEAD_DIM, block), BF16),
                ((n_tp, feats, block), BF16),
            ],
            (first, a_rows, b_query, *wins),
            None,
            [
                pltpu.VMEM((windows, kv_rows, block), BF16),
                pltpu.VMEM((window, block), F32),
                pltpu.VMEM((windows, KV, HEAD_DIM, block), F32),
                pltpu.VMEM((2, window, block), F32),
                *factor_scratch,
            ],
        )
        dn_parts[1] = after(dn_parts[1], mixed)
        for s in range(2, n_f):
            dn_parts.append(ahead(dn_parts[-1], 1, "down" + str(s)))
        mid, attn_out, normed_ffn = call(
            project_kernel,
            "project",
            [((block, width), F32), ((block, width), F32), ((block, width), BF16)],
            (own_x, mixed, o_own, o_other, gains),
        )

        near_rows = (normed_ffn, core(normed_ffn, "nf"))
        far_own = chip(normed_ffn, "nf")

        far_own, gu_rest = lax.optimization_barrier((far_own, gu_rest))
        far_own, dn_parts[-1], gu_rest = lax.optimization_barrier(
            (far_own, dn_parts[-1], gu_rest)
        )
        pieces = (own_gu, far_gu, pair_gu, gu_across, gu_rest, *dn_parts)
        far_rows = (far_own, core(far_own, "nf_far"))
        whole_ht = ((3 * hidden, 2 * block), BF16)
        two_sums = [((block, width), F32), ((block, width), BF16)]
        far_ht, far_back, far_back1, weights = call(
            far_kernel,
            "feed_far",
            [whole_ht, *two_sums, ((3 * hidden, width), BF16)],
            (*far_rows, far_cot, *pieces),
            [WHOLE] * 3 + [REMOTE] * len(pieces),
            [pltpu.SemaphoreType.DMA((2 * n_piece,))],
            room=12,
        )
        across = (far_back + core(far_back1, "dn_far").astype(F32)).astype(BF16)
        near_ht, near_back, near_back1, near_out, near_out1, far_out, far_out1 = call(
            near_kernel,
            "feed_near",
            [whole_ht, *two_sums * 3],
            (after(near_rows[0], across), near_rows[1], near_cot, weights, far_ht),
            room=12,
        )
        across = chip(across, "dn")
        beside = core(near_back1, "dn_near")

        grad_args = (near_ht, far_ht, *near_rows, *far_rows, near_cot, far_cot)
        own_d, send_d = call(
            down_grad_kernel,
            "down_grad",
            [((2, n_c, hidden, LANES), F32), ((2, n_c, hidden, LANES), BF16)],
            grad_args,
            room=12,
        )
        got_d = first_step(send_d, "d")
        keep_a, send_a = call(
            gate_up_grad_kernel,
            "gate_up_grad",
            [((2 * hidden, half_width), BF16)] * 2,
            (after(grad_args[0], send_d), *grad_args[1:]),
            room=12,
        )
        got_a = ctx(send_a, "grads_a")
        across = after(across, send_a)

        delta_mid, gain_grad, grad_mixed, keep_o, send_o = call(
            middle_kernel,
            "middle",
            [
                ((block, width), F32),
                ((8, width), F32),
                ((n_tp, feats, block), BF16),
                ((2 * o_rows, width), BF16),
                ((2 * o_rows, width), BF16),
            ],
            (own_cot, near_back, beside, across, mid, gains, o_own, o_other, mixed),
        )
        near_sum = attn_out + near_out + core(after(near_out1, across), "out_near").astype(F32)
        far_sum = far_out + core(after(far_out1, across), "out_far").astype(F32)
        out_send = jnp.stack([far_sum, near_sum]).astype(BF16)
        grad_mixed = after(grad_mixed, out_send)
        rows_got = core(send_o, "go")
        out_got = chip(out_send, "out")
        back_args = (first, a_rows, b_query, *wins, lse, query, grad_mixed)
        sums = [
            ((RANK_Q, HEAD_DIM, block), F32),
            ((windows, KV, HEAD_DIM, block), F32),
            ((windows, heads * KV, block), F32),
        ]
        grad_a_out = ((pairs // 2, pair_rows, block), F32)
        back_scratch = [
            pltpu.VMEM((windows, kv_rows, block), BF16),
            pltpu.VMEM((window, block), F32),
            pltpu.VMEM((windows, KV, HEAD_DIM, block), F32),
            pltpu.VMEM((2, window, block), F32),
            pltpu.VMEM((2, window, block), F32),
            *factor_scratch,
        ]
        grad_a0, *sums_out = call(
            lambda *refs: attention_back_kernel(0, *refs),
            "attention_back_a",
            [grad_a_out] + sums,
            back_args,
            None,
            back_scratch,
        )
        sums_out[0], own_d, got_d, _ = lax.optimization_barrier(
            (sums_out[0], own_d, got_d, grad_a0)
        )
        own_d, got_d = second_step(own_d, got_d, "d")
        grad_a1, grad_bq, *sends = call(
            lambda *refs: attention_back_kernel(1, *refs),
            "attention_back_b",
            [
                grad_a_out,
                sums[0],
                ((kv_rows, block), BF16),
                ((kv_rows, block), BF16),
                ((kv_rows, block), BF16),
                ((kv_rows, block), F32),
            ],
            (*back_args, *sums_out),
            None,
            [pltpu.VMEM(shape, kind) for shape, kind in sums[1:]] + back_scratch,
        )
        *sends[:3], out_got, rows_got = lax.optimization_barrier((*sends[:3], out_got, rows_got))
        second_got = places(sends[0], -2, every, "x_kv_back_second")
        beside_got = places(sends[1], -1, every, "x_kv_back_beside")
        third_got = places(sends[2], -3, every, "x_kv_back_third")
        own_a, send_a = split(after(keep_a, sends[0]), got_a)
        got_a = first_step(send_a, "a")
        rows_o = keep_o.astype(F32) + after(rows_got, send_a).astype(F32)
        rows_keep, rows_send = rows_o[:o_rows], rows_o[o_rows:].astype(BF16)
        rows_got = chip(rows_send, "go")
        *got, got_d = lax.optimization_barrier((second_got, beside_got, third_got, got_d))
        out_rows = (out_send[::-1].astype(F32) + out_got.astype(F32)).astype(BF16)

        delta, keep0, keep1, send0, send1 = call(
            last_kernel,
            "last",
            [
                ((block, width), BF16),
                *[((2, n_f, pack_rows, LANES), BF16)] * 4,
            ],
            (
                own_x,
                sends[3],
                *got,
                grad_bq,
                grad_a0,
                grad_a1,
                cosine,
                sine,
                weight_b,
                weight_a,
                normed,
                gains,
                delta_mid,
                gain_grad,
            ),
            [WHOLE] * 16,
            [
                pltpu.VMEM((width, b_cols), F32),
                pltpu.VMEM((n_tp, a_pad, width), F32),
                pltpu.VMEM((block, width), F32),
                pltpu.VMEM((8, width), F32),
            ],
        )

        part_send = (keep1.astype(F32) + core(send1, "gp").astype(F32)).astype(BF16)
        total_d = own_d + got_d.astype(F32)
        part_send, got_a = lax.optimization_barrier((part_send, got_a))
        part_got = ctx(part_send, "gp")
        own_a, got_a = second_step(own_a, got_a, "a")
        part = keep0.astype(F32) + core(after(send0, part_send), "gp_near").astype(F32)
        rows_got, part = lax.optimization_barrier((rows_got, part))
        rows_o = rows_keep + rows_got.astype(F32)
        rows_keep, rows_send = rows_o[:, :half_width], rows_o[:, half_width:].astype(BF16)
        across_delta = chip(delta, "delta")
        rows_go = ctx(rows_send, "go")
        out_rows = after(out_rows, part_send)
        out_beside = core(out_rows, "out_rows")
        block_out = add_rows(
            resid_in, (out_rows[0], out_rows[1], out_beside[0], out_beside[1]), True
        )
        part_got, across_delta = lax.optimization_barrier((part_got, across_delta, block_out))[:2]
        part = part + part_got.astype(F32)
        part_send = part[1].astype(BF16)
        part_got = chip(part_send, "gp")
        across_delta = after(across_delta, part_send)
        beside_delta = core(after(delta, part_send), "delta")
        got_last = ctx(after(total_d[1], part_send).astype(BF16), "d")
        part_got, rows_go, got_a = lax.optimization_barrier((part_got, rows_go, got_a))
        part = part[0] + part_got.astype(F32)
        rows_o = rows_keep + rows_go.astype(F32)
        part = [
            jnp.concatenate([part[s], rows_o[:, s * LANES : (s + 1) * LANES]], axis=0)
            for s in range(n_f)
        ]
        is_even_f = f_index % 2 == 0
        part_send = [
            jnp.where(is_even_f, part[3], part[1]),
            jnp.where(is_even_f, part[1], part[3]),
        ]
        part_send = jnp.stack(part_send).astype(BF16)
        part_own, part_got = second_step(
            jnp.stack([part[0], part[2]]), first_step(part_send, "gp"), "gp"
        )
        across_delta = after(across_delta, part_send)
        resid_grad = add_rows(
            cotangent,
            (delta, across_delta, beside_delta, core(across_delta, "delta_far")),
            False,
        )
        part_got, got_last = lax.optimization_barrier((part_got, got_last, resid_grad))[:2]
        grad_down = total_d[0] + got_last.astype(F32)
        grad_gate_up = (own_a + got_a.astype(F32)).reshape(1, 2, hidden, fc_cols)
        part_b, part_a, part_g0, part_g1, grad_out = call(
            unpack_kernel,
            "unpack",
            [
                ((1, b_rows, b_cols), F32),
                ((1, a_cols, fc_cols), F32),
                ((1, gain_part), F32),
                ((1, gain_part), F32),
                ((1, o_rows, LANES), F32),
            ],
            (part_own, part_got),
        )
        return (
            block_out,
            resid_grad,
            part_a.transpose(0, 2, 1),
            part_b,
            grad_out,
            grad_gate_up.transpose(0, 1, 3, 2),
            grad_down[None],
            part_g0,
            part_g1,
        )

    return shards


def make_shards(mesh):
    fused, general = make_fused(mesh), make_general(mesh)
    fits = mesh.shape["fsdp"] == 4 and mesh.shape["ctx"] == 2 and mesh.shape["tp"] == 4

    def shards(*args):
        return (fused if fits and args[7].shape[2] == LANES else general)(*args)

    return shards


def solution(mesh):
    return jax.shard_map(
        make_shards(mesh),
        mesh=mesh,
        in_specs=(
            P("fsdp", "ctx", None),
            P("fsdp", None),
            P("fsdp", "ctx", None),
            P(None, ("fsdp", "ctx"), "tp"),
            P(None, ("fsdp", "ctx", "tp"), None),
            P(None, "tp", ("fsdp", "ctx")),
            P(None, None, ("fsdp", "ctx"), "tp"),
            P(None, "tp", ("fsdp", "ctx")),
            P(None, ("fsdp", "ctx", "tp")),
            P(None, ("fsdp", "ctx", "tp")),
        ),
        out_specs=(
            P("fsdp", "ctx", None),
            P("fsdp", "ctx", None),
            P(None, ("fsdp", "ctx"), "tp"),
            P(None, ("fsdp", "ctx", "tp"), None),
            P(None, "tp", ("fsdp", "ctx")),
            P(None, None, ("fsdp", "ctx"), "tp"),
            P(None, "tp", ("fsdp", "ctx")),
            P(None, ("fsdp", "ctx", "tp")),
            P(None, ("fsdp", "ctx", "tp")),
        ),
        check_vma=False,
    )
```

profile of v0, /device:TPU:0, one launch (start us, length us, event | category | flops | bytes accessed | tf_op | source)
XLA Modules:
  0.0 214.2 jit_solution(6772122234260497253)
XLA Ops:
  4.5 5.0 %collective-permute-start.6 = (bf16[224,128]{1,0:T(8,128)(2,1)S(1)}, bf16[224,128]{1,0:T(8,128)(2,1)S(1)}, u32[]{:S(2)}, u32[]{:S(2)}) collective-permute-start(bf16[224,128]{1,0:T(8,128)(2,1)S(1)} %pack.1), channel_id=1, source_target_pairs={{0,24},{8,0},{16,8},{24,16},{1,25},{9,1},{17,9},{25,17},{2,26},{10... | collective-permute-start | bytes 172040 | tf_op jit(solution)/shard_map/z_pack/ppermute | solution.py:39
  11.5 2.9 %collective-permute-start.2 = (bf16[256,128]{1,0:T(8,128)(2,1)S(1)}, bf16[256,128]{1,0:T(8,128)(2,1)S(1)}, u32[]{:S(2)}, u32[]{:S(2)}) collective-permute-start(bf16[256,128]{1,0:T(8,128)(2,1)S(1)} %get-tuple-element.250), channel_id=1, source_target_pairs={{0,24},{8,0},{16,8},{24,16},{1,25},{9,1},{17,9},{25,17},{2,26},{10... | collective-permute-start | bytes 196616 | tf_op jit(solution)/shard_map/z_wo/ppermute | solution.py:39
  19.0 3.1 %collective-permute-start.9 = (bf16[1584,128]{1,0:T(8,128)(2,1)S(1)}, bf16[1584,128]{1,0:T(8,128)(2,1)S(1)}, u32[]{:S(2)}, u32[]{:S(2)}) collective-permute-start(bf16[1584,128]{1,0:T(8,128)(2,1)S(1)} %get-tuple-element.132.refs_0_), channel_id=1, source_target_pairs={{0,16},{8,24},{16,0},{24,8},{1,17},{9,25},{17,1},{25,9},{2,18},{10... | collective-permute-start | bytes 1216520 | tf_op jit(solution)/shard_map/z_gate_up/ppermute | solution.py:44
  24.1 3.7 %collective-permute-done.10 = bf16[528,128]{1,0:T(8,128)(2,1)S(1)} collective-permute-done((bf16[528,128]{1,0:T(8,128)(2,1)S(1)}, bf16[528,128]{1,0:T(8,128)(2,1)S(1)}, u32[]{:S(2)}, u32[]{:S(2)}) %collective-permute-start.10) | collective-permute-done | bytes 135200 | tf_op jit(solution)/shard_map/x_down/ppermute | solution.py:44
  30.8 3.2 %rows.1 = (f32[256,1024]{1,0:T(8,128)S(1)}, f32[256,1024]{1,0:T(8,128)S(1)}, bf16[512,1024]{1,0:T(8,128)(2,1)S(1)}, bf16[512,1024]{1,0:T(8,128)(2,1)S(1)}) custom-call(s32[15]{0:T(128)S(1)} %stack.138.meta_ref.refs_0_, f32[1,1024,1024]{2,1,0:T(8,128)} %refs_1_.2, f32[1,1024,1024]{2,1,0:T(8,128)} %refs_1_.3), custom_call_target="tpu_custom_call" | custom-call | tf_op jit(solution)/shard_map/rows/pallas_call | solution.py:663
  34.1 4.5 %collective-permute-done.9.refs_1_ = bf16[1584,128]{1,0:T(8,128)(2,1)S(1)} collective-permute-done((bf16[1584,128]{1,0:T(8,128)(2,1)S(1)}, bf16[1584,128]{1,0:T(8,128)(2,1)S(1)}, u32[]{:S(2)}, u32[]{:S(2)}) %collective-permute-start.9) | collective-permute-done | bytes 405536 | tf_op jit(solution)/shard_map/z_gate_up/ppermute | solution.py:44
  48.1 4.1 %collective-permute-done.15.refs_3_ = bf16[1584,128]{1,0:T(8,128)(2,1)S(1)} collective-permute-done((bf16[1584,128]{1,0:T(8,128)(2,1)S(1)}, bf16[1584,128]{1,0:T(8,128)(2,1)S(1)}, u32[]{:S(2)}, u32[]{:S(2)}) %collective-permute-start.15) | collective-permute-done | bytes 405536 | tf_op jit(solution)/shard_map/x_gate_up/ppermute | solution.py:44
  52.8 6.6 %collective-permute-done.14.refs_2_ = bf16[2,1584,128]{2,1,0:T(8,128)(2,1)S(1)} collective-permute-done((bf16[2,1584,128]{2,1,0:T(8,128)(2,1)S(1)}, bf16[2,1584,128]{2,1,0:T(8,128)(2,1)S(1)}, u32[]{:S(2)}, u32[]{:S(2)}) %collective-permute-start.14) | collective-permute-done | bytes 811040 | tf_op jit(solution)/shard_map/z_gate_up_pair/ppermute | solution.py:44
  63.4 12.0 %attention.1 = (f32[8,2,256]{2,1,0:T(2,128)S(1)}, bf16[4,4,64,256]{3,2,1,0:T(8,128)(2,1)S(1)}, bf16[4,256,256]{2,1,0:T(8,128)(2,1)S(1)}) custom-call(s32[15]{0:T(128)S(1)} %stack.138.meta_ref.refs_0_, s32[1,256]{1,0:T(1,128)S(1)} %bitcast.105, f32[4,48,256]{2,1,0:T(8,128)S(1)} %get-tuple-element.137.a_ref.refs_2_, ...), custom_call_target="tpu_custom_call" | custom-call | tf_op jit(solution)/shard_map/attention/pallas_call | solution.py:663
  81.1 4.4 %collective-permute-done.23.refs_7_ = bf16[2,528,128]{2,1,0:T(8,128)(2,1)S(1)} collective-permute-done((bf16[2,528,128]{2,1,0:T(8,128)(2,1)S(1)}, bf16[2,528,128]{2,1,0:T(8,128)(2,1)S(1)}, u32[]{:S(2)}, u32[]{:S(2)}) %collective-permute-start.23) | collective-permute-done | bytes 270368 | tf_op jit(solution)/shard_map/z_down2/ppermute | solution.py:39
  86.3 3.9 %collective-permute-done.21.refs_4_ = bf16[3,1584,128]{2,1,0:T(8,128)(2,1)S(1)} collective-permute-done((bf16[3,1584,128]{2,1,0:T(8,128)(2,1)S(1)}, bf16[3,1584,128]{2,1,0:T(8,128)(2,1)S(1)}, u32[]{:S(2)}, u32[]{:S(2)}) %collective-permute-start.21) | collective-permute-done | bytes 1216544 | tf_op jit(solution)/shard_map/x_gate_up_rest/ppermute | solution.py:44
  96.5 6.4 %feed_far.1 = (bf16[2112,512]{1,0:T(8,128)(2,1)S(1)}, f32[256,1024]{1,0:T(8,128)S(1)}, bf16[256,1024]{1,0:T(8,128)(2,1)S(1)}, bf16[2112,1024]{1,0:T(8,128)(2,1)S(1)}) custom-call(s32[15]{0:T(128)S(1)} %stack.138.meta_ref.refs_0_, bf16[256,1024]{1,0:T(8,128)(2,1)S(1)} %collective-permute-done.20.n0_ref.refs_4_, ...), custom_call_target="tpu_custom_call" | custom-call | tf_op jit(solution)/shard_map/feed_far/pallas_call | solution.py:663
  106.6 6.6 %feed_near.1 = (bf16[2112,512]{1,0:T(8,128)(2,1)S(1)}, f32[256,1024]{1,0:T(8,128)S(1)}, bf16[256,1024]{1,0:T(8,128)(2,1)S(1)}, f32[256,1024]{1,0:T(8,128)S(1)}, ...) custom-call(s32[15]{0:T(128)S(1)} %stack.138.meta_ref.refs_0_, ...), custom_call_target="tpu_custom_call" | custom-call | tf_op jit(solution)/shard_map/feed_near/pallas_call | solution.py:663
  115.7 3.7 %gate_up_grad.1 = (bf16[1408,512]{1,0:T(8,128)(2,1)S(1)}, bf16[1408,512]{1,0:T(8,128)(2,1)S(1)}) custom-call(s32[15]{0:T(128)S(1)} %stack.138.meta_ref.refs_0_, bf16[2112,512]{1,0:T(8,128)(2,1)S(1)} %get-tuple-element.171.refs_0_, bf16[2112,512]{1,0:T(8,128)(2,1)S(1)} %get-tuple-element.166.far_ht_ref.refs_1_, ...), custom_call_target="tpu_custom_call" | custom-call | tf_op jit(solution)/shard_map/gate_up_grad/pallas_call | solution.py:663
  125.3 9.6 %attention_back_a.1 = (f32[4,24,256]{2,1,0:T(8,128)S(1)}, f32[6,64,256]{2,1,0:T(8,128)S(1)}, f32[4,4,64,256]{3,2,1,0:T(8,128)S(1)}, f32[4,64,256]{2,1,0:T(8,128)S(1)}) custom-call(s32[15]{0:T(128)S(1)} %stack.138.meta_ref.refs_0_, s32[1,256]{1,0:T(1,128)S(1)} %bitcast.106, f32[4,48,256]{2,1,0:T(8,128)S(1)} %get-tuple-element.137.a_ref.refs_2_, ...), custom_call_target="tpu_custom_call" | custom-call | tf_op jit(solution)/shard_map/attention_back_a/pallas_call | solution.py:663
  134.9 3.7 %collective-permute-done.32 = bf16[2,2,704,128]{3,2,1,0:T(8,128)(2,1)S(1)} collective-permute-done((bf16[2,2,704,128]{3,2,1,0:T(8,128)(2,1)S(1)}, bf16[2,2,704,128]{3,2,1,0:T(8,128)(2,1)S(1)}, u32[]{:S(2)}, u32[]{:S(2)}) %collective-permute-start.32) | collective-permute-done | bytes 720928 | tf_op jit(solution)/shard_map/z1_d/ppermute | solution.py:44
  138.9 9.5 %attention_back_b.1 = (f32[4,24,256]{2,1,0:T(8,128)S(1)}, f32[6,64,256]{2,1,0:T(8,128)S(1)}, bf16[320,256]{1,0:T(8,128)(2,1)S(1)}, bf16[320,256]{1,0:T(8,128)(2,...) custom-call(s32[15]{0:T(128)S(1)} %stack.138.meta_ref.refs_0_, s32[1,256]{1,0:T(1,128)S(1)} %bitcast.107, ...), custom_call_target="tpu_custom_call" | custom-call | tf_op jit(solution)/shard_map/attention_back_b/pallas_call | solution.py:663
  151.2 2.9 %collective-permute-done.40.got_ref = bf16[1408,512]{1,0:T(8,128)(2,1)S(1)} collective-permute-done((bf16[1408,512]{1,0:T(8,128)(2,1)S(1)}, bf16[1408,512]{1,0:T(8,128)(2,1)S(1)}, u32[]{:S(2)}, u32[]{:S(2)}) %collective-permute-start.40) | collective-permute-done | bytes 1441824 | tf_op jit(solution)/shard_map/x_grads_a/ppermute | solution.py:44
  161.5 4.2 %collective-permute-done.37.third_ref = bf16[320,256]{1,0:T(8,128)(2,1)S(1)} collective-permute-done((bf16[320,256]{1,0:T(8,128)(2,1)S(1)}, bf16[320,256]{1,0:T(8,128)(2,1)S(1)}, u32[]{:S(2)}, u32[]{:S(2)}) %collective-permute-start.37) | collective-permute-done | bytes 163872 | tf_op jit(solution)/shard_map/x_kv_back_third/ppermute | solution.py:1389
  165.7 3.0 %last.1 = (bf16[256,1024]{1,0:T(8,128)(2,1)S(1)}, bf16[2,4,224,128]{3,2,1,0:T(8,128)(2,1)S(1)}, bf16[2,4,224,128]{3,2,1,0:T(8,128)(2,1)S(1)}, bf16[2,4,224,128]{...) custom-call(s32[15]{0:T(128)S(1)} %stack.138.meta_ref.refs_0_, f32[256,1024]{1,0:T(8,128)S(1)} %get-tuple-element.130.x_ref, ...), custom_call_target="tpu_custom_call" | custom-call | tf_op jit(solution)/shard_map/last/pallas_call | solution.py:663
  178.8 7.4 %add_rows.2 = f32[1,1024,1024]{2,1,0:T(8,128)} custom-call(s32[15]{0:T(128)S(1)} %stack.138.meta_ref.refs_0_, f32[1,1024,1024]{2,1,0:T(8,128)} %refs_1_.2, bf16[256,1024]{1,0:T(8,128)(2,1)S(1)} %get-tuple-element.254.refs_2_, bf16[256,1024]{1,0:T(8,128)(2,1)S(1)} %get-tuple-element.253.refs_3_, bf16[256,1024]{1,0:T(8,128)(2,1)S(1)} %get-tuple-element.252.refs_4_, ...), custom_call_target="tpu_custom_call" | custom-call | tf_op jit(solution)/shard_map/add_rows/pallas_call | solution.py:663
  190.0 4.8 %collective-permute-done.49 = bf16[1408,128]{1,0:T(8,128)(2,1)S(1)} collective-permute-done((bf16[1408,128]{1,0:T(8,128)(2,1)S(1)}, bf16[1408,128]{1,0:T(8,128)(2,1)S(1)}, u32[]{:S(2)}, u32[]{:S(2)}) %collective-permute-start.49) | collective-permute-done | bytes 360480 | tf_op jit(solution)/shard_map/z2_a/ppermute | solution.py:44
  197.4 7.0 %collective-permute-done.52 = bf16[2,480,128]{2,1,0:T(8,128)(2,1)S(1)} collective-permute-done((bf16[2,480,128]{2,1,0:T(8,128)(2,1)S(1)}, bf16[2,480,128]{2,1,0:T(8,128)(2,1)S(1)}, u32[]{:S(2)}, u32[]{:S(2)}) %collective-permute-start.52) | collective-permute-done | bytes 245792 | tf_op jit(solution)/shard_map/z1_gp/ppermute | solution.py:44
  204.6 7.3 %add_rows.3 = f32[1,1024,1024]{2,1,0:T(8,128)} custom-call(s32[15]{0:T(128)S(1)} %stack.138.meta_ref.refs_0_, f32[1,1024,1024]{2,1,0:T(8,128)} %refs_1_.3, bf16[256,1024]{1,0:T(8,128)(2,1)S(1)} %get-tuple-element.238.refs_2_, bf16[256,1024]{1,0:T(8,128)(2,1)S(1)} %collective-permute-done.44.refs_3_, bf16[256,1024]{1,0:T(8,128)(2,1)S(1)} %collective-permute-done.50.refs_4_, ...), custom_call_target="tpu_custom_call" | custom-call | tf_op jit(solution)/shard_map/add_rows/pallas_call | solution.py:663
  (175 shorter events, 83.3 us)
Async XLA Ops:
  4.5 11.7 %collective-permute-start.6 = (bf16[224,128]{1,0:T(8,128)(2,1)S(1)}, bf16[224,128]{1,0:T(8,128)(2,1)S(1)}, u32[]{:S(2)}, u32[]{:S(2)}) collective-permute-start(bf16[224,128]{1,0:T(8,128)(2,1)S(1)} %pack.1), channel_id=1, source_target_pairs={{0,24},{8,0},{16,8},{24,16},{1,25},{9,1},{17,9},{25,17},{2,26},{10... | collective-permute-start | bytes 172040 | tf_op jit(solution)/shard_map/z_pack/ppermute | solution.py:39
  19.0 19.6 %collective-permute-start.9 = (bf16[1584,128]{1,0:T(8,128)(2,1)S(1)}, bf16[1584,128]{1,0:T(8,128)(2,1)S(1)}, u32[]{:S(2)}, u32[]{:S(2)}) collective-permute-start(bf16[1584,128]{1,0:T(8,128)(2,1)S(1)} %get-tuple-element.132.refs_0_), channel_id=1, source_target_pairs={{0,16},{8,24},{16,0},{24,8},{1,17},{9,25},{17,1},{25,9},{2,18},{10... | collective-permute-start | bytes 1216520 | tf_op jit(solution)/shard_map/z_gate_up/ppermute | solution.py:44
  38.8 20.5 %collective-permute-start.14 = (bf16[2,1584,128]{2,1,0:T(8,128)(2,1)S(1)}, bf16[2,1584,128]{2,1,0:T(8,128)(2,1)S(1)}, u32[]{:S(2)}, u32[]{:S(2)}) collective-permute-start(bf16[2,1584,128]{2,1,0:T(8,128)(2,1)S(1)} %pad_maximum_fusion.4), channel_id=1, source_target_pairs={{0,8},{8,0},{16,24},{24,16},{1,9},{9,1},{17,25},{25,17},{2,10},{10... | collective-permute-start | bytes 2433032 | tf_op jit(solution)/shard_map/z_gate_up_pair/ppermute | solution.py:44
  41.7 17.7 %collective-permute-start.18 = (bf16[256,1024]{1,0:T(8,128)(2,1)S(1)}, bf16[256,1024]{1,0:T(8,128)(2,1)S(1)}, u32[]{:S(2)}, u32[]{:S(2)}) collective-permute-start(bf16[256,1024]{1,0:T(8,128)(2,1)S(1)} %slice_dynamic-update-slice_fusion), channel_id=1, source_target_pairs={{0,2},{1,3},{2,0},{3,1},{4,6},{5,7},{6,4},{7,5},{8,10},{9,11},{10,... | collective-permute-start | bytes 1572872 | tf_op jit(solution)/shard_map/y_wo/ppermute | solution.py:44
  45.5 13.8 %collective-permute-start.13 = (bf16[320,256]{1,0:T(8,128)(2,1)S(1)}, bf16[320,256]{1,0:T(8,128)(2,1)S(1)}, u32[]{:S(2)}, u32[]{:S(2)}) collective-permute-start(bf16[320,256]{1,0:T(8,128)(2,1)S(1)} %get-tuple-element.139.w4_ref.refs_8_), channel_id=1, source_target_pairs={{0,2},{1,3},{2,4},{3,5},{4,6},{5,7},{8,10},{9,11},{10,12},{11,13},... | collective-permute-start | bytes 491528 | tf_op jit(solution)/shard_map/x_kv_second/ppermute | solution.py:1389
  60.8 17.3 %collective-permute-start.19 = (bf16[512,1024]{1,0:T(8,128)(2,1)S(1)}, bf16[512,1024]{1,0:T(8,128)(2,1)S(1)}, u32[]{:S(2)}, u32[]{:S(2)}) collective-permute-start(bf16[512,1024]{1,0:T(8,128)(2,1)S(1)} %pad_maximum_fusion.1.o0_ref), channel_id=1, source_target_pairs={{0,1},{1,0},{2,3},{3,2},{4,5},{5,4},{6,7},{7,6},{8,9},{9,8},{10,11... | collective-permute-start | bytes 3145736 | tf_op jit(solution)/shard_map/core_wo/ppermute | solution.py:44
  61.0 29.1 %collective-permute-start.21 = (bf16[3,1584,128]{2,1,0:T(8,128)(2,1)S(1)}, bf16[3,1584,128]{2,1,0:T(8,128)(2,1)S(1)}, u32[]{:S(2)}, u32[]{:S(2)}) collective-permute-start(bf16[3,1584,128]{2,1,0:T(8,128)(2,1)S(1)} %pad_maximum_fusion), channel_id=1, source_target_pairs={{0,4},{4,0},{1,5},{5,1},{2,6},{6,2},{3,7},{7,3},{8,12},{12,8},{9,1... | collective-permute-start | bytes 3649544 | tf_op jit(solution)/shard_map/x_gate_up_rest/ppermute | solution.py:44
  62.6 12.8 %collective-permute-start.22 = (bf16[2,528,128]{2,1,0:T(8,128)(2,1)S(1)}, bf16[2,528,128]{2,1,0:T(8,128)(2,1)S(1)}, u32[]{:S(2)}, u32[]{:S(2)}) collective-permute-start(bf16[2,528,128]{2,1,0:T(8,128)(2,1)S(1)} %pad_maximum_fusion.6.refs_5_), channel_id=1, source_target_pairs={{0,8},{8,16},{16,24},{24,0},{1,9},{9,17},{17,25},{25,1},{2,10},{10... | collective-permute-start | bytes 811016 | tf_op jit(solution)/shard_map/z_down1/ppermute | solution.py:39
  79.5 13.4 %collective-permute-start.20 = (bf16[256,1024]{1,0:T(8,128)(2,1)S(1)}, bf16[256,1024]{1,0:T(8,128)(2,1)S(1)}, u32[]{:S(2)}, u32[]{:S(2)}) collective-permute-start(bf16[256,1024]{1,0:T(8,128)(2,1)S(1)} %get-tuple-element.163.n0_ref.refs_2_), channel_id=1, source_target_pairs={{0,2},{1,3},{2,0},{3,1},{4,6},{5,7},{6,4},{7,5},{8,10},{9,11},{10,... | collective-permute-start | bytes 1572872 | tf_op jit(solution)/shard_map/y_nf/ppermute | solution.py:44
  105.0 14.5 %collective-permute-start.28 = (bf16[256,1024]{1,0:T(8,128)(2,1)S(1)}, bf16[256,1024]{1,0:T(8,128)(2,1)S(1)}, u32[]{:S(2)}, u32[]{:S(2)}) collective-permute-start(bf16[256,1024]{1,0:T(8,128)(2,1)S(1)} %add_convert_fusion.3), channel_id=1, source_target_pairs={{0,2},{1,3},{2,0},{3,1},{4,6},{5,7},{6,4},{7,5},{8,10},{9,11},{10,... | collective-permute-start | bytes 1572872 | tf_op jit(solution)/shard_map/y_dn/ppermute | solution.py:44
  120.1 18.5 %collective-permute-start.32 = (bf16[2,2,704,128]{3,2,1,0:T(8,128)(2,1)S(1)}, bf16[2,2,704,128]{3,2,1,0:T(8,128)(2,1)S(1)}, u32[]{:S(2)}, u32[]{:S(2)}) collective-permute-start(bf16[2,2,704,128]{3,2,1,0:T(8,128)(2,1)S(1)} %get-tuple-element.170), channel_id=1, source_target_pairs={{0,8},{8,0},{16,24},{24,16},{1,9},{9,1},{17,25},{25,17},{2,10},{10... | collective-permute-start | bytes 2162696 | tf_op jit(solution)/shard_map/z1_d/ppermute | solution.py:44
  120.1 33.9 %collective-permute-start.40 = (bf16[1408,512]{1,0:T(8,128)(2,1)S(1)}, bf16[1408,512]{1,0:T(8,128)(2,1)S(1)}, u32[]{:S(2)}, u32[]{:S(2)}) collective-permute-start(bf16[1408,512]{1,0:T(8,128)(2,1)S(1)} %get-tuple-element.172), channel_id=1, source_target_pairs={{0,4},{4,0},{1,5},{5,1},{2,6},{6,2},{3,7},{7,3},{8,12},{12,8},{9,1... | collective-permute-start | bytes 4325384 | tf_op jit(solution)/shard_map/x_grads_a/ppermute | solution.py:44
  123.7 24.8 %collective-permute-start.34 = (bf16[512,1024]{1,0:T(8,128)(2,1)S(1)}, bf16[512,1024]{1,0:T(8,128)(2,1)S(1)}, u32[]{:S(2)}, u32[]{:S(2)}) collective-permute-start(bf16[512,1024]{1,0:T(8,128)(2,1)S(1)} %get-tuple-element.196), channel_id=1, source_target_pairs={{0,1},{1,0},{2,3},{3,2},{4,5},{5,4},{6,7},{7,6},{8,9},{9,8},{10,11... | collective-permute-start | bytes 3145736 | tf_op jit(solution)/shard_map/core_go/ppermute | solution.py:44
  124.5 25.5 %collective-permute-start.33 = (bf16[2,256,1024]{2,1,0:T(8,128)(2,1)S(1)}, bf16[2,256,1024]{2,1,0:T(8,128)(2,1)S(1)}, u32[]{:S(2)}, u32[]{:S(2)}) collective-permute-start(bf16[2,256,1024]{2,1,0:T(8,128)(2,1)S(1)} %pad_maximum_fusion.2), channel_id=1, source_target_pairs={{0,2},{1,3},{2,0},{3,1},{4,6},{5,7},{6,4},{7,5},{8,10},{9,11},{10,... | collective-permute-start | bytes 3145736 | tf_op jit(solution)/shard_map/y_out/ppermute | solution.py:44
  138.8 21.3 %collective-permute-start.38 = (bf16[2,704,128]{2,1,0:T(8,128)(2,1)S(1)}, bf16[2,704,128]{2,1,0:T(8,128)(2,1)S(1)}, u32[]{:S(2)}, u32[]{:S(2)}) collective-permute-start(bf16[2,704,128]{2,1,0:T(8,128)(2,1)S(1)} %fusion.5), channel_id=1, source_target_pairs={{0,16},{8,24},{16,0},{24,8},{1,17},{9,25},{17,1},{25,9},{2,18},{10... | collective-permute-start | bytes 1081352 | tf_op jit(solution)/shard_map/z2_d/ppermute | solution.py:44
  149.9 15.8 %collective-permute-start.35 = (bf16[320,256]{1,0:T(8,128)(2,1)S(1)}, bf16[320,256]{1,0:T(8,128)(2,1)S(1)}, u32[]{:S(2)}, u32[]{:S(2)}) collective-permute-start(bf16[320,256]{1,0:T(8,128)(2,1)S(1)} %get-tuple-element.199), channel_id=1, source_target_pairs={{2,0},{3,1},{4,2},{5,3},{6,4},{7,5},{10,8},{11,9},{12,10},{13,11},... | collective-permute-start | bytes 491528 | tf_op jit(solution)/shard_map/x_kv_back_second/ppermute | solution.py:1389
  155.0 17.8 %collective-permute-start.41 = (bf16[2,1408,128]{2,1,0:T(8,128)(2,1)S(1)}, bf16[2,1408,128]{2,1,0:T(8,128)(2,1)S(1)}, u32[]{:S(2)}, u32[]{:S(2)}) collective-permute-start(bf16[2,1408,128]{2,1,0:T(8,128)(2,1)S(1)} %get-tuple-element.218), channel_id=1, source_target_pairs={{0,8},{8,0},{16,24},{24,16},{1,9},{9,1},{17,25},{25,17},{2,10},{10... | collective-permute-start | bytes 2162696 | tf_op jit(solution)/shard_map/z1_a/ppermute | solution.py:44
  160.1 15.7 %collective-permute-start.45 = (bf16[256,1024]{1,0:T(8,128)(2,1)S(1)}, bf16[256,1024]{1,0:T(8,128)(2,1)S(1)}, u32[]{:S(2)}, u32[]{:S(2)}) collective-permute-start(bf16[256,1024]{1,0:T(8,128)(2,1)S(1)} %slice.198), channel_id=1, source_target_pairs={{0,2},{1,3},{2,0},{3,1},{4,6},{5,7},{6,4},{7,5},{8,10},{9,11},{10,... | collective-permute-start | bytes 1572872 | tf_op jit(solution)/shard_map/y_go/ppermute | solution.py:44
  170.9 15.7 %collective-permute-start.44 = (bf16[256,1024]{1,0:T(8,128)(2,1)S(1)}, bf16[256,1024]{1,0:T(8,128)(2,1)S(1)}, u32[]{:S(2)}, u32[]{:S(2)}) collective-permute-start(bf16[256,1024]{1,0:T(8,128)(2,1)S(1)} %get-tuple-element.238.refs_2_), channel_id=1, source_target_pairs={{0,2},{1,3},{2,0},{3,1},{4,6},{5,7},{6,4},{7,5},{8,10},{9,11},{10,... | collective-permute-start | bytes 1572872 | tf_op jit(solution)/shard_map/y_delta/ppermute | solution.py:44
  172.8 13.8 %collective-permute-start.43 = (bf16[2,4,224,128]{3,2,1,0:T(8,128)(2,1)S(1)}, bf16[2,4,224,128]{3,2,1,0:T(8,128)(2,1)S(1)}, u32[]{:S(2)}, u32[]{:S(2)}) collective-permute-start(bf16[2,4,224,128]{3,2,1,0:T(8,128)(2,1)S(1)} %add_convert_fusion.4), channel_id=1, source_target_pairs={{0,4},{4,0},{1,5},{5,1},{2,6},{6,2},{3,7},{7,3},{8,12},{12,8},{9,1... | collective-permute-start | bytes 1376264 | tf_op jit(solution)/shard_map/x_gp/ppermute | solution.py:44
  175.7 19.1 %collective-permute-start.49 = (bf16[1408,128]{1,0:T(8,128)(2,1)S(1)}, bf16[1408,128]{1,0:T(8,128)(2,1)S(1)}, u32[]{:S(2)}, u32[]{:S(2)}) collective-permute-start(bf16[1408,128]{1,0:T(8,128)(2,1)S(1)} %fusion.6), channel_id=1, source_target_pairs={{0,16},{8,24},{16,0},{24,8},{1,17},{9,25},{17,1},{25,9},{2,18},{10... | collective-permute-start | bytes 1081352 | tf_op jit(solution)/shard_map/z2_a/ppermute | solution.py:44
  176.1 18.7 %collective-permute-start.48 = (bf16[256,512]{1,0:T(8,128)(2,1)S(1)}, bf16[256,512]{1,0:T(8,128)(2,1)S(1)}, u32[]{:S(2)}, u32[]{:S(2)}) collective-permute-start(bf16[256,512]{1,0:T(8,128)(2,1)S(1)} %slice.199), channel_id=1, source_target_pairs={{0,4},{4,0},{1,5},{5,1},{2,6},{6,2},{3,7},{7,3},{8,12},{12,8},{9,1... | collective-permute-start | bytes 786440 | tf_op jit(solution)/shard_map/x_go/ppermute | solution.py:44
  189.3 22.5 %collective-permute-start.54 = (bf16[704,128]{1,0:T(8,128)(2,1)S(1)}, bf16[704,128]{1,0:T(8,128)(2,1)S(1)}, u32[]{:S(2)}, u32[]{:S(2)}) collective-permute-start(bf16[704,128]{1,0:T(8,128)(2,1)S(1)} %slice_bitcast_fusion.8), channel_id=1, source_target_pairs={{0,4},{4,0},{1,5},{5,1},{2,6},{6,2},{3,7},{7,3},{8,12},{12,8},{9,1... | collective-permute-start | bytes 540680 | tf_op jit(solution)/shard_map/x_d/ppermute | solution.py:44
  190.0 14.6 %collective-permute-start.50 = (bf16[256,1024]{1,0:T(8,128)(2,1)S(1)}, bf16[256,1024]{1,0:T(8,128)(2,1)S(1)}, u32[]{:S(2)}, u32[]{:S(2)}) collective-permute-start(bf16[256,1024]{1,0:T(8,128)(2,1)S(1)} %get-tuple-element.238.refs_2_), channel_id=1, source_target_pairs={{0,1},{1,0},{2,3},{3,2},{4,5},{5,4},{6,7},{7,6},{8,9},{9,8},{10,11... | collective-permute-start | bytes 1572872 | tf_op jit(solution)/shard_map/core_delta/ppermute | solution.py:44
  (38 other events, 246.9 us)
where the time goes:
time: 215 us; the launch traced here: 214 us
  Pallas kernels  80.7 us (38%)
  waiting for transfers between devices  65 us (30%)
  starting transfers between devices  56.3 us (26%)
  other arithmetic  6.33 us (3%)
  local copies, waits for them, and re-layouts  4.42 us (2%)
    pallas_call x18, Pallas kernels, call(): pl.pallas_call(kernel, out_shape=[jax.ShapeDtypeStruct(s, d) for s, d in...  80.7 us
    ppermute x41, waiting for transfers between devices, swap(): return lax.ppermute(value, axis, [(i, i ^ bit) for i in range(size)])  54.4 us
    ppermute x41, starting transfers between devices, swap(): return lax.ppermute(value, axis, [(i, i ^ bit) for i in range(size)])  34.8 us
    ppermute x9, starting transfers between devices, shift(): lax.ppermute(value, axes, [(i, (i + step) % size) for i in range(size)])  14.3 us
    ppermute x5, starting transfers between devices, places(): return lax.ppermute(value, ('ctx', 'tp'), pairs)  7.19 us
    ppermute x9, waiting for transfers between devices, shift(): lax.ppermute(value, axes, [(i, (i + step) % size) for i in range(size)])  6.43 us
  transfers between devices with their start and end apart: 55, of which 26 were waited for; matrix products, arithmetic and copies ran while one was open for 3% of the time, Pallas kernels for 34%

commit v1 on v0

--- a/solution.py
+++ b/solution.py
@@ -613,6 +613,7 @@
         kv_rows = kv_b + heads * KV
         half_width = width // n_c
         pairs = heads // 2
+        first_part = 5 * pairs // 8
         pair_rows = 8 * (-(-2 * RANKS // 8))
         early = 2 * hidden + 16 * (hidden // 64)
         assert n_f == 4 and fc_cols == LANES and o_rows == feats and n_tp == 4 and n_c == 2
@@ -818,7 +819,7 @@
             spread_factors(a_ref, win_ref, own_ref, kv_ref)
             spans = [pl.ds(j * block, block) for j in range(windows)]
 
-            def one_pair(pair, carry):
+            def one_pair(pair, slot):
                 own = own_ref[pair]
                 factors = kv_factors(kv_ref, pair)
                 for g in range(2):
@@ -835,23 +836,27 @@
                         keys, value_rows = kv_rows_of(factors, wide_ref, g, j)
                         values.append(value_rows)
                         scores = dot(keys, query, ((0,), (0,))) + bias_ref[span, :]
-                        s_ref[g, span, :] = scores
+                        s_ref[slot + g, span, :] = scores
                         top = jnp.maximum(top, jnp.max(scores, axis=0, keepdims=True))
                     total = jnp.zeros((1, block), F32)
                     for span in spans:
-                        weight = jnp.exp(s_ref[g, span, :] - top)
-                        s_ref[g, span, :] = weight
+                        weight = jnp.exp(s_ref[slot + g, span, :] - top)
+                        s_ref[slot + g, span, :] = weight
                         total = total + jnp.sum(weight, axis=0, keepdims=True)
                     lse_ref[pair, g : g + 1, :] = top + jnp.log(total)
                     scale = 1.0 / total
                     mixed = jnp.zeros((HEAD_DIM, block), F32)
                     for j, span in enumerate(spans):
-                        probs = (s_ref[g, span, :] * scale).astype(BF16)
+                        probs = (s_ref[slot + g, span, :] * scale).astype(BF16)
                         mixed = mixed + dot(values[j], probs, ((1,), (0,)))
                     mixed_ref[tp, rows, :] = mixed.astype(BF16)
+
+            def one_member(tp, carry):
+                for k in range(group // 2):
+                    one_pair(tp * (group // 2) + k, 2 * k)
                 return carry
 
-            lax.fori_loop(0, pairs, one_pair, 0)
+            lax.fori_loop(0, n_tp, one_member, 0)
 
         def project_kernel(
             meta_ref, x_ref, mixed_ref, o0_ref, o1_ref, gain_ref, mid_ref, attn_ref, nf_ref
@@ -896,10 +901,13 @@
                         own_ref[:, lanes] = part
             own_load.wait()
 
-        def feed_rows(n_refs, gb_ref, w_ref, ht_ref, back0_ref, back1_ref):
+        def feed_rows(n_refs, gb_ref, w_ref, ht_ref, back0_ref, back1_ref, rows_ref):
             for i in range(2):
-                cut = slice(i * block, (i + 1) * block)
-                rows = n_refs[i][...]
+                rows_ref[i] = n_refs[i][...]
+
+            def one_block(i, carry):
+                cut = pl.ds(pl.multiple_of(i * block, block), block)
+                rows = rows_ref[i]
                 gate = dot(w_ref[0:hidden, :], rows, ((1,), (1,)))
                 up = dot(w_ref[hidden : 2 * hidden, :], rows, ((1,), (1,)))
                 grad_act = dot(w_ref[2 * hidden :, :], gb_ref[cut, :], ((1,), (1,)))
@@ -910,6 +918,9 @@
                     grad_act * up * squash * (1.0 + gate * (1.0 - squash))
                 ).astype(BF16)
                 ht_ref[hidden : 2 * hidden, cut] = (grad_act * soft).astype(BF16)
+                return carry
+
+            lax.fori_loop(0, 2, one_block, 0)
             back = dot(ht_ref[: 2 * hidden, :], w_ref[: 2 * hidden, :], ((0,), (0,)))
             back0_ref[...] = back[:block]
             back1_ref[...] = back[block:].astype(BF16)
@@ -917,7 +928,7 @@
         def far_kernel(meta_ref, n0_ref, n1_ref, gb_ref, *refs):
             own_gu_ref, far_gu_ref, pair_gu_ref, gu_across_ref, gu_rest_ref = refs[:5]
             dn_refs = refs[5 : 5 + n_f]
-            ht_ref, back0_ref, back1_ref, w_ref, sems = refs[5 + n_f :]
+            ht_ref, back0_ref, back1_ref, w_ref, rows_ref, sems = refs[5 + n_f :]
             gate_up = [own_gu_ref, far_gu_ref, pair_gu_ref.at[0], pair_gu_ref.at[1], gu_across_ref]
             gate_up += [gu_rest_ref.at[s] for s in range(n_f - 1)]
             beside_shift = meta_ref[AT_ME + 2]
@@ -943,11 +954,11 @@
                 load.start()
             for load in loads:
                 load.wait()
-            feed_rows((n0_ref, n1_ref), gb_ref, w_ref, ht_ref, back0_ref, back1_ref)
+            feed_rows((n0_ref, n1_ref), gb_ref, w_ref, ht_ref, back0_ref, back1_ref, rows_ref)
 
         def near_kernel(meta_ref, n0_ref, n1_ref, gb_ref, w_ref, far_ht_ref, ht_ref, *refs):
-            back0_ref, back1_ref, *ahead_refs = refs
-            feed_rows((n0_ref, n1_ref), gb_ref, w_ref, ht_ref, back0_ref, back1_ref)
+            back0_ref, back1_ref, *ahead_refs, rows_ref = refs
+            feed_rows((n0_ref, n1_ref), gb_ref, w_ref, ht_ref, back0_ref, back1_ref, rows_ref)
             for k, ref in enumerate((ht_ref, far_ht_ref)):
                 ahead = dot(ref[2 * hidden :, :], w_ref[2 * hidden :, :], ((0,), (0,)))
                 ahead_refs[2 * k][...] = ahead[:block]
@@ -1073,7 +1084,7 @@
                 gwb_ref[...] = refs[1][...]
                 gwa_ref[...] = refs[2][...]
             spans = [pl.ds(j * block, block) for j in range(windows)]
-            first_pair = part * (pairs // 2)
+            first_pair, stop_pair = ((0, first_part), (first_part, pairs))[part]
 
             def one_pair(pair, carry):
                 own = own_ref[pair]
@@ -1122,7 +1133,7 @@
                     gwa_ref[j, pl.ds(start, 2 * KV), :] = jnp.concatenate(grad_kv[j], axis=0)
                 return carry
 
-            lax.fori_loop(first_pair, first_pair + pairs // 2, one_pair, 0)
+            lax.fori_loop(first_pair, stop_pair, one_pair, 0)
             if part == 0:
                 return
 
@@ -1186,7 +1197,10 @@
                 half = group // 2
                 at = [tp * half + k for k in range(half)]
                 own_a = [
-                    (ga0_ref, ga1_ref)[k * 2 // pairs][k % (pairs // 2), : 2 * RANKS, :] for k in at
+                    ga0_ref[k, : 2 * RANKS, :]
+                    if k < first_part
+                    else ga1_ref[k - first_part, : 2 * RANKS, :]
+                    for k in at
                 ]
                 own_a.append(jnp.zeros((a_pad - a_cols, block), F32))
                 own_a = jnp.concatenate(own_a, axis=0)
@@ -1420,7 +1434,7 @@
                 pltpu.VMEM((windows, kv_rows, block), BF16),
                 pltpu.VMEM((window, block), F32),
                 pltpu.VMEM((windows, KV, HEAD_DIM, block), F32),
-                pltpu.VMEM((2, window, block), F32),
+                pltpu.VMEM((group, window, block), F32),
                 *factor_scratch,
             ],
         )
@@ -1451,7 +1465,7 @@
             [whole_ht, *two_sums, ((3 * hidden, width), BF16)],
             (*far_rows, far_cot, *pieces),
             [WHOLE] * 3 + [REMOTE] * len(pieces),
-            [pltpu.SemaphoreType.DMA((2 * n_piece,))],
+            [pltpu.VMEM((2, block, width), BF16), pltpu.SemaphoreType.DMA((2 * n_piece,))],
             room=12,
         )
         across = (far_back + core(far_back1, "dn_far").astype(F32)).astype(BF16)
@@ -1460,6 +1474,8 @@
             "feed_near",
             [whole_ht, *two_sums * 3],
             (after(near_rows[0], across), near_rows[1], near_cot, weights, far_ht),
+            None,
+            [pltpu.VMEM((2, block, width), BF16)],
             room=12,
         )
         across = chip(across, "dn")
@@ -1508,7 +1524,6 @@
             ((windows, KV, HEAD_DIM, block), F32),
             ((windows, heads * KV, block), F32),
         ]
-        grad_a_out = ((pairs // 2, pair_rows, block), F32)
         back_scratch = [
             pltpu.VMEM((windows, kv_rows, block), BF16),
             pltpu.VMEM((window, block), F32),
@@ -1520,7 +1535,7 @@
         grad_a0, *sums_out = call(
             lambda *refs: attention_back_kernel(0, *refs),
             "attention_back_a",
-            [grad_a_out] + sums,
+            [((first_part, pair_rows, block), F32)] + sums,
             back_args,
             None,
             back_scratch,
@@ -1533,7 +1548,7 @@
             lambda *refs: attention_back_kernel(1, *refs),
             "attention_back_b",
             [
-                grad_a_out,
+                ((pairs - first_part, pair_rows, block), F32),
                 sums[0],
                 ((kv_rows, block), BF16),
                 ((kv_rows, block), BF16),

time: 215 us -> 214 us (level)
  transfers between devices with their start and end apart: 55 -> 55, of which waited for: 26 -> 26; matrix products, arithmetic and copies ran while one was open for 3% -> 3% of each run, Pallas kernels for 34% -> 33%
where the time goes in v1:
time: 214 us
  Pallas kernels  79.6 us (37%)
  waiting for transfers between devices  65.5 us (31%)
  starting transfers between devices  56.2 us (26%)
  other arithmetic  6.29 us (3%)
  local copies, waits for them, and re-layouts  4.42 us (2%)
    pallas_call x18, Pallas kernels, call(): pl.pallas_call(kernel, out_shape=[jax.ShapeDtypeStruct(s, d) for s, d in...  79.6 us
    ppermute x41, waiting for transfers between devices, swap(): return lax.ppermute(value, axis, [(i, i ^ bit) for i in range(size)])  54.9 us
    ppermute x41, starting transfers between devices, swap(): return lax.ppermute(value, axis, [(i, i ^ bit) for i in range(size)])  34.7 us
    ppermute x9, starting transfers between devices, shift(): lax.ppermute(value, axes, [(i, (i + step) % size) for i in range(size)])  14.3 us
    ppermute x5, starting transfers between devices, places(): return lax.ppermute(value, ('ctx', 'tp'), pairs)  7.19 us
    ppermute x9, waiting for transfers between devices, shift(): lax.ppermute(value, axes, [(i, (i + step) % size) for i in range(size)])  6.42 us
  transfers between devices with their start and end apart: 55, of which 26 were waited for; matrix products, arithmetic and copies ran while one was open for 3% of the time, Pallas kernels for 33%

profile of v1, /device:TPU:0, one launch (start us, length us, event | category | flops | bytes accessed | tf_op | source)
XLA Modules:
  0.0 213.5 jit_solution(18187211334686515857)
XLA Ops:
  4.5 5.0 %collective-permute-start.6 = (bf16[224,128]{1,0:T(8,128)(2,1)S(1)}, bf16[224,128]{1,0:T(8,128)(2,1)S(1)}, u32[]{:S(2)}, u32[]{:S(2)}) collective-permute-start(bf16[224,128]{1,0:T(8,128)(2,1)S(1)} %pack.1), channel_id=1, source_target_pairs={{0,24},{8,0},{16,8},{24,16},{1,25},{9,1},{17,9},{25,17},{2,26},{10... | collective-permute-start | bytes 172040 | tf_op jit(solution)/shard_map/z_pack/ppermute | solution.py:39
  11.5 2.9 %collective-permute-start.2 = (bf16[256,128]{1,0:T(8,128)(2,1)S(1)}, bf16[256,128]{1,0:T(8,128)(2,1)S(1)}, u32[]{:S(2)}, u32[]{:S(2)}) collective-permute-start(bf16[256,128]{1,0:T(8,128)(2,1)S(1)} %get-tuple-element.250), channel_id=1, source_target_pairs={{0,24},{8,0},{16,8},{24,16},{1,25},{9,1},{17,9},{25,17},{2,26},{10... | collective-permute-start | bytes 196616 | tf_op jit(solution)/shard_map/z_wo/ppermute | solution.py:39
  19.0 3.1 %collective-permute-start.9 = (bf16[1584,128]{1,0:T(8,128)(2,1)S(1)}, bf16[1584,128]{1,0:T(8,128)(2,1)S(1)}, u32[]{:S(2)}, u32[]{:S(2)}) collective-permute-start(bf16[1584,128]{1,0:T(8,128)(2,1)S(1)} %get-tuple-element.132.refs_0_), channel_id=1, source_target_pairs={{0,16},{8,24},{16,0},{24,8},{1,17},{9,25},{17,1},{25,9},{2,18},{10... | collective-permute-start | bytes 1216520 | tf_op jit(solution)/shard_map/z_gate_up/ppermute | solution.py:44
  24.1 3.7 %collective-permute-done.10 = bf16[528,128]{1,0:T(8,128)(2,1)S(1)} collective-permute-done((bf16[528,128]{1,0:T(8,128)(2,1)S(1)}, bf16[528,128]{1,0:T(8,128)(2,1)S(1)}, u32[]{:S(2)}, u32[]{:S(2)}) %collective-permute-start.10) | collective-permute-done | bytes 135200 | tf_op jit(solution)/shard_map/x_down/ppermute | solution.py:44
  30.8 3.2 %rows.1 = (f32[256,1024]{1,0:T(8,128)S(1)}, f32[256,1024]{1,0:T(8,128)S(1)}, bf16[512,1024]{1,0:T(8,128)(2,1)S(1)}, bf16[512,1024]{1,0:T(8,128)(2,1)S(1)}) custom-call(s32[15]{0:T(128)S(1)} %stack.138.meta_ref.refs_0_, f32[1,1024,1024]{2,1,0:T(8,128)} %refs_1_.2, f32[1,1024,1024]{2,1,0:T(8,128)} %refs_1_.3), custom_call_target="tpu_custom_call" | custom-call | tf_op jit(solution)/shard_map/rows/pallas_call | solution.py:664
  34.1 4.5 %collective-permute-done.9.refs_1_ = bf16[1584,128]{1,0:T(8,128)(2,1)S(1)} collective-permute-done((bf16[1584,128]{1,0:T(8,128)(2,1)S(1)}, bf16[1584,128]{1,0:T(8,128)(2,1)S(1)}, u32[]{:S(2)}, u32[]{:S(2)}) %collective-permute-start.9) | collective-permute-done | bytes 405536 | tf_op jit(solution)/shard_map/z_gate_up/ppermute | solution.py:44
  48.1 4.1 %collective-permute-done.15.refs_3_ = bf16[1584,128]{1,0:T(8,128)(2,1)S(1)} collective-permute-done((bf16[1584,128]{1,0:T(8,128)(2,1)S(1)}, bf16[1584,128]{1,0:T(8,128)(2,1)S(1)}, u32[]{:S(2)}, u32[]{:S(2)}) %collective-permute-start.15) | collective-permute-done | bytes 405536 | tf_op jit(solution)/shard_map/x_gate_up/ppermute | solution.py:44
  52.8 6.6 %collective-permute-done.14.refs_2_ = bf16[2,1584,128]{2,1,0:T(8,128)(2,1)S(1)} collective-permute-done((bf16[2,1584,128]{2,1,0:T(8,128)(2,1)S(1)}, bf16[2,1584,128]{2,1,0:T(8,128)(2,1)S(1)}, u32[]{:S(2)}, u32[]{:S(2)}) %collective-permute-start.14) | collective-permute-done | bytes 811040 | tf_op jit(solution)/shard_map/z_gate_up_pair/ppermute | solution.py:44
  63.4 10.7 %attention.1 = (f32[8,2,256]{2,1,0:T(2,128)S(1)}, bf16[4,4,64,256]{3,2,1,0:T(8,128)(2,1)S(1)}, bf16[4,256,256]{2,1,0:T(8,128)(2,1)S(1)}) custom-call(s32[15]{0:T(128)S(1)} %stack.138.meta_ref.refs_0_, s32[1,256]{1,0:T(1,128)S(1)} %bitcast.105, f32[4,48,256]{2,1,0:T(8,128)S(1)} %get-tuple-element.137.a_ref.refs_2_, ...), custom_call_target="tpu_custom_call" | custom-call | tf_op jit(solution)/shard_map/attention/pallas_call | solution.py:664
  79.8 4.4 %collective-permute-done.23.refs_7_ = bf16[2,528,128]{2,1,0:T(8,128)(2,1)S(1)} collective-permute-done((bf16[2,528,128]{2,1,0:T(8,128)(2,1)S(1)}, bf16[2,528,128]{2,1,0:T(8,128)(2,1)S(1)}, u32[]{:S(2)}, u32[]{:S(2)}) %collective-permute-start.23) | collective-permute-done | bytes 270368 | tf_op jit(solution)/shard_map/z_down2/ppermute | solution.py:39
  85.0 5.1 %collective-permute-done.21.refs_4_ = bf16[3,1584,128]{2,1,0:T(8,128)(2,1)S(1)} collective-permute-done((bf16[3,1584,128]{2,1,0:T(8,128)(2,1)S(1)}, bf16[3,1584,128]{2,1,0:T(8,128)(2,1)S(1)}, u32[]{:S(2)}, u32[]{:S(2)}) %collective-permute-start.21) | collective-permute-done | bytes 1216544 | tf_op jit(solution)/shard_map/x_gate_up_rest/ppermute | solution.py:44
  95.2 6.6 %feed_far.1 = (bf16[2112,512]{1,0:T(8,128)(2,1)S(1)}, f32[256,1024]{1,0:T(8,128)S(1)}, bf16[256,1024]{1,0:T(8,128)(2,1)S(1)}, bf16[2112,1024]{1,0:T(8,128)(2,1)S(1)}) custom-call(s32[15]{0:T(128)S(1)} %stack.138.meta_ref.refs_0_, bf16[256,1024]{1,0:T(8,128)(2,1)S(1)} %collective-permute-done.20.n0_ref.refs_4_, ...), custom_call_target="tpu_custom_call" | custom-call | tf_op jit(solution)/shard_map/feed_far/pallas_call | solution.py:664
  105.6 6.9 %feed_near.1 = (bf16[2112,512]{1,0:T(8,128)(2,1)S(1)}, f32[256,1024]{1,0:T(8,128)S(1)}, bf16[256,1024]{1,0:T(8,128)(2,1)S(1)}, f32[256,1024]{1,0:T(8,128)S(1)}, ...) custom-call(s32[15]{0:T(128)S(1)} %stack.138.meta_ref.refs_0_, ...), custom_call_target="tpu_custom_call" | custom-call | tf_op jit(solution)/shard_map/feed_near/pallas_call | solution.py:664
  115.1 3.7 %gate_up_grad.1 = (bf16[1408,512]{1,0:T(8,128)(2,1)S(1)}, bf16[1408,512]{1,0:T(8,128)(2,1)S(1)}) custom-call(s32[15]{0:T(128)S(1)} %stack.138.meta_ref.refs_0_, bf16[2112,512]{1,0:T(8,128)(2,1)S(1)} %get-tuple-element.171.refs_0_, bf16[2112,512]{1,0:T(8,128)(2,1)S(1)} %get-tuple-element.166.far_ht_ref.refs_1_, ...), custom_call_target="tpu_custom_call" | custom-call | tf_op jit(solution)/shard_map/gate_up_grad/pallas_call | solution.py:664
  124.3 11.5 %attention_back_a.1 = (f32[5,24,256]{2,1,0:T(8,128)S(1)}, f32[6,64,256]{2,1,0:T(8,128)S(1)}, f32[4,4,64,256]{3,2,1,0:T(8,128)S(1)}, f32[4,64,256]{2,1,0:T(8,128)S(1)}) custom-call(s32[15]{0:T(128)S(1)} %stack.138.meta_ref.refs_0_, s32[1,256]{1,0:T(1,128)S(1)} %bitcast.106, f32[4,48,256]{2,1,0:T(8,128)S(1)} %get-tuple-element.137.a_ref.refs_2_, ...), custom_call_target="tpu_custom_call" | custom-call | tf_op jit(solution)/shard_map/attention_back_a/pallas_call | solution.py:664
  138.3 7.3 %attention_back_b.1 = (f32[3,24,256]{2,1,0:T(8,128)S(1)}, f32[6,64,256]{2,1,0:T(8,128)S(1)}, bf16[320,256]{1,0:T(8,128)(2,1)S(1)}, bf16[320,256]{1,0:T(8,128)(2,...) custom-call(s32[15]{0:T(128)S(1)} %stack.138.meta_ref.refs_0_, s32[1,256]{1,0:T(1,128)S(1)} %bitcast.107, ...), custom_call_target="tpu_custom_call" | custom-call | tf_op jit(solution)/shard_map/attention_back_b/pallas_call | solution.py:664
  145.7 3.5 %collective-permute-done.33 = bf16[2,256,1024]{2,1,0:T(8,128)(2,1)S(1)} collective-permute-done((bf16[2,256,1024]{2,1,0:T(8,128)(2,1)S(1)}, bf16[2,256,1024]{2,1,0:T(8,128)(2,1)S(1)}, u32[]{:S(2)}, u32[]{:S(2)}) %collective-permute-start.33) | collective-permute-done | bytes 1048608 | tf_op jit(solution)/shard_map/y_out/ppermute | solution.py:44
  150.5 2.9 %collective-permute-done.40.got_ref = bf16[1408,512]{1,0:T(8,128)(2,1)S(1)} collective-permute-done((bf16[1408,512]{1,0:T(8,128)(2,1)S(1)}, bf16[1408,512]{1,0:T(8,128)(2,1)S(1)}, u32[]{:S(2)}, u32[]{:S(2)}) %collective-permute-start.40) | collective-permute-done | bytes 1441824 | tf_op jit(solution)/shard_map/x_grads_a/ppermute | solution.py:44
  160.8 4.2 %collective-permute-done.37.third_ref = bf16[320,256]{1,0:T(8,128)(2,1)S(1)} collective-permute-done((bf16[320,256]{1,0:T(8,128)(2,1)S(1)}, bf16[320,256]{1,0:T(8,128)(2,1)S(1)}, u32[]{:S(2)}, u32[]{:S(2)}) %collective-permute-start.37) | collective-permute-done | bytes 163872 | tf_op jit(solution)/shard_map/x_kv_back_third/ppermute | solution.py:1403
  165.0 3.0 %last.1 = (bf16[256,1024]{1,0:T(8,128)(2,1)S(1)}, bf16[2,4,224,128]{3,2,1,0:T(8,128)(2,1)S(1)}, bf16[2,4,224,128]{3,2,1,0:T(8,128)(2,1)S(1)}, bf16[2,4,224,128]{...) custom-call(s32[15]{0:T(128)S(1)} %stack.138.meta_ref.refs_0_, f32[256,1024]{1,0:T(8,128)S(1)} %get-tuple-element.130.x_ref, ...), custom_call_target="tpu_custom_call" | custom-call | tf_op jit(solution)/shard_map/last/pallas_call | solution.py:664
  178.1 7.4 %add_rows.2 = f32[1,1024,1024]{2,1,0:T(8,128)} custom-call(s32[15]{0:T(128)S(1)} %stack.138.meta_ref.refs_0_, f32[1,1024,1024]{2,1,0:T(8,128)} %refs_1_.2, bf16[256,1024]{1,0:T(8,128)(2,1)S(1)} %get-tuple-element.254.refs_2_, bf16[256,1024]{1,0:T(8,128)(2,1)S(1)} %get-tuple-element.253.refs_3_, bf16[256,1024]{1,0:T(8,128)(2,1)S(1)} %get-tuple-element.252.refs_4_, ...), custom_call_target="tpu_custom_call" | custom-call | tf_op jit(solution)/shard_map/add_rows/pallas_call | solution.py:664
  189.3 4.7 %collective-permute-done.49 = bf16[1408,128]{1,0:T(8,128)(2,1)S(1)} collective-permute-done((bf16[1408,128]{1,0:T(8,128)(2,1)S(1)}, bf16[1408,128]{1,0:T(8,128)(2,1)S(1)}, u32[]{:S(2)}, u32[]{:S(2)}) %collective-permute-start.49) | collective-permute-done | bytes 360480 | tf_op jit(solution)/shard_map/z2_a/ppermute | solution.py:44
  196.7 7.0 %collective-permute-done.52 = bf16[2,480,128]{2,1,0:T(8,128)(2,1)S(1)} collective-permute-done((bf16[2,480,128]{2,1,0:T(8,128)(2,1)S(1)}, bf16[2,480,128]{2,1,0:T(8,128)(2,1)S(1)}, u32[]{:S(2)}, u32[]{:S(2)}) %collective-permute-start.52) | collective-permute-done | bytes 245792 | tf_op jit(solution)/shard_map/z1_gp/ppermute | solution.py:44
  203.9 7.3 %add_rows.3 = f32[1,1024,1024]{2,1,0:T(8,128)} custom-call(s32[15]{0:T(128)S(1)} %stack.138.meta_ref.refs_0_, f32[1,1024,1024]{2,1,0:T(8,128)} %refs_1_.3, bf16[256,1024]{1,0:T(8,128)(2,1)S(1)} %get-tuple-element.238.refs_2_, bf16[256,1024]{1,0:T(8,128)(2,1)S(1)} %collective-permute-done.44.refs_3_, bf16[256,1024]{1,0:T(8,128)(2,1)S(1)} %collective-permute-done.50.refs_4_, ...), custom_call_target="tpu_custom_call" | custom-call | tf_op jit(solution)/shard_map/add_rows/pallas_call | solution.py:664
  (175 shorter events, 82.6 us)
Async XLA Ops:
  4.5 11.7 %collective-permute-start.6 = (bf16[224,128]{1,0:T(8,128)(2,1)S(1)}, bf16[224,128]{1,0:T(8,128)(2,1)S(1)}, u32[]{:S(2)}, u32[]{:S(2)}) collective-permute-start(bf16[224,128]{1,0:T(8,128)(2,1)S(1)} %pack.1), channel_id=1, source_target_pairs={{0,24},{8,0},{16,8},{24,16},{1,25},{9,1},{17,9},{25,17},{2,26},{10... | collective-permute-start | bytes 172040 | tf_op jit(solution)/shard_map/z_pack/ppermute | solution.py:39
  19.0 19.6 %collective-permute-start.9 = (bf16[1584,128]{1,0:T(8,128)(2,1)S(1)}, bf16[1584,128]{1,0:T(8,128)(2,1)S(1)}, u32[]{:S(2)}, u32[]{:S(2)}) collective-permute-start(bf16[1584,128]{1,0:T(8,128)(2,1)S(1)} %get-tuple-element.132.refs_0_), channel_id=1, source_target_pairs={{0,16},{8,24},{16,0},{24,8},{1,17},{9,25},{17,1},{25,9},{2,18},{10... | collective-permute-start | bytes 1216520 | tf_op jit(solution)/shard_map/z_gate_up/ppermute | solution.py:44
  38.8 20.5 %collective-permute-start.14 = (bf16[2,1584,128]{2,1,0:T(8,128)(2,1)S(1)}, bf16[2,1584,128]{2,1,0:T(8,128)(2,1)S(1)}, u32[]{:S(2)}, u32[]{:S(2)}) collective-permute-start(bf16[2,1584,128]{2,1,0:T(8,128)(2,1)S(1)} %pad_maximum_fusion.4), channel_id=1, source_target_pairs={{0,8},{8,0},{16,24},{24,16},{1,9},{9,1},{17,25},{25,17},{2,10},{10... | collective-permute-start | bytes 2433032 | tf_op jit(solution)/shard_map/z_gate_up_pair/ppermute | solution.py:44
  41.7 17.7 %collective-permute-start.18 = (bf16[256,1024]{1,0:T(8,128)(2,1)S(1)}, bf16[256,1024]{1,0:T(8,128)(2,1)S(1)}, u32[]{:S(2)}, u32[]{:S(2)}) collective-permute-start(bf16[256,1024]{1,0:T(8,128)(2,1)S(1)} %slice_dynamic-update-slice_fusion), channel_id=1, source_target_pairs={{0,2},{1,3},{2,0},{3,1},{4,6},{5,7},{6,4},{7,5},{8,10},{9,11},{10,... | collective-permute-start | bytes 1572872 | tf_op jit(solution)/shard_map/y_wo/ppermute | solution.py:44
  45.5 13.8 %collective-permute-start.13 = (bf16[320,256]{1,0:T(8,128)(2,1)S(1)}, bf16[320,256]{1,0:T(8,128)(2,1)S(1)}, u32[]{:S(2)}, u32[]{:S(2)}) collective-permute-start(bf16[320,256]{1,0:T(8,128)(2,1)S(1)} %get-tuple-element.139.w4_ref.refs_8_), channel_id=1, source_target_pairs={{0,2},{1,3},{2,4},{3,5},{4,6},{5,7},{8,10},{9,11},{10,12},{11,13},... | collective-permute-start | bytes 491528 | tf_op jit(solution)/shard_map/x_kv_second/ppermute | solution.py:1403
  60.8 16.0 %collective-permute-start.19 = (bf16[512,1024]{1,0:T(8,128)(2,1)S(1)}, bf16[512,1024]{1,0:T(8,128)(2,1)S(1)}, u32[]{:S(2)}, u32[]{:S(2)}) collective-permute-start(bf16[512,1024]{1,0:T(8,128)(2,1)S(1)} %pad_maximum_fusion.1.o0_ref), channel_id=1, source_target_pairs={{0,1},{1,0},{2,3},{3,2},{4,5},{5,4},{6,7},{7,6},{8,9},{9,8},{10,11... | collective-permute-start | bytes 3145736 | tf_op jit(solution)/shard_map/core_wo/ppermute | solution.py:44
  61.0 29.1 %collective-permute-start.21 = (bf16[3,1584,128]{2,1,0:T(8,128)(2,1)S(1)}, bf16[3,1584,128]{2,1,0:T(8,128)(2,1)S(1)}, u32[]{:S(2)}, u32[]{:S(2)}) collective-permute-start(bf16[3,1584,128]{2,1,0:T(8,128)(2,1)S(1)} %pad_maximum_fusion), channel_id=1, source_target_pairs={{0,4},{4,0},{1,5},{5,1},{2,6},{6,2},{3,7},{7,3},{8,12},{12,8},{9,1... | collective-permute-start | bytes 3649544 | tf_op jit(solution)/shard_map/x_gate_up_rest/ppermute | solution.py:44
  62.6 11.6 %collective-permute-start.22 = (bf16[2,528,128]{2,1,0:T(8,128)(2,1)S(1)}, bf16[2,528,128]{2,1,0:T(8,128)(2,1)S(1)}, u32[]{:S(2)}, u32[]{:S(2)}) collective-permute-start(bf16[2,528,128]{2,1,0:T(8,128)(2,1)S(1)} %pad_maximum_fusion.6.refs_5_), channel_id=1, source_target_pairs={{0,8},{8,16},{16,24},{24,0},{1,9},{9,17},{17,25},{25,1},{2,10},{10... | collective-permute-start | bytes 811016 | tf_op jit(solution)/shard_map/z_down1/ppermute | solution.py:39
  78.2 13.4 %collective-permute-start.20 = (bf16[256,1024]{1,0:T(8,128)(2,1)S(1)}, bf16[256,1024]{1,0:T(8,128)(2,1)S(1)}, u32[]{:S(2)}, u32[]{:S(2)}) collective-permute-start(bf16[256,1024]{1,0:T(8,128)(2,1)S(1)} %get-tuple-element.163.n0_ref.refs_2_), channel_id=1, source_target_pairs={{0,2},{1,3},{2,0},{3,1},{4,6},{5,7},{6,4},{7,5},{8,10},{9,11},{10,... | collective-permute-start | bytes 1572872 | tf_op jit(solution)/shard_map/y_nf/ppermute | solution.py:44
  104.0 14.8 %collective-permute-start.28 = (bf16[256,1024]{1,0:T(8,128)(2,1)S(1)}, bf16[256,1024]{1,0:T(8,128)(2,1)S(1)}, u32[]{:S(2)}, u32[]{:S(2)}) collective-permute-start(bf16[256,1024]{1,0:T(8,128)(2,1)S(1)} %add_convert_fusion.3), channel_id=1, source_target_pairs={{0,2},{1,3},{2,0},{3,1},{4,6},{5,7},{6,4},{7,5},{8,10},{9,11},{10,... | collective-permute-start | bytes 1572872 | tf_op jit(solution)/shard_map/y_dn/ppermute | solution.py:44
  119.4 18.5 %collective-permute-start.32 = (bf16[2,2,704,128]{3,2,1,0:T(8,128)(2,1)S(1)}, bf16[2,2,704,128]{3,2,1,0:T(8,128)(2,1)S(1)}, u32[]{:S(2)}, u32[]{:S(2)}) collective-permute-start(bf16[2,2,704,128]{3,2,1,0:T(8,128)(2,1)S(1)} %get-tuple-element.170), channel_id=1, source_target_pairs={{0,8},{8,0},{16,24},{24,16},{1,9},{9,1},{17,25},{25,17},{2,10},{10... | collective-permute-start | bytes 2162696 | tf_op jit(solution)/shard_map/z1_d/ppermute | solution.py:44
  119.4 33.9 %collective-permute-start.40 = (bf16[1408,512]{1,0:T(8,128)(2,1)S(1)}, bf16[1408,512]{1,0:T(8,128)(2,1)S(1)}, u32[]{:S(2)}, u32[]{:S(2)}) collective-permute-start(bf16[1408,512]{1,0:T(8,128)(2,1)S(1)} %get-tuple-element.172), channel_id=1, source_target_pairs={{0,4},{4,0},{1,5},{5,1},{2,6},{6,2},{3,7},{7,3},{8,12},{12,8},{9,1... | collective-permute-start | bytes 4325384 | tf_op jit(solution)/shard_map/x_grads_a/ppermute | solution.py:44
  122.9 22.7 %collective-permute-start.34 = (bf16[512,1024]{1,0:T(8,128)(2,1)S(1)}, bf16[512,1024]{1,0:T(8,128)(2,1)S(1)}, u32[]{:S(2)}, u32[]{:S(2)}) collective-permute-start(bf16[512,1024]{1,0:T(8,128)(2,1)S(1)} %get-tuple-element.196), channel_id=1, source_target_pairs={{0,1},{1,0},{2,3},{3,2},{4,5},{5,4},{6,7},{7,6},{8,9},{9,8},{10,11... | collective-permute-start | bytes 3145736 | tf_op jit(solution)/shard_map/core_go/ppermute | solution.py:44
  123.7 25.5 %collective-permute-start.33 = (bf16[2,256,1024]{2,1,0:T(8,128)(2,1)S(1)}, bf16[2,256,1024]{2,1,0:T(8,128)(2,1)S(1)}, u32[]{:S(2)}, u32[]{:S(2)}) collective-permute-start(bf16[2,256,1024]{2,1,0:T(8,128)(2,1)S(1)} %pad_maximum_fusion.2), channel_id=1, source_target_pairs={{0,2},{1,3},{2,0},{3,1},{4,6},{5,7},{6,4},{7,5},{8,10},{9,11},{10,... | collective-permute-start | bytes 3145736 | tf_op jit(solution)/shard_map/y_out/ppermute | solution.py:44
  138.1 21.3 %collective-permute-start.38 = (bf16[2,704,128]{2,1,0:T(8,128)(2,1)S(1)}, bf16[2,704,128]{2,1,0:T(8,128)(2,1)S(1)}, u32[]{:S(2)}, u32[]{:S(2)}) collective-permute-start(bf16[2,704,128]{2,1,0:T(8,128)(2,1)S(1)} %fusion.5), channel_id=1, source_target_pairs={{0,16},{8,24},{16,0},{24,8},{1,17},{9,25},{17,1},{25,9},{2,18},{10... | collective-permute-start | bytes 1081352 | tf_op jit(solution)/shard_map/z2_d/ppermute | solution.py:44
  149.2 15.8 %collective-permute-start.35 = (bf16[320,256]{1,0:T(8,128)(2,1)S(1)}, bf16[320,256]{1,0:T(8,128)(2,1)S(1)}, u32[]{:S(2)}, u32[]{:S(2)}) collective-permute-start(bf16[320,256]{1,0:T(8,128)(2,1)S(1)} %get-tuple-element.199), channel_id=1, source_target_pairs={{2,0},{3,1},{4,2},{5,3},{6,4},{7,5},{10,8},{11,9},{12,10},{13,11},... | collective-permute-start | bytes 491528 | tf_op jit(solution)/shard_map/x_kv_back_second/ppermute | solution.py:1403
  154.3 17.8 %collective-permute-start.41 = (bf16[2,1408,128]{2,1,0:T(8,128)(2,1)S(1)}, bf16[2,1408,128]{2,1,0:T(8,128)(2,1)S(1)}, u32[]{:S(2)}, u32[]{:S(2)}) collective-permute-start(bf16[2,1408,128]{2,1,0:T(8,128)(2,1)S(1)} %get-tuple-element.218), channel_id=1, source_target_pairs={{0,8},{8,0},{16,24},{24,16},{1,9},{9,1},{17,25},{25,17},{2,10},{10... | collective-permute-start | bytes 2162696 | tf_op jit(solution)/shard_map/z1_a/ppermute | solution.py:44
  159.4 15.6 %collective-permute-start.45 = (bf16[256,1024]{1,0:T(8,128)(2,1)S(1)}, bf16[256,1024]{1,0:T(8,128)(2,1)S(1)}, u32[]{:S(2)}, u32[]{:S(2)}) collective-permute-start(bf16[256,1024]{1,0:T(8,128)(2,1)S(1)} %slice.198), channel_id=1, source_target_pairs={{0,2},{1,3},{2,0},{3,1},{4,6},{5,7},{6,4},{7,5},{8,10},{9,11},{10,... | collective-permute-start | bytes 1572872 | tf_op jit(solution)/shard_map/y_go/ppermute | solution.py:44
  170.2 15.7 %collective-permute-start.44 = (bf16[256,1024]{1,0:T(8,128)(2,1)S(1)}, bf16[256,1024]{1,0:T(8,128)(2,1)S(1)}, u32[]{:S(2)}, u32[]{:S(2)}) collective-permute-start(bf16[256,1024]{1,0:T(8,128)(2,1)S(1)} %get-tuple-element.238.refs_2_), channel_id=1, source_target_pairs={{0,2},{1,3},{2,0},{3,1},{4,6},{5,7},{6,4},{7,5},{8,10},{9,11},{10,... | collective-permute-start | bytes 1572872 | tf_op jit(solution)/shard_map/y_delta/ppermute | solution.py:44
  172.1 13.8 %collective-permute-start.43 = (bf16[2,4,224,128]{3,2,1,0:T(8,128)(2,1)S(1)}, bf16[2,4,224,128]{3,2,1,0:T(8,128)(2,1)S(1)}, u32[]{:S(2)}, u32[]{:S(2)}) collective-permute-start(bf16[2,4,224,128]{3,2,1,0:T(8,128)(2,1)S(1)} %add_convert_fusion.4), channel_id=1, source_target_pairs={{0,4},{4,0},{1,5},{5,1},{2,6},{6,2},{3,7},{7,3},{8,12},{12,8},{9,1... | collective-permute-start | bytes 1376264 | tf_op jit(solution)/shard_map/x_gp/ppermute | solution.py:44
  175.0 19.1 %collective-permute-start.49 = (bf16[1408,128]{1,0:T(8,128)(2,1)S(1)}, bf16[1408,128]{1,0:T(8,128)(2,1)S(1)}, u32[]{:S(2)}, u32[]{:S(2)}) collective-permute-start(bf16[1408,128]{1,0:T(8,128)(2,1)S(1)} %fusion.6), channel_id=1, source_target_pairs={{0,16},{8,24},{16,0},{24,8},{1,17},{9,25},{17,1},{25,9},{2,18},{10... | collective-permute-start | bytes 1081352 | tf_op jit(solution)/shard_map/z2_a/ppermute | solution.py:44
  175.3 18.7 %collective-permute-start.48 = (bf16[256,512]{1,0:T(8,128)(2,1)S(1)}, bf16[256,512]{1,0:T(8,128)(2,1)S(1)}, u32[]{:S(2)}, u32[]{:S(2)}) collective-permute-start(bf16[256,512]{1,0:T(8,128)(2,1)S(1)} %slice.199), channel_id=1, source_target_pairs={{0,4},{4,0},{1,5},{5,1},{2,6},{6,2},{3,7},{7,3},{8,12},{12,8},{9,1... | collective-permute-start | bytes 786440 | tf_op jit(solution)/shard_map/x_go/ppermute | solution.py:44
  188.6 22.5 %collective-permute-start.54 = (bf16[704,128]{1,0:T(8,128)(2,1)S(1)}, bf16[704,128]{1,0:T(8,128)(2,1)S(1)}, u32[]{:S(2)}, u32[]{:S(2)}) collective-permute-start(bf16[704,128]{1,0:T(8,128)(2,1)S(1)} %slice_bitcast_fusion.8), channel_id=1, source_target_pairs={{0,4},{4,0},{1,5},{5,1},{2,6},{6,2},{3,7},{7,3},{8,12},{12,8},{9,1... | collective-permute-start | bytes 540680 | tf_op jit(solution)/shard_map/x_d/ppermute | solution.py:44
  189.3 14.6 %collective-permute-start.50 = (bf16[256,1024]{1,0:T(8,128)(2,1)S(1)}, bf16[256,1024]{1,0:T(8,128)(2,1)S(1)}, u32[]{:S(2)}, u32[]{:S(2)}) collective-permute-start(bf16[256,1024]{1,0:T(8,128)(2,1)S(1)} %get-tuple-element.238.refs_2_), channel_id=1, source_target_pairs={{0,1},{1,0},{2,3},{3,2},{4,5},{5,4},{6,7},{7,6},{8,9},{9,8},{10,11... | collective-permute-start | bytes 1572872 | tf_op jit(solution)/shard_map/core_delta/ppermute | solution.py:44
  (38 other events, 246.8 us)

commit v2 on v1

--- a/solution.py
+++ b/solution.py
@@ -901,13 +901,16 @@
                         own_ref[:, lanes] = part
             own_load.wait()
 
-        def feed_rows(n_refs, gb_ref, w_ref, ht_ref, back0_ref, back1_ref, rows_ref):
-            for i in range(2):
-                rows_ref[i] = n_refs[i][...]
+        def feed_rows(n_refs, gb_ref, w_ref, ht_ref, back0_ref, back1_ref, rows_ref=None):
+            if rows_ref is not None:
+                for i in range(2):
+                    rows_ref[i] = n_refs[i][...]
 
             def one_block(i, carry):
-                cut = pl.ds(pl.multiple_of(i * block, block), block)
-                rows = rows_ref[i]
+                if rows_ref is None:
+                    cut, rows = pl.ds(i * block, block), n_refs[i][...]
+                else:
+                    cut, rows = pl.ds(pl.multiple_of(i * block, block), block), rows_ref[i]
                 gate = dot(w_ref[0:hidden, :], rows, ((1,), (1,)))
                 up = dot(w_ref[hidden : 2 * hidden, :], rows, ((1,), (1,)))
                 grad_act = dot(w_ref[2 * hidden :, :], gb_ref[cut, :], ((1,), (1,)))
@@ -920,7 +923,11 @@
                 ht_ref[hidden : 2 * hidden, cut] = (grad_act * soft).astype(BF16)
                 return carry
 
-            lax.fori_loop(0, 2, one_block, 0)
+            if rows_ref is None:
+                for i in range(2):
+                    one_block(i, 0)
+            else:
+                lax.fori_loop(0, 2, one_block, 0)
             back = dot(ht_ref[: 2 * hidden, :], w_ref[: 2 * hidden, :], ((0,), (0,)))
             back0_ref[...] = back[:block]
             back1_ref[...] = back[block:].astype(BF16)
@@ -928,7 +935,7 @@
         def far_kernel(meta_ref, n0_ref, n1_ref, gb_ref, *refs):
             own_gu_ref, far_gu_ref, pair_gu_ref, gu_across_ref, gu_rest_ref = refs[:5]
             dn_refs = refs[5 : 5 + n_f]
-            ht_ref, back0_ref, back1_ref, w_ref, rows_ref, sems = refs[5 + n_f :]
+            ht_ref, back0_ref, back1_ref, w_ref, sems = refs[5 + n_f :]
             gate_up = [own_gu_ref, far_gu_ref, pair_gu_ref.at[0], pair_gu_ref.at[1], gu_across_ref]
             gate_up += [gu_rest_ref.at[s] for s in range(n_f - 1)]
             beside_shift = meta_ref[AT_ME + 2]
@@ -954,7 +961,7 @@
                 load.start()
             for load in loads:
                 load.wait()
-            feed_rows((n0_ref, n1_ref), gb_ref, w_ref, ht_ref, back0_ref, back1_ref, rows_ref)
+            feed_rows((n0_ref, n1_ref), gb_ref, w_ref, ht_ref, back0_ref, back1_ref)
 
         def near_kernel(meta_ref, n0_ref, n1_ref, gb_ref, w_ref, far_ht_ref, ht_ref, *refs):
             back0_ref, back1_ref, *ahead_refs, rows_ref = refs
@@ -1465,7 +1472,7 @@
             [whole_ht, *two_sums, ((3 * hidden, width), BF16)],
             (*far_rows, far_cot, *pieces),
             [WHOLE] * 3 + [REMOTE] * len(pieces),
-            [pltpu.VMEM((2, block, width), BF16), pltpu.SemaphoreType.DMA((2 * n_piece,))],
+            [pltpu.SemaphoreType.DMA((2 * n_piece,))],
             room=12,
         )
         across = (far_back + core(far_back1, "dn_far").astype(F32)).astype(BF16)

time: 214 us -> 214 us (level)
  transfers between devices with their start and end apart: 55 -> 55, of which waited for: 26 -> 25; matrix products, arithmetic and copies ran while one was open for 3% -> 3% of each run, Pallas kernels for 33% -> 33%
where the time goes in v2:
time: 214 us; the launch traced here: 213 us
  Pallas kernels  79.4 us (37%)
  waiting for transfers between devices  65.6 us (31%)
  starting transfers between devices  56.1 us (26%)
  other arithmetic  6.27 us (3%)
  local copies, waits for them, and re-layouts  4.42 us (2%)
    pallas_call x18, Pallas kernels, call(): pl.pallas_call(kernel, out_shape=[jax.ShapeDtypeStruct(s, d) for s, d in...  79.4 us
    ppermute x41, waiting for transfers between devices, swap(): return lax.ppermute(value, axis, [(i, i ^ bit) for i in range(size)])  54.9 us
    ppermute x41, starting transfers between devices, swap(): return lax.ppermute(value, axis, [(i, i ^ bit) for i in range(size)])  34.7 us
    ppermute x9, starting transfers between devices, shift(): lax.ppermute(value, axes, [(i, (i + step) % size) for i in range(size)])  14.3 us
    ppermute x5, starting transfers between devices, places(): return lax.ppermute(value, ('ctx', 'tp'), pairs)  7.19 us
    ppermute x9, waiting for transfers between devices, shift(): lax.ppermute(value, axes, [(i, (i + step) % size) for i in range(size)])  6.44 us
  transfers between devices with their start and end apart: 55, of which 25 were waited for; matrix products, arithmetic and copies ran while one was open for 3% of the time, Pallas kernels for 33%

profile of v2, /device:TPU:0, one launch (start us, length us, event | category | flops | bytes accessed | tf_op | source)
XLA Modules:
  0.0 213.2 jit_solution(14283366058101848198)
XLA Ops:
  4.5 5.0 %collective-permute-start.6 = (bf16[224,128]{1,0:T(8,128)(2,1)S(1)}, bf16[224,128]{1,0:T(8,128)(2,1)S(1)}, u32[]{:S(2)}, u32[]{:S(2)}) collective-permute-start(bf16[224,128]{1,0:T(8,128)(2,1)S(1)} %pack.1), channel_id=1, source_target_pairs={{0,24},{8,0},{16,8},{24,16},{1,25},{9,1},{17,9},{25,17},{2,26},{10... | collective-permute-start | bytes 172040 | tf_op jit(solution)/shard_map/z_pack/ppermute | solution.py:39
  11.5 2.9 %collective-permute-start.2 = (bf16[256,128]{1,0:T(8,128)(2,1)S(1)}, bf16[256,128]{1,0:T(8,128)(2,1)S(1)}, u32[]{:S(2)}, u32[]{:S(2)}) collective-permute-start(bf16[256,128]{1,0:T(8,128)(2,1)S(1)} %get-tuple-element.250), channel_id=1, source_target_pairs={{0,24},{8,0},{16,8},{24,16},{1,25},{9,1},{17,9},{25,17},{2,26},{10... | collective-permute-start | bytes 196616 | tf_op jit(solution)/shard_map/z_wo/ppermute | solution.py:39
  19.0 3.1 %collective-permute-start.9 = (bf16[1584,128]{1,0:T(8,128)(2,1)S(1)}, bf16[1584,128]{1,0:T(8,128)(2,1)S(1)}, u32[]{:S(2)}, u32[]{:S(2)}) collective-permute-start(bf16[1584,128]{1,0:T(8,128)(2,1)S(1)} %get-tuple-element.132.refs_0_), channel_id=1, source_target_pairs={{0,16},{8,24},{16,0},{24,8},{1,17},{9,25},{17,1},{25,9},{2,18},{10... | collective-permute-start | bytes 1216520 | tf_op jit(solution)/shard_map/z_gate_up/ppermute | solution.py:44
  24.1 3.7 %collective-permute-done.10 = bf16[528,128]{1,0:T(8,128)(2,1)S(1)} collective-permute-done((bf16[528,128]{1,0:T(8,128)(2,1)S(1)}, bf16[528,128]{1,0:T(8,128)(2,1)S(1)}, u32[]{:S(2)}, u32[]{:S(2)}) %collective-permute-start.10) | collective-permute-done | bytes 135200 | tf_op jit(solution)/shard_map/x_down/ppermute | solution.py:44
  30.8 3.2 %rows.1 = (f32[256,1024]{1,0:T(8,128)S(1)}, f32[256,1024]{1,0:T(8,128)S(1)}, bf16[512,1024]{1,0:T(8,128)(2,1)S(1)}, bf16[512,1024]{1,0:T(8,128)(2,1)S(1)}) custom-call(s32[15]{0:T(128)S(1)} %stack.138.meta_ref.refs_0_, f32[1,1024,1024]{2,1,0:T(8,128)} %refs_1_.2, f32[1,1024,1024]{2,1,0:T(8,128)} %refs_1_.3), custom_call_target="tpu_custom_call" | custom-call | tf_op jit(solution)/shard_map/rows/pallas_call | solution.py:664
  34.1 4.5 %collective-permute-done.9.refs_1_ = bf16[1584,128]{1,0:T(8,128)(2,1)S(1)} collective-permute-done((bf16[1584,128]{1,0:T(8,128)(2,1)S(1)}, bf16[1584,128]{1,0:T(8,128)(2,1)S(1)}, u32[]{:S(2)}, u32[]{:S(2)}) %collective-permute-start.9) | collective-permute-done | bytes 405536 | tf_op jit(solution)/shard_map/z_gate_up/ppermute | solution.py:44
  48.1 4.1 %collective-permute-done.15.refs_3_ = bf16[1584,128]{1,0:T(8,128)(2,1)S(1)} collective-permute-done((bf16[1584,128]{1,0:T(8,128)(2,1)S(1)}, bf16[1584,128]{1,0:T(8,128)(2,1)S(1)}, u32[]{:S(2)}, u32[]{:S(2)}) %collective-permute-start.15) | collective-permute-done | bytes 405536 | tf_op jit(solution)/shard_map/x_gate_up/ppermute | solution.py:44
  52.8 6.6 %collective-permute-done.14.refs_2_ = bf16[2,1584,128]{2,1,0:T(8,128)(2,1)S(1)} collective-permute-done((bf16[2,1584,128]{2,1,0:T(8,128)(2,1)S(1)}, bf16[2,1584,128]{2,1,0:T(8,128)(2,1)S(1)}, u32[]{:S(2)}, u32[]{:S(2)}) %collective-permute-start.14) | collective-permute-done | bytes 811040 | tf_op jit(solution)/shard_map/z_gate_up_pair/ppermute | solution.py:44
  63.4 10.7 %attention.1 = (f32[8,2,256]{2,1,0:T(2,128)S(1)}, bf16[4,4,64,256]{3,2,1,0:T(8,128)(2,1)S(1)}, bf16[4,256,256]{2,1,0:T(8,128)(2,1)S(1)}) custom-call(s32[15]{0:T(128)S(1)} %stack.138.meta_ref.refs_0_, s32[1,256]{1,0:T(1,128)S(1)} %bitcast.105, f32[4,48,256]{2,1,0:T(8,128)S(1)} %get-tuple-element.137.a_ref.refs_2_, ...), custom_call_target="tpu_custom_call" | custom-call | tf_op jit(solution)/shard_map/attention/pallas_call | solution.py:664
  79.8 4.4 %collective-permute-done.23.refs_7_ = bf16[2,528,128]{2,1,0:T(8,128)(2,1)S(1)} collective-permute-done((bf16[2,528,128]{2,1,0:T(8,128)(2,1)S(1)}, bf16[2,528,128]{2,1,0:T(8,128)(2,1)S(1)}, u32[]{:S(2)}, u32[]{:S(2)}) %collective-permute-start.23) | collective-permute-done | bytes 270368 | tf_op jit(solution)/shard_map/z_down2/ppermute | solution.py:39
  85.0 5.1 %collective-permute-done.21.refs_4_ = bf16[3,1584,128]{2,1,0:T(8,128)(2,1)S(1)} collective-permute-done((bf16[3,1584,128]{2,1,0:T(8,128)(2,1)S(1)}, bf16[3,1584,128]{2,1,0:T(8,128)(2,1)S(1)}, u32[]{:S(2)}, u32[]{:S(2)}) %collective-permute-start.21) | collective-permute-done | bytes 1216544 | tf_op jit(solution)/shard_map/x_gate_up_rest/ppermute | solution.py:44
  95.2 6.4 %feed_far.1 = (bf16[2112,512]{1,0:T(8,128)(2,1)S(1)}, f32[256,1024]{1,0:T(8,128)S(1)}, bf16[256,1024]{1,0:T(8,128)(2,1)S(1)}, bf16[2112,1024]{1,0:T(8,128)(2,1)S(1)}) custom-call(s32[15]{0:T(128)S(1)} %stack.138.meta_ref.refs_0_, bf16[256,1024]{1,0:T(8,128)(2,1)S(1)} %collective-permute-done.20.n0_ref.refs_4_, ...), custom_call_target="tpu_custom_call" | custom-call | tf_op jit(solution)/shard_map/feed_far/pallas_call | solution.py:664
  105.3 6.9 %feed_near.1 = (bf16[2112,512]{1,0:T(8,128)(2,1)S(1)}, f32[256,1024]{1,0:T(8,128)S(1)}, bf16[256,1024]{1,0:T(8,128)(2,1)S(1)}, f32[256,1024]{1,0:T(8,128)S(1)}, ...) custom-call(s32[15]{0:T(128)S(1)} %stack.138.meta_ref.refs_0_, ...), custom_call_target="tpu_custom_call" | custom-call | tf_op jit(solution)/shard_map/feed_near/pallas_call | solution.py:664
  114.8 3.7 %gate_up_grad.1 = (bf16[1408,512]{1,0:T(8,128)(2,1)S(1)}, bf16[1408,512]{1,0:T(8,128)(2,1)S(1)}) custom-call(s32[15]{0:T(128)S(1)} %stack.138.meta_ref.refs_0_, bf16[2112,512]{1,0:T(8,128)(2,1)S(1)} %get-tuple-element.171.refs_0_, bf16[2112,512]{1,0:T(8,128)(2,1)S(1)} %get-tuple-element.166.far_ht_ref.refs_1_, ...), custom_call_target="tpu_custom_call" | custom-call | tf_op jit(solution)/shard_map/gate_up_grad/pallas_call | solution.py:664
  124.0 11.5 %attention_back_a.1 = (f32[5,24,256]{2,1,0:T(8,128)S(1)}, f32[6,64,256]{2,1,0:T(8,128)S(1)}, f32[4,4,64,256]{3,2,1,0:T(8,128)S(1)}, f32[4,64,256]{2,1,0:T(8,128)S(1)}) custom-call(s32[15]{0:T(128)S(1)} %stack.138.meta_ref.refs_0_, s32[1,256]{1,0:T(1,128)S(1)} %bitcast.106, f32[4,48,256]{2,1,0:T(8,128)S(1)} %get-tuple-element.137.a_ref.refs_2_, ...), custom_call_target="tpu_custom_call" | custom-call | tf_op jit(solution)/shard_map/attention_back_a/pallas_call | solution.py:664
  138.1 7.3 %attention_back_b.1 = (f32[3,24,256]{2,1,0:T(8,128)S(1)}, f32[6,64,256]{2,1,0:T(8,128)S(1)}, bf16[320,256]{1,0:T(8,128)(2,1)S(1)}, bf16[320,256]{1,0:T(8,128)(2,...) custom-call(s32[15]{0:T(128)S(1)} %stack.138.meta_ref.refs_0_, s32[1,256]{1,0:T(1,128)S(1)} %bitcast.107, ...), custom_call_target="tpu_custom_call" | custom-call | tf_op jit(solution)/shard_map/attention_back_b/pallas_call | solution.py:664
  145.4 3.5 %collective-permute-done.33 = bf16[2,256,1024]{2,1,0:T(8,128)(2,1)S(1)} collective-permute-done((bf16[2,256,1024]{2,1,0:T(8,128)(2,1)S(1)}, bf16[2,256,1024]{2,1,0:T(8,128)(2,1)S(1)}, u32[]{:S(2)}, u32[]{:S(2)}) %collective-permute-start.33) | collective-permute-done | bytes 1048608 | tf_op jit(solution)/shard_map/y_out/ppermute | solution.py:44
  150.2 2.9 %collective-permute-done.40.got_ref = bf16[1408,512]{1,0:T(8,128)(2,1)S(1)} collective-permute-done((bf16[1408,512]{1,0:T(8,128)(2,1)S(1)}, bf16[1408,512]{1,0:T(8,128)(2,1)S(1)}, u32[]{:S(2)}, u32[]{:S(2)}) %collective-permute-start.40) | collective-permute-done | bytes 1441824 | tf_op jit(solution)/shard_map/x_grads_a/ppermute | solution.py:44
  160.5 4.2 %collective-permute-done.37.third_ref = bf16[320,256]{1,0:T(8,128)(2,1)S(1)} collective-permute-done((bf16[320,256]{1,0:T(8,128)(2,1)S(1)}, bf16[320,256]{1,0:T(8,128)(2,1)S(1)}, u32[]{:S(2)}, u32[]{:S(2)}) %collective-permute-start.37) | collective-permute-done | bytes 163872 | tf_op jit(solution)/shard_map/x_kv_back_third/ppermute | solution.py:1410
  164.8 3.0 %last.1 = (bf16[256,1024]{1,0:T(8,128)(2,1)S(1)}, bf16[2,4,224,128]{3,2,1,0:T(8,128)(2,1)S(1)}, bf16[2,4,224,128]{3,2,1,0:T(8,128)(2,1)S(1)}, bf16[2,4,224,128]{...) custom-call(s32[15]{0:T(128)S(1)} %stack.138.meta_ref.refs_0_, f32[256,1024]{1,0:T(8,128)S(1)} %get-tuple-element.130.x_ref, ...), custom_call_target="tpu_custom_call" | custom-call | tf_op jit(solution)/shard_map/last/pallas_call | solution.py:664
  177.8 7.4 %add_rows.2 = f32[1,1024,1024]{2,1,0:T(8,128)} custom-call(s32[15]{0:T(128)S(1)} %stack.138.meta_ref.refs_0_, f32[1,1024,1024]{2,1,0:T(8,128)} %refs_1_.2, bf16[256,1024]{1,0:T(8,128)(2,1)S(1)} %get-tuple-element.254.refs_2_, bf16[256,1024]{1,0:T(8,128)(2,1)S(1)} %get-tuple-element.253.refs_3_, bf16[256,1024]{1,0:T(8,128)(2,1)S(1)} %get-tuple-element.252.refs_4_, ...), custom_call_target="tpu_custom_call" | custom-call | tf_op jit(solution)/shard_map/add_rows/pallas_call | solution.py:664
  189.0 4.8 %collective-permute-done.49 = bf16[1408,128]{1,0:T(8,128)(2,1)S(1)} collective-permute-done((bf16[1408,128]{1,0:T(8,128)(2,1)S(1)}, bf16[1408,128]{1,0:T(8,128)(2,1)S(1)}, u32[]{:S(2)}, u32[]{:S(2)}) %collective-permute-start.49) | collective-permute-done | bytes 360480 | tf_op jit(solution)/shard_map/z2_a/ppermute | solution.py:44
  196.4 7.0 %collective-permute-done.52 = bf16[2,480,128]{2,1,0:T(8,128)(2,1)S(1)} collective-permute-done((bf16[2,480,128]{2,1,0:T(8,128)(2,1)S(1)}, bf16[2,480,128]{2,1,0:T(8,128)(2,1)S(1)}, u32[]{:S(2)}, u32[]{:S(2)}) %collective-permute-start.52) | collective-permute-done | bytes 245792 | tf_op jit(solution)/shard_map/z1_gp/ppermute | solution.py:44
  203.6 7.3 %add_rows.3 = f32[1,1024,1024]{2,1,0:T(8,128)} custom-call(s32[15]{0:T(128)S(1)} %stack.138.meta_ref.refs_0_, f32[1,1024,1024]{2,1,0:T(8,128)} %refs_1_.3, bf16[256,1024]{1,0:T(8,128)(2,1)S(1)} %get-tuple-element.238.refs_2_, bf16[256,1024]{1,0:T(8,128)(2,1)S(1)} %collective-permute-done.44.refs_3_, bf16[256,1024]{1,0:T(8,128)(2,1)S(1)} %collective-permute-done.50.refs_4_, ...), custom_call_target="tpu_custom_call" | custom-call | tf_op jit(solution)/shard_map/add_rows/pallas_call | solution.py:664
  (175 shorter events, 82.5 us)
Async XLA Ops:
  4.5 11.7 %collective-permute-start.6 = (bf16[224,128]{1,0:T(8,128)(2,1)S(1)}, bf16[224,128]{1,0:T(8,128)(2,1)S(1)}, u32[]{:S(2)}, u32[]{:S(2)}) collective-permute-start(bf16[224,128]{1,0:T(8,128)(2,1)S(1)} %pack.1), channel_id=1, source_target_pairs={{0,24},{8,0},{16,8},{24,16},{1,25},{9,1},{17,9},{25,17},{2,26},{10... | collective-permute-start | bytes 172040 | tf_op jit(solution)/shard_map/z_pack/ppermute | solution.py:39
  19.0 19.6 %collective-permute-start.9 = (bf16[1584,128]{1,0:T(8,128)(2,1)S(1)}, bf16[1584,128]{1,0:T(8,128)(2,1)S(1)}, u32[]{:S(2)}, u32[]{:S(2)}) collective-permute-start(bf16[1584,128]{1,0:T(8,128)(2,1)S(1)} %get-tuple-element.132.refs_0_), channel_id=1, source_target_pairs={{0,16},{8,24},{16,0},{24,8},{1,17},{9,25},{17,1},{25,9},{2,18},{10... | collective-permute-start | bytes 1216520 | tf_op jit(solution)/shard_map/z_gate_up/ppermute | solution.py:44
  38.8 20.5 %collective-permute-start.14 = (bf16[2,1584,128]{2,1,0:T(8,128)(2,1)S(1)}, bf16[2,1584,128]{2,1,0:T(8,128)(2,1)S(1)}, u32[]{:S(2)}, u32[]{:S(2)}) collective-permute-start(bf16[2,1584,128]{2,1,0:T(8,128)(2,1)S(1)} %pad_maximum_fusion.4), channel_id=1, source_target_pairs={{0,8},{8,0},{16,24},{24,16},{1,9},{9,1},{17,25},{25,17},{2,10},{10... | collective-permute-start | bytes 2433032 | tf_op jit(solution)/shard_map/z_gate_up_pair/ppermute | solution.py:44
  41.7 17.7 %collective-permute-start.18 = (bf16[256,1024]{1,0:T(8,128)(2,1)S(1)}, bf16[256,1024]{1,0:T(8,128)(2,1)S(1)}, u32[]{:S(2)}, u32[]{:S(2)}) collective-permute-start(bf16[256,1024]{1,0:T(8,128)(2,1)S(1)} %slice_dynamic-update-slice_fusion), channel_id=1, source_target_pairs={{0,2},{1,3},{2,0},{3,1},{4,6},{5,7},{6,4},{7,5},{8,10},{9,11},{10,... | collective-permute-start | bytes 1572872 | tf_op jit(solution)/shard_map/y_wo/ppermute | solution.py:44
  45.5 13.8 %collective-permute-start.13 = (bf16[320,256]{1,0:T(8,128)(2,1)S(1)}, bf16[320,256]{1,0:T(8,128)(2,1)S(1)}, u32[]{:S(2)}, u32[]{:S(2)}) collective-permute-start(bf16[320,256]{1,0:T(8,128)(2,1)S(1)} %get-tuple-element.139.w4_ref.refs_8_), channel_id=1, source_target_pairs={{0,2},{1,3},{2,4},{3,5},{4,6},{5,7},{8,10},{9,11},{10,12},{11,13},... | collective-permute-start | bytes 491528 | tf_op jit(solution)/shard_map/x_kv_second/ppermute | solution.py:1410
  60.8 16.0 %collective-permute-start.19 = (bf16[512,1024]{1,0:T(8,128)(2,1)S(1)}, bf16[512,1024]{1,0:T(8,128)(2,1)S(1)}, u32[]{:S(2)}, u32[]{:S(2)}) collective-permute-start(bf16[512,1024]{1,0:T(8,128)(2,1)S(1)} %pad_maximum_fusion.1.o0_ref), channel_id=1, source_target_pairs={{0,1},{1,0},{2,3},{3,2},{4,5},{5,4},{6,7},{7,6},{8,9},{9,8},{10,11... | collective-permute-start | bytes 3145736 | tf_op jit(solution)/shard_map/core_wo/ppermute | solution.py:44
  61.0 29.1 %collective-permute-start.21 = (bf16[3,1584,128]{2,1,0:T(8,128)(2,1)S(1)}, bf16[3,1584,128]{2,1,0:T(8,128)(2,1)S(1)}, u32[]{:S(2)}, u32[]{:S(2)}) collective-permute-start(bf16[3,1584,128]{2,1,0:T(8,128)(2,1)S(1)} %pad_maximum_fusion), channel_id=1, source_target_pairs={{0,4},{4,0},{1,5},{5,1},{2,6},{6,2},{3,7},{7,3},{8,12},{12,8},{9,1... | collective-permute-start | bytes 3649544 | tf_op jit(solution)/shard_map/x_gate_up_rest/ppermute | solution.py:44
  62.6 11.6 %collective-permute-start.22 = (bf16[2,528,128]{2,1,0:T(8,128)(2,1)S(1)}, bf16[2,528,128]{2,1,0:T(8,128)(2,1)S(1)}, u32[]{:S(2)}, u32[]{:S(2)}) collective-permute-start(bf16[2,528,128]{2,1,0:T(8,128)(2,1)S(1)} %pad_maximum_fusion.6.refs_5_), channel_id=1, source_target_pairs={{0,8},{8,16},{16,24},{24,0},{1,9},{9,17},{17,25},{25,1},{2,10},{10... | collective-permute-start | bytes 811016 | tf_op jit(solution)/shard_map/z_down1/ppermute | solution.py:39
  78.2 13.4 %collective-permute-start.20 = (bf16[256,1024]{1,0:T(8,128)(2,1)S(1)}, bf16[256,1024]{1,0:T(8,128)(2,1)S(1)}, u32[]{:S(2)}, u32[]{:S(2)}) collective-permute-start(bf16[256,1024]{1,0:T(8,128)(2,1)S(1)} %get-tuple-element.163.n0_ref.refs_2_), channel_id=1, source_target_pairs={{0,2},{1,3},{2,0},{3,1},{4,6},{5,7},{6,4},{7,5},{8,10},{9,11},{10,... | collective-permute-start | bytes 1572872 | tf_op jit(solution)/shard_map/y_nf/ppermute | solution.py:44
  103.7 14.8 %collective-permute-start.28 = (bf16[256,1024]{1,0:T(8,128)(2,1)S(1)}, bf16[256,1024]{1,0:T(8,128)(2,1)S(1)}, u32[]{:S(2)}, u32[]{:S(2)}) collective-permute-start(bf16[256,1024]{1,0:T(8,128)(2,1)S(1)} %add_convert_fusion.3), channel_id=1, source_target_pairs={{0,2},{1,3},{2,0},{3,1},{4,6},{5,7},{6,4},{7,5},{8,10},{9,11},{10,... | collective-permute-start | bytes 1572872 | tf_op jit(solution)/shard_map/y_dn/ppermute | solution.py:44
  119.2 18.5 %collective-permute-start.32 = (bf16[2,2,704,128]{3,2,1,0:T(8,128)(2,1)S(1)}, bf16[2,2,704,128]{3,2,1,0:T(8,128)(2,1)S(1)}, u32[]{:S(2)}, u32[]{:S(2)}) collective-permute-start(bf16[2,2,704,128]{3,2,1,0:T(8,128)(2,1)S(1)} %get-tuple-element.170), channel_id=1, source_target_pairs={{0,8},{8,0},{16,24},{24,16},{1,9},{9,1},{17,25},{25,17},{2,10},{10... | collective-permute-start | bytes 2162696 | tf_op jit(solution)/shard_map/z1_d/ppermute | solution.py:44
  119.2 33.9 %collective-permute-start.40 = (bf16[1408,512]{1,0:T(8,128)(2,1)S(1)}, bf16[1408,512]{1,0:T(8,128)(2,1)S(1)}, u32[]{:S(2)}, u32[]{:S(2)}) collective-permute-start(bf16[1408,512]{1,0:T(8,128)(2,1)S(1)} %get-tuple-element.172), channel_id=1, source_target_pairs={{0,4},{4,0},{1,5},{5,1},{2,6},{6,2},{3,7},{7,3},{8,12},{12,8},{9,1... | collective-permute-start | bytes 4325384 | tf_op jit(solution)/shard_map/x_grads_a/ppermute | solution.py:44
  122.7 22.7 %collective-permute-start.34 = (bf16[512,1024]{1,0:T(8,128)(2,1)S(1)}, bf16[512,1024]{1,0:T(8,128)(2,1)S(1)}, u32[]{:S(2)}, u32[]{:S(2)}) collective-permute-start(bf16[512,1024]{1,0:T(8,128)(2,1)S(1)} %get-tuple-element.196), channel_id=1, source_target_pairs={{0,1},{1,0},{2,3},{3,2},{4,5},{5,4},{6,7},{7,6},{8,9},{9,8},{10,11... | collective-permute-start | bytes 3145736 | tf_op jit(solution)/shard_map/core_go/ppermute | solution.py:44
  123.5 25.5 %collective-permute-start.33 = (bf16[2,256,1024]{2,1,0:T(8,128)(2,1)S(1)}, bf16[2,256,1024]{2,1,0:T(8,128)(2,1)S(1)}, u32[]{:S(2)}, u32[]{:S(2)}) collective-permute-start(bf16[2,256,1024]{2,1,0:T(8,128)(2,1)S(1)} %pad_maximum_fusion.2), channel_id=1, source_target_pairs={{0,2},{1,3},{2,0},{3,1},{4,6},{5,7},{6,4},{7,5},{8,10},{9,11},{10,... | collective-permute-start | bytes 3145736 | tf_op jit(solution)/shard_map/y_out/ppermute | solution.py:44
  137.8 21.3 %collective-permute-start.38 = (bf16[2,704,128]{2,1,0:T(8,128)(2,1)S(1)}, bf16[2,704,128]{2,1,0:T(8,128)(2,1)S(1)}, u32[]{:S(2)}, u32[]{:S(2)}) collective-permute-start(bf16[2,704,128]{2,1,0:T(8,128)(2,1)S(1)} %fusion.5), channel_id=1, source_target_pairs={{0,16},{8,24},{16,0},{24,8},{1,17},{9,25},{17,1},{25,9},{2,18},{10... | collective-permute-start | bytes 1081352 | tf_op jit(solution)/shard_map/z2_d/ppermute | solution.py:44
  148.9 15.8 %collective-permute-start.35 = (bf16[320,256]{1,0:T(8,128)(2,1)S(1)}, bf16[320,256]{1,0:T(8,128)(2,1)S(1)}, u32[]{:S(2)}, u32[]{:S(2)}) collective-permute-start(bf16[320,256]{1,0:T(8,128)(2,1)S(1)} %get-tuple-element.199), channel_id=1, source_target_pairs={{2,0},{3,1},{4,2},{5,3},{6,4},{7,5},{10,8},{11,9},{12,10},{13,11},... | collective-permute-start | bytes 491528 | tf_op jit(solution)/shard_map/x_kv_back_second/ppermute | solution.py:1410
  154.0 17.8 %collective-permute-start.41 = (bf16[2,1408,128]{2,1,0:T(8,128)(2,1)S(1)}, bf16[2,1408,128]{2,1,0:T(8,128)(2,1)S(1)}, u32[]{:S(2)}, u32[]{:S(2)}) collective-permute-start(bf16[2,1408,128]{2,1,0:T(8,128)(2,1)S(1)} %get-tuple-element.218), channel_id=1, source_target_pairs={{0,8},{8,0},{16,24},{24,16},{1,9},{9,1},{17,25},{25,17},{2,10},{10... | collective-permute-start | bytes 2162696 | tf_op jit(solution)/shard_map/z1_a/ppermute | solution.py:44
  159.2 15.7 %collective-permute-start.45 = (bf16[256,1024]{1,0:T(8,128)(2,1)S(1)}, bf16[256,1024]{1,0:T(8,128)(2,1)S(1)}, u32[]{:S(2)}, u32[]{:S(2)}) collective-permute-start(bf16[256,1024]{1,0:T(8,128)(2,1)S(1)} %slice.198), channel_id=1, source_target_pairs={{0,2},{1,3},{2,0},{3,1},{4,6},{5,7},{6,4},{7,5},{8,10},{9,11},{10,... | collective-permute-start | bytes 1572872 | tf_op jit(solution)/shard_map/y_go/ppermute | solution.py:44
  169.9 15.8 %collective-permute-start.44 = (bf16[256,1024]{1,0:T(8,128)(2,1)S(1)}, bf16[256,1024]{1,0:T(8,128)(2,1)S(1)}, u32[]{:S(2)}, u32[]{:S(2)}) collective-permute-start(bf16[256,1024]{1,0:T(8,128)(2,1)S(1)} %get-tuple-element.238.refs_2_), channel_id=1, source_target_pairs={{0,2},{1,3},{2,0},{3,1},{4,6},{5,7},{6,4},{7,5},{8,10},{9,11},{10,... | collective-permute-start | bytes 1572872 | tf_op jit(solution)/shard_map/y_delta/ppermute | solution.py:44
  171.9 13.8 %collective-permute-start.43 = (bf16[2,4,224,128]{3,2,1,0:T(8,128)(2,1)S(1)}, bf16[2,4,224,128]{3,2,1,0:T(8,128)(2,1)S(1)}, u32[]{:S(2)}, u32[]{:S(2)}) collective-permute-start(bf16[2,4,224,128]{3,2,1,0:T(8,128)(2,1)S(1)} %add_convert_fusion.4), channel_id=1, source_target_pairs={{0,4},{4,0},{1,5},{5,1},{2,6},{6,2},{3,7},{7,3},{8,12},{12,8},{9,1... | collective-permute-start | bytes 1376264 | tf_op jit(solution)/shard_map/x_gp/ppermute | solution.py:44
  174.7 19.1 %collective-permute-start.49 = (bf16[1408,128]{1,0:T(8,128)(2,1)S(1)}, bf16[1408,128]{1,0:T(8,128)(2,1)S(1)}, u32[]{:S(2)}, u32[]{:S(2)}) collective-permute-start(bf16[1408,128]{1,0:T(8,128)(2,1)S(1)} %fusion.6), channel_id=1, source_target_pairs={{0,16},{8,24},{16,0},{24,8},{1,17},{9,25},{17,1},{25,9},{2,18},{10... | collective-permute-start | bytes 1081352 | tf_op jit(solution)/shard_map/z2_a/ppermute | solution.py:44
  175.1 18.7 %collective-permute-start.48 = (bf16[256,512]{1,0:T(8,128)(2,1)S(1)}, bf16[256,512]{1,0:T(8,128)(2,1)S(1)}, u32[]{:S(2)}, u32[]{:S(2)}) collective-permute-start(bf16[256,512]{1,0:T(8,128)(2,1)S(1)} %slice.199), channel_id=1, source_target_pairs={{0,4},{4,0},{1,5},{5,1},{2,6},{6,2},{3,7},{7,3},{8,12},{12,8},{9,1... | collective-permute-start | bytes 786440 | tf_op jit(solution)/shard_map/x_go/ppermute | solution.py:44
  188.4 22.5 %collective-permute-start.54 = (bf16[704,128]{1,0:T(8,128)(2,1)S(1)}, bf16[704,128]{1,0:T(8,128)(2,1)S(1)}, u32[]{:S(2)}, u32[]{:S(2)}) collective-permute-start(bf16[704,128]{1,0:T(8,128)(2,1)S(1)} %slice_bitcast_fusion.8), channel_id=1, source_target_pairs={{0,4},{4,0},{1,5},{5,1},{2,6},{6,2},{3,7},{7,3},{8,12},{12,8},{9,1... | collective-permute-start | bytes 540680 | tf_op jit(solution)/shard_map/x_d/ppermute | solution.py:44
  189.0 14.6 %collective-permute-start.50 = (bf16[256,1024]{1,0:T(8,128)(2,1)S(1)}, bf16[256,1024]{1,0:T(8,128)(2,1)S(1)}, u32[]{:S(2)}, u32[]{:S(2)}) collective-permute-start(bf16[256,1024]{1,0:T(8,128)(2,1)S(1)} %get-tuple-element.238.refs_2_), channel_id=1, source_target_pairs={{0,1},{1,0},{2,3},{3,2},{4,5},{5,4},{6,7},{7,6},{8,9},{9,8},{10,11... | collective-permute-start | bytes 1572872 | tf_op jit(solution)/shard_map/core_delta/ppermute | solution.py:44
  (38 other events, 246.9 us)

commit v3 on v1

--- a/solution.py
+++ b/solution.py
@@ -1243,8 +1243,8 @@
                         out[hi, s, n_b + a_pad :, :] = pair.astype(BF16)
 
         def add_kernel(arrival, meta_ref, x_ref, d0_ref, d1_ref, d2_ref, d3_ref, out_ref):
-            step = pl.program_id(0) // 2
-            rows = pl.ds(pl.multiple_of((pl.program_id(0) % 2) * (block // 2), 8), block // 2)
+            step = pl.program_id(0)
+            rows = pl.ds(0, block)
             for i, ref in enumerate((d0_ref, d1_ref, d2_ref, d3_ref)):
 
                 @pl.when(step == i)
@@ -1344,7 +1344,7 @@
 
         def add_rows(whole, parts, arrival):
             rows = pl.BlockSpec(
-                (1, block // 2, width), lambda i, m: (0, 2 * m[AT_TP + i // 2] + i % 2, 0)
+                (1, block, width), lambda i, m: (0, m[AT_TP + i], 0)
             )
             (out,) = call(
                 lambda *refs: add_kernel(arrival, *refs),
@@ -1353,7 +1353,7 @@
                 (whole, *parts),
                 [rows] + [WHOLE] * 4,
                 (),
-                (2 * n_tp,),
+                (n_tp,),
                 [rows],
             )
             return out

time: 214 us -> 214 us (level)
  Pallas kernels: 79.6 us -> 75.9 us
  waiting for transfers between devices: 65.5 us -> 69.1 us
    pallas_call x18, Pallas kernels: 79.6 us -> 75.9 us  [call(): pl.pallas_call(kernel, out_shape=[jax.ShapeDtypeStruct(s, d) for s, d in...]
    ppermute x41, waiting for transfers between devices: 54.9 us -> 58.5 us  [swap(): return lax.ppermute(value, axis, [(i, i ^ bit) for i in range(size)])]
  transfers between devices with their start and end apart: 55 -> 55, of which waited for: 26 -> 26; matrix products, arithmetic and copies ran while one was open for 3% -> 3% of each run, Pallas kernels for 33% -> 32%
where the time goes in v3:
time: 214 us
  Pallas kernels  75.9 us (35%)
  waiting for transfers between devices  69.1 us (32%)
  starting transfers between devices  56.4 us (26%)
  other arithmetic  6.29 us (3%)
  local copies, waits for them, and re-layouts  4.42 us (2%)
    pallas_call x18, Pallas kernels, call(): pl.pallas_call(kernel, out_shape=[jax.ShapeDtypeStruct(s, d) for s, d in...  75.9 us
    ppermute x41, waiting for transfers between devices, swap(): return lax.ppermute(value, axis, [(i, i ^ bit) for i in range(size)])  58.5 us
    ppermute x41, starting transfers between devices, swap(): return lax.ppermute(value, axis, [(i, i ^ bit) for i in range(size)])  34.9 us
    ppermute x9, starting transfers between devices, shift(): lax.ppermute(value, axes, [(i, (i + step) % size) for i in range(size)])  14.3 us
    ppermute x5, starting transfers between devices, places(): return lax.ppermute(value, ('ctx', 'tp'), pairs)  7.19 us
    ppermute x9, waiting for transfers between devices, shift(): lax.ppermute(value, axes, [(i, (i + step) % size) for i in range(size)])  6.42 us
  transfers between devices with their start and end apart: 55, of which 26 were waited for; matrix products, arithmetic and copies ran while one was open for 3% of the time, Pallas kernels for 32%

profile of v3, /device:TPU:0, one launch (start us, length us, event | category | flops | bytes accessed | tf_op | source)
XLA Modules:
  0.0 213.5 jit_solution(9622584946488537289)
XLA Ops:
  4.5 5.0 %collective-permute-start.6 = (bf16[224,128]{1,0:T(8,128)(2,1)S(1)}, bf16[224,128]{1,0:T(8,128)(2,1)S(1)}, u32[]{:S(2)}, u32[]{:S(2)}) collective-permute-start(bf16[224,128]{1,0:T(8,128)(2,1)S(1)} %pack.1), channel_id=1, source_target_pairs={{0,24},{8,0},{16,8},{24,16},{1,25},{9,1},{17,9},{25,17},{2,26},{10... | collective-permute-start | bytes 172040 | tf_op jit(solution)/shard_map/z_pack/ppermute | solution.py:39
  11.5 2.9 %collective-permute-start.2 = (bf16[256,128]{1,0:T(8,128)(2,1)S(1)}, bf16[256,128]{1,0:T(8,128)(2,1)S(1)}, u32[]{:S(2)}, u32[]{:S(2)}) collective-permute-start(bf16[256,128]{1,0:T(8,128)(2,1)S(1)} %get-tuple-element.250), channel_id=1, source_target_pairs={{0,24},{8,0},{16,8},{24,16},{1,25},{9,1},{17,9},{25,17},{2,26},{10... | collective-permute-start | bytes 196616 | tf_op jit(solution)/shard_map/z_wo/ppermute | solution.py:39
  19.0 3.1 %collective-permute-start.9 = (bf16[1584,128]{1,0:T(8,128)(2,1)S(1)}, bf16[1584,128]{1,0:T(8,128)(2,1)S(1)}, u32[]{:S(2)}, u32[]{:S(2)}) collective-permute-start(bf16[1584,128]{1,0:T(8,128)(2,1)S(1)} %get-tuple-element.132.refs_0_), channel_id=1, source_target_pairs={{0,16},{8,24},{16,0},{24,8},{1,17},{9,25},{17,1},{25,9},{2,18},{10... | collective-permute-start | bytes 1216520 | tf_op jit(solution)/shard_map/z_gate_up/ppermute | solution.py:44
  24.1 3.7 %collective-permute-done.10 = bf16[528,128]{1,0:T(8,128)(2,1)S(1)} collective-permute-done((bf16[528,128]{1,0:T(8,128)(2,1)S(1)}, bf16[528,128]{1,0:T(8,128)(2,1)S(1)}, u32[]{:S(2)}, u32[]{:S(2)}) %collective-permute-start.10) | collective-permute-done | bytes 135200 | tf_op jit(solution)/shard_map/x_down/ppermute | solution.py:44
  30.8 3.2 %rows.1 = (f32[256,1024]{1,0:T(8,128)S(1)}, f32[256,1024]{1,0:T(8,128)S(1)}, bf16[512,1024]{1,0:T(8,128)(2,1)S(1)}, bf16[512,1024]{1,0:T(8,128)(2,1)S(1)}) custom-call(s32[15]{0:T(128)S(1)} %stack.138.meta_ref.refs_0_, f32[1,1024,1024]{2,1,0:T(8,128)} %refs_1_.2, f32[1,1024,1024]{2,1,0:T(8,128)} %refs_1_.3), custom_call_target="tpu_custom_call" | custom-call | tf_op jit(solution)/shard_map/rows/pallas_call | solution.py:664
  34.1 4.5 %collective-permute-done.9.refs_1_ = bf16[1584,128]{1,0:T(8,128)(2,1)S(1)} collective-permute-done((bf16[1584,128]{1,0:T(8,128)(2,1)S(1)}, bf16[1584,128]{1,0:T(8,128)(2,1)S(1)}, u32[]{:S(2)}, u32[]{:S(2)}) %collective-permute-start.9) | collective-permute-done | bytes 405536 | tf_op jit(solution)/shard_map/z_gate_up/ppermute | solution.py:44
  48.1 4.1 %collective-permute-done.15.refs_3_ = bf16[1584,128]{1,0:T(8,128)(2,1)S(1)} collective-permute-done((bf16[1584,128]{1,0:T(8,128)(2,1)S(1)}, bf16[1584,128]{1,0:T(8,128)(2,1)S(1)}, u32[]{:S(2)}, u32[]{:S(2)}) %collective-permute-start.15) | collective-permute-done | bytes 405536 | tf_op jit(solution)/shard_map/x_gate_up/ppermute | solution.py:44
  52.8 6.6 %collective-permute-done.14.refs_2_ = bf16[2,1584,128]{2,1,0:T(8,128)(2,1)S(1)} collective-permute-done((bf16[2,1584,128]{2,1,0:T(8,128)(2,1)S(1)}, bf16[2,1584,128]{2,1,0:T(8,128)(2,1)S(1)}, u32[]{:S(2)}, u32[]{:S(2)}) %collective-permute-start.14) | collective-permute-done | bytes 811040 | tf_op jit(solution)/shard_map/z_gate_up_pair/ppermute | solution.py:44
  63.4 10.7 %attention.1 = (f32[8,2,256]{2,1,0:T(2,128)S(1)}, bf16[4,4,64,256]{3,2,1,0:T(8,128)(2,1)S(1)}, bf16[4,256,256]{2,1,0:T(8,128)(2,1)S(1)}) custom-call(s32[15]{0:T(128)S(1)} %stack.138.meta_ref.refs_0_, s32[1,256]{1,0:T(1,128)S(1)} %bitcast.105, f32[4,48,256]{2,1,0:T(8,128)S(1)} %get-tuple-element.137.a_ref.refs_2_, ...), custom_call_target="tpu_custom_call" | custom-call | tf_op jit(solution)/shard_map/attention/pallas_call | solution.py:664
  79.8 4.4 %collective-permute-done.23.refs_7_ = bf16[2,528,128]{2,1,0:T(8,128)(2,1)S(1)} collective-permute-done((bf16[2,528,128]{2,1,0:T(8,128)(2,1)S(1)}, bf16[2,528,128]{2,1,0:T(8,128)(2,1)S(1)}, u32[]{:S(2)}, u32[]{:S(2)}) %collective-permute-start.23) | collective-permute-done | bytes 270368 | tf_op jit(solution)/shard_map/z_down2/ppermute | solution.py:39
  85.0 5.1 %collective-permute-done.21.refs_4_ = bf16[3,1584,128]{2,1,0:T(8,128)(2,1)S(1)} collective-permute-done((bf16[3,1584,128]{2,1,0:T(8,128)(2,1)S(1)}, bf16[3,1584,128]{2,1,0:T(8,128)(2,1)S(1)}, u32[]{:S(2)}, u32[]{:S(2)}) %collective-permute-start.21) | collective-permute-done | bytes 1216544 | tf_op jit(solution)/shard_map/x_gate_up_rest/ppermute | solution.py:44
  95.2 6.6 %feed_far.1 = (bf16[2112,512]{1,0:T(8,128)(2,1)S(1)}, f32[256,1024]{1,0:T(8,128)S(1)}, bf16[256,1024]{1,0:T(8,128)(2,1)S(1)}, bf16[2112,1024]{1,0:T(8,128)(2,1)S(1)}) custom-call(s32[15]{0:T(128)S(1)} %stack.138.meta_ref.refs_0_, bf16[256,1024]{1,0:T(8,128)(2,1)S(1)} %collective-permute-done.20.n0_ref.refs_4_, ...), custom_call_target="tpu_custom_call" | custom-call | tf_op jit(solution)/shard_map/feed_far/pallas_call | solution.py:664
  105.6 6.9 %feed_near.1 = (bf16[2112,512]{1,0:T(8,128)(2,1)S(1)}, f32[256,1024]{1,0:T(8,128)S(1)}, bf16[256,1024]{1,0:T(8,128)(2,1)S(1)}, f32[256,1024]{1,0:T(8,128)S(1)}, ...) custom-call(s32[15]{0:T(128)S(1)} %stack.138.meta_ref.refs_0_, ...), custom_call_target="tpu_custom_call" | custom-call | tf_op jit(solution)/shard_map/feed_near/pallas_call | solution.py:664
  115.1 3.7 %gate_up_grad.1 = (bf16[1408,512]{1,0:T(8,128)(2,1)S(1)}, bf16[1408,512]{1,0:T(8,128)(2,1)S(1)}) custom-call(s32[15]{0:T(128)S(1)} %stack.138.meta_ref.refs_0_, bf16[2112,512]{1,0:T(8,128)(2,1)S(1)} %get-tuple-element.171.refs_0_, bf16[2112,512]{1,0:T(8,128)(2,1)S(1)} %get-tuple-element.166.far_ht_ref.refs_1_, ...), custom_call_target="tpu_custom_call" | custom-call | tf_op jit(solution)/shard_map/gate_up_grad/pallas_call | solution.py:664
  124.3 11.5 %attention_back_a.1 = (f32[5,24,256]{2,1,0:T(8,128)S(1)}, f32[6,64,256]{2,1,0:T(8,128)S(1)}, f32[4,4,64,256]{3,2,1,0:T(8,128)S(1)}, f32[4,64,256]{2,1,0:T(8,128)S(1)}) custom-call(s32[15]{0:T(128)S(1)} %stack.138.meta_ref.refs_0_, s32[1,256]{1,0:T(1,128)S(1)} %bitcast.106, f32[4,48,256]{2,1,0:T(8,128)S(1)} %get-tuple-element.137.a_ref.refs_2_, ...), custom_call_target="tpu_custom_call" | custom-call | tf_op jit(solution)/shard_map/attention_back_a/pallas_call | solution.py:664
  138.3 7.3 %attention_back_b.1 = (f32[3,24,256]{2,1,0:T(8,128)S(1)}, f32[6,64,256]{2,1,0:T(8,128)S(1)}, bf16[320,256]{1,0:T(8,128)(2,1)S(1)}, bf16[320,256]{1,0:T(8,128)(2,...) custom-call(s32[15]{0:T(128)S(1)} %stack.138.meta_ref.refs_0_, s32[1,256]{1,0:T(1,128)S(1)} %bitcast.107, ...), custom_call_target="tpu_custom_call" | custom-call | tf_op jit(solution)/shard_map/attention_back_b/pallas_call | solution.py:664
  145.7 3.5 %collective-permute-done.33 = bf16[2,256,1024]{2,1,0:T(8,128)(2,1)S(1)} collective-permute-done((bf16[2,256,1024]{2,1,0:T(8,128)(2,1)S(1)}, bf16[2,256,1024]{2,1,0:T(8,128)(2,1)S(1)}, u32[]{:S(2)}, u32[]{:S(2)}) %collective-permute-start.33) | collective-permute-done | bytes 1048608 | tf_op jit(solution)/shard_map/y_out/ppermute | solution.py:44
  150.5 2.9 %collective-permute-done.40.got_ref = bf16[1408,512]{1,0:T(8,128)(2,1)S(1)} collective-permute-done((bf16[1408,512]{1,0:T(8,128)(2,1)S(1)}, bf16[1408,512]{1,0:T(8,128)(2,1)S(1)}, u32[]{:S(2)}, u32[]{:S(2)}) %collective-permute-start.40) | collective-permute-done | bytes 1441824 | tf_op jit(solution)/shard_map/x_grads_a/ppermute | solution.py:44
  160.8 4.2 %collective-permute-done.37.third_ref = bf16[320,256]{1,0:T(8,128)(2,1)S(1)} collective-permute-done((bf16[320,256]{1,0:T(8,128)(2,1)S(1)}, bf16[320,256]{1,0:T(8,128)(2,1)S(1)}, u32[]{:S(2)}, u32[]{:S(2)}) %collective-permute-start.37) | collective-permute-done | bytes 163872 | tf_op jit(solution)/shard_map/x_kv_back_third/ppermute | solution.py:1403
  165.0 3.0 %last.1 = (bf16[256,1024]{1,0:T(8,128)(2,1)S(1)}, bf16[2,4,224,128]{3,2,1,0:T(8,128)(2,1)S(1)}, bf16[2,4,224,128]{3,2,1,0:T(8,128)(2,1)S(1)}, bf16[2,4,224,128]{...) custom-call(s32[15]{0:T(128)S(1)} %stack.138.meta_ref.refs_0_, f32[256,1024]{1,0:T(8,128)S(1)} %get-tuple-element.130.x_ref, ...), custom_call_target="tpu_custom_call" | custom-call | tf_op jit(solution)/shard_map/last/pallas_call | solution.py:664
  178.1 5.6 %add_rows.2 = f32[1,1024,1024]{2,1,0:T(8,128)} custom-call(s32[15]{0:T(128)S(1)} %stack.138.meta_ref.refs_0_, f32[1,1024,1024]{2,1,0:T(8,128)} %refs_1_.2, bf16[256,1024]{1,0:T(8,128)(2,1)S(1)} %get-tuple-element.254.refs_2_, bf16[256,1024]{1,0:T(8,128)(2,1)S(1)} %get-tuple-element.253.refs_3_, bf16[256,1024]{1,0:T(8,128)(2,1)S(1)} %get-tuple-element.252.refs_4_, ...), custom_call_target="tpu_custom_call" | custom-call | tf_op jit(solution)/shard_map/add_rows/pallas_call | solution.py:664
  189.3 4.7 %collective-permute-done.49 = bf16[1408,128]{1,0:T(8,128)(2,1)S(1)} collective-permute-done((bf16[1408,128]{1,0:T(8,128)(2,1)S(1)}, bf16[1408,128]{1,0:T(8,128)(2,1)S(1)}, u32[]{:S(2)}, u32[]{:S(2)}) %collective-permute-start.49) | collective-permute-done | bytes 360480 | tf_op jit(solution)/shard_map/z2_a/ppermute | solution.py:44
  196.7 7.0 %collective-permute-done.52 = bf16[2,480,128]{2,1,0:T(8,128)(2,1)S(1)} collective-permute-done((bf16[2,480,128]{2,1,0:T(8,128)(2,1)S(1)}, bf16[2,480,128]{2,1,0:T(8,128)(2,1)S(1)}, u32[]{:S(2)}, u32[]{:S(2)}) %collective-permute-start.52) | collective-permute-done | bytes 245792 | tf_op jit(solution)/shard_map/z1_gp/ppermute | solution.py:44
  204.0 5.3 %add_rows.3 = f32[1,1024,1024]{2,1,0:T(8,128)} custom-call(s32[15]{0:T(128)S(1)} %stack.138.meta_ref.refs_0_, f32[1,1024,1024]{2,1,0:T(8,128)} %refs_1_.3, bf16[256,1024]{1,0:T(8,128)(2,1)S(1)} %get-tuple-element.238.refs_2_, bf16[256,1024]{1,0:T(8,128)(2,1)S(1)} %collective-permute-done.44.refs_3_, bf16[256,1024]{1,0:T(8,128)(2,1)S(1)} %collective-permute-done.50.refs_4_, ...), custom_call_target="tpu_custom_call" | custom-call | tf_op jit(solution)/shard_map/add_rows/pallas_call | solution.py:664
  (175 shorter events, 86.3 us)
Async XLA Ops:
  4.5 11.7 %collective-permute-start.6 = (bf16[224,128]{1,0:T(8,128)(2,1)S(1)}, bf16[224,128]{1,0:T(8,128)(2,1)S(1)}, u32[]{:S(2)}, u32[]{:S(2)}) collective-permute-start(bf16[224,128]{1,0:T(8,128)(2,1)S(1)} %pack.1), channel_id=1, source_target_pairs={{0,24},{8,0},{16,8},{24,16},{1,25},{9,1},{17,9},{25,17},{2,26},{10... | collective-permute-start | bytes 172040 | tf_op jit(solution)/shard_map/z_pack/ppermute | solution.py:39
  19.0 19.6 %collective-permute-start.9 = (bf16[1584,128]{1,0:T(8,128)(2,1)S(1)}, bf16[1584,128]{1,0:T(8,128)(2,1)S(1)}, u32[]{:S(2)}, u32[]{:S(2)}) collective-permute-start(bf16[1584,128]{1,0:T(8,128)(2,1)S(1)} %get-tuple-element.132.refs_0_), channel_id=1, source_target_pairs={{0,16},{8,24},{16,0},{24,8},{1,17},{9,25},{17,1},{25,9},{2,18},{10... | collective-permute-start | bytes 1216520 | tf_op jit(solution)/shard_map/z_gate_up/ppermute | solution.py:44
  38.8 20.5 %collective-permute-start.14 = (bf16[2,1584,128]{2,1,0:T(8,128)(2,1)S(1)}, bf16[2,1584,128]{2,1,0:T(8,128)(2,1)S(1)}, u32[]{:S(2)}, u32[]{:S(2)}) collective-permute-start(bf16[2,1584,128]{2,1,0:T(8,128)(2,1)S(1)} %pad_maximum_fusion.4), channel_id=1, source_target_pairs={{0,8},{8,0},{16,24},{24,16},{1,9},{9,1},{17,25},{25,17},{2,10},{10... | collective-permute-start | bytes 2433032 | tf_op jit(solution)/shard_map/z_gate_up_pair/ppermute | solution.py:44
  40.6 11.6 %collective-permute-start.15 = (bf16[1584,128]{1,0:T(8,128)(2,1)S(1)}, bf16[1584,128]{1,0:T(8,128)(2,1)S(1)}, u32[]{:S(2)}, u32[]{:S(2)}) collective-permute-start(bf16[1584,128]{1,0:T(8,128)(2,1)S(1)} %get-tuple-element.132.refs_0_), channel_id=1, source_target_pairs={{0,4},{4,0},{1,5},{5,1},{2,6},{6,2},{3,7},{7,3},{8,12},{12,8},{9,1... | collective-permute-start | bytes 1216520 | tf_op jit(solution)/shard_map/x_gate_up/ppermute | solution.py:44
  41.7 17.7 %collective-permute-start.18 = (bf16[256,1024]{1,0:T(8,128)(2,1)S(1)}, bf16[256,1024]{1,0:T(8,128)(2,1)S(1)}, u32[]{:S(2)}, u32[]{:S(2)}) collective-permute-start(bf16[256,1024]{1,0:T(8,128)(2,1)S(1)} %slice_dynamic-update-slice_fusion), channel_id=1, source_target_pairs={{0,2},{1,3},{2,0},{3,1},{4,6},{5,7},{6,4},{7,5},{8,10},{9,11},{10,... | collective-permute-start | bytes 1572872 | tf_op jit(solution)/shard_map/y_wo/ppermute | solution.py:44
  45.5 13.8 %collective-permute-start.13 = (bf16[320,256]{1,0:T(8,128)(2,1)S(1)}, bf16[320,256]{1,0:T(8,128)(2,1)S(1)}, u32[]{:S(2)}, u32[]{:S(2)}) collective-permute-start(bf16[320,256]{1,0:T(8,128)(2,1)S(1)} %get-tuple-element.139.w4_ref.refs_8_), channel_id=1, source_target_pairs={{0,2},{1,3},{2,4},{3,5},{4,6},{5,7},{8,10},{9,11},{10,12},{11,13},... | collective-permute-start | bytes 491528 | tf_op jit(solution)/shard_map/x_kv_second/ppermute | solution.py:1403
  60.8 16.0 %collective-permute-start.19 = (bf16[512,1024]{1,0:T(8,128)(2,1)S(1)}, bf16[512,1024]{1,0:T(8,128)(2,1)S(1)}, u32[]{:S(2)}, u32[]{:S(2)}) collective-permute-start(bf16[512,1024]{1,0:T(8,128)(2,1)S(1)} %pad_maximum_fusion.1.o0_ref), channel_id=1, source_target_pairs={{0,1},{1,0},{2,3},{3,2},{4,5},{5,4},{6,7},{7,6},{8,9},{9,8},{10,11... | collective-permute-start | bytes 3145736 | tf_op jit(solution)/shard_map/core_wo/ppermute | solution.py:44
  61.0 29.1 %collective-permute-start.21 = (bf16[3,1584,128]{2,1,0:T(8,128)(2,1)S(1)}, bf16[3,1584,128]{2,1,0:T(8,128)(2,1)S(1)}, u32[]{:S(2)}, u32[]{:S(2)}) collective-permute-start(bf16[3,1584,128]{2,1,0:T(8,128)(2,1)S(1)} %pad_maximum_fusion), channel_id=1, source_target_pairs={{0,4},{4,0},{1,5},{5,1},{2,6},{6,2},{3,7},{7,3},{8,12},{12,8},{9,1... | collective-permute-start | bytes 3649544 | tf_op jit(solution)/shard_map/x_gate_up_rest/ppermute | solution.py:44
  78.2 13.4 %collective-permute-start.20 = (bf16[256,1024]{1,0:T(8,128)(2,1)S(1)}, bf16[256,1024]{1,0:T(8,128)(2,1)S(1)}, u32[]{:S(2)}, u32[]{:S(2)}) collective-permute-start(bf16[256,1024]{1,0:T(8,128)(2,1)S(1)} %get-tuple-element.163.n0_ref.refs_2_), channel_id=1, source_target_pairs={{0,2},{1,3},{2,0},{3,1},{4,6},{5,7},{6,4},{7,5},{8,10},{9,11},{10,... | collective-permute-start | bytes 1572872 | tf_op jit(solution)/shard_map/y_nf/ppermute | solution.py:44
  104.0 14.8 %collective-permute-start.28 = (bf16[256,1024]{1,0:T(8,128)(2,1)S(1)}, bf16[256,1024]{1,0:T(8,128)(2,1)S(1)}, u32[]{:S(2)}, u32[]{:S(2)}) collective-permute-start(bf16[256,1024]{1,0:T(8,128)(2,1)S(1)} %add_convert_fusion.3), channel_id=1, source_target_pairs={{0,2},{1,3},{2,0},{3,1},{4,6},{5,7},{6,4},{7,5},{8,10},{9,11},{10,... | collective-permute-start | bytes 1572872 | tf_op jit(solution)/shard_map/y_dn/ppermute | solution.py:44
  119.4 18.5 %collective-permute-start.32 = (bf16[2,2,704,128]{3,2,1,0:T(8,128)(2,1)S(1)}, bf16[2,2,704,128]{3,2,1,0:T(8,128)(2,1)S(1)}, u32[]{:S(2)}, u32[]{:S(2)}) collective-permute-start(bf16[2,2,704,128]{3,2,1,0:T(8,128)(2,1)S(1)} %get-tuple-element.170), channel_id=1, source_target_pairs={{0,8},{8,0},{16,24},{24,16},{1,9},{9,1},{17,25},{25,17},{2,10},{10... | collective-permute-start | bytes 2162696 | tf_op jit(solution)/shard_map/z1_d/ppermute | solution.py:44
  119.4 33.9 %collective-permute-start.40 = (bf16[1408,512]{1,0:T(8,128)(2,1)S(1)}, bf16[1408,512]{1,0:T(8,128)(2,1)S(1)}, u32[]{:S(2)}, u32[]{:S(2)}) collective-permute-start(bf16[1408,512]{1,0:T(8,128)(2,1)S(1)} %get-tuple-element.172), channel_id=1, source_target_pairs={{0,4},{4,0},{1,5},{5,1},{2,6},{6,2},{3,7},{7,3},{8,12},{12,8},{9,1... | collective-permute-start | bytes 4325384 | tf_op jit(solution)/shard_map/x_grads_a/ppermute | solution.py:44
  122.9 22.7 %collective-permute-start.34 = (bf16[512,1024]{1,0:T(8,128)(2,1)S(1)}, bf16[512,1024]{1,0:T(8,128)(2,1)S(1)}, u32[]{:S(2)}, u32[]{:S(2)}) collective-permute-start(bf16[512,1024]{1,0:T(8,128)(2,1)S(1)} %get-tuple-element.196), channel_id=1, source_target_pairs={{0,1},{1,0},{2,3},{3,2},{4,5},{5,4},{6,7},{7,6},{8,9},{9,8},{10,11... | collective-permute-start | bytes 3145736 | tf_op jit(solution)/shard_map/core_go/ppermute | solution.py:44
  123.7 25.5 %collective-permute-start.33 = (bf16[2,256,1024]{2,1,0:T(8,128)(2,1)S(1)}, bf16[2,256,1024]{2,1,0:T(8,128)(2,1)S(1)}, u32[]{:S(2)}, u32[]{:S(2)}) collective-permute-start(bf16[2,256,1024]{2,1,0:T(8,128)(2,1)S(1)} %pad_maximum_fusion.2), channel_id=1, source_target_pairs={{0,2},{1,3},{2,0},{3,1},{4,6},{5,7},{6,4},{7,5},{8,10},{9,11},{10,... | collective-permute-start | bytes 3145736 | tf_op jit(solution)/shard_map/y_out/ppermute | solution.py:44
  138.1 21.3 %collective-permute-start.38 = (bf16[2,704,128]{2,1,0:T(8,128)(2,1)S(1)}, bf16[2,704,128]{2,1,0:T(8,128)(2,1)S(1)}, u32[]{:S(2)}, u32[]{:S(2)}) collective-permute-start(bf16[2,704,128]{2,1,0:T(8,128)(2,1)S(1)} %fusion.5), channel_id=1, source_target_pairs={{0,16},{8,24},{16,0},{24,8},{1,17},{9,25},{17,1},{25,9},{2,18},{10... | collective-permute-start | bytes 1081352 | tf_op jit(solution)/shard_map/z2_d/ppermute | solution.py:44
  149.2 15.8 %collective-permute-start.35 = (bf16[320,256]{1,0:T(8,128)(2,1)S(1)}, bf16[320,256]{1,0:T(8,128)(2,1)S(1)}, u32[]{:S(2)}, u32[]{:S(2)}) collective-permute-start(bf16[320,256]{1,0:T(8,128)(2,1)S(1)} %get-tuple-element.199), channel_id=1, source_target_pairs={{2,0},{3,1},{4,2},{5,3},{6,4},{7,5},{10,8},{11,9},{12,10},{13,11},... | collective-permute-start | bytes 491528 | tf_op jit(solution)/shard_map/x_kv_back_second/ppermute | solution.py:1403
  154.3 17.8 %collective-permute-start.41 = (bf16[2,1408,128]{2,1,0:T(8,128)(2,1)S(1)}, bf16[2,1408,128]{2,1,0:T(8,128)(2,1)S(1)}, u32[]{:S(2)}, u32[]{:S(2)}) collective-permute-start(bf16[2,1408,128]{2,1,0:T(8,128)(2,1)S(1)} %get-tuple-element.218), channel_id=1, source_target_pairs={{0,8},{8,0},{16,24},{24,16},{1,9},{9,1},{17,25},{25,17},{2,10},{10... | collective-permute-start | bytes 2162696 | tf_op jit(solution)/shard_map/z1_a/ppermute | solution.py:44
  159.4 15.6 %collective-permute-start.45 = (bf16[256,1024]{1,0:T(8,128)(2,1)S(1)}, bf16[256,1024]{1,0:T(8,128)(2,1)S(1)}, u32[]{:S(2)}, u32[]{:S(2)}) collective-permute-start(bf16[256,1024]{1,0:T(8,128)(2,1)S(1)} %slice.198), channel_id=1, source_target_pairs={{0,2},{1,3},{2,0},{3,1},{4,6},{5,7},{6,4},{7,5},{8,10},{9,11},{10,... | collective-permute-start | bytes 1572872 | tf_op jit(solution)/shard_map/y_go/ppermute | solution.py:44
  170.2 15.7 %collective-permute-start.44 = (bf16[256,1024]{1,0:T(8,128)(2,1)S(1)}, bf16[256,1024]{1,0:T(8,128)(2,1)S(1)}, u32[]{:S(2)}, u32[]{:S(2)}) collective-permute-start(bf16[256,1024]{1,0:T(8,128)(2,1)S(1)} %get-tuple-element.238.refs_2_), channel_id=1, source_target_pairs={{0,2},{1,3},{2,0},{3,1},{4,6},{5,7},{6,4},{7,5},{8,10},{9,11},{10,... | collective-permute-start | bytes 1572872 | tf_op jit(solution)/shard_map/y_delta/ppermute | solution.py:44
  172.1 13.8 %collective-permute-start.43 = (bf16[2,4,224,128]{3,2,1,0:T(8,128)(2,1)S(1)}, bf16[2,4,224,128]{3,2,1,0:T(8,128)(2,1)S(1)}, u32[]{:S(2)}, u32[]{:S(2)}) collective-permute-start(bf16[2,4,224,128]{3,2,1,0:T(8,128)(2,1)S(1)} %add_convert_fusion.4), channel_id=1, source_target_pairs={{0,4},{4,0},{1,5},{5,1},{2,6},{6,2},{3,7},{7,3},{8,12},{12,8},{9,1... | collective-permute-start | bytes 1376264 | tf_op jit(solution)/shard_map/x_gp/ppermute | solution.py:44
  175.0 19.1 %collective-permute-start.49 = (bf16[1408,128]{1,0:T(8,128)(2,1)S(1)}, bf16[1408,128]{1,0:T(8,128)(2,1)S(1)}, u32[]{:S(2)}, u32[]{:S(2)}) collective-permute-start(bf16[1408,128]{1,0:T(8,128)(2,1)S(1)} %fusion.6), channel_id=1, source_target_pairs={{0,16},{8,24},{16,0},{24,8},{1,17},{9,25},{17,1},{25,9},{2,18},{10... | collective-permute-start | bytes 1081352 | tf_op jit(solution)/shard_map/z2_a/ppermute | solution.py:44
  175.3 18.7 %collective-permute-start.48 = (bf16[256,512]{1,0:T(8,128)(2,1)S(1)}, bf16[256,512]{1,0:T(8,128)(2,1)S(1)}, u32[]{:S(2)}, u32[]{:S(2)}) collective-permute-start(bf16[256,512]{1,0:T(8,128)(2,1)S(1)} %slice.199), channel_id=1, source_target_pairs={{0,4},{4,0},{1,5},{5,1},{2,6},{6,2},{3,7},{7,3},{8,12},{12,8},{9,1... | collective-permute-start | bytes 786440 | tf_op jit(solution)/shard_map/x_go/ppermute | solution.py:44
  188.6 20.8 %collective-permute-start.54 = (bf16[704,128]{1,0:T(8,128)(2,1)S(1)}, bf16[704,128]{1,0:T(8,128)(2,1)S(1)}, u32[]{:S(2)}, u32[]{:S(2)}) collective-permute-start(bf16[704,128]{1,0:T(8,128)(2,1)S(1)} %slice_bitcast_fusion.8), channel_id=1, source_target_pairs={{0,4},{4,0},{1,5},{5,1},{2,6},{6,2},{3,7},{7,3},{8,12},{12,8},{9,1... | collective-permute-start | bytes 540680 | tf_op jit(solution)/shard_map/x_d/ppermute | solution.py:44
  189.3 14.7 %collective-permute-start.50 = (bf16[256,1024]{1,0:T(8,128)(2,1)S(1)}, bf16[256,1024]{1,0:T(8,128)(2,1)S(1)}, u32[]{:S(2)}, u32[]{:S(2)}) collective-permute-start(bf16[256,1024]{1,0:T(8,128)(2,1)S(1)} %get-tuple-element.238.refs_2_), channel_id=1, source_target_pairs={{0,1},{1,0},{2,3},{3,2},{4,5},{5,4},{6,7},{7,6},{8,9},{9,8},{10,11... | collective-permute-start | bytes 1572872 | tf_op jit(solution)/shard_map/core_delta/ppermute | solution.py:44
  (38 other events, 247.0 us)
